TPU v7x, 512 devices: a whole 4x4x16 slice. The times are simulated.
512 devices in a mesh: depth: 8 (over x_lo, y), lat: 64 (over x_hi, z, core).
Axes of the slice: x: 4 (x_hi: 2, x_lo: 2; x = x_hi * 2 + x_lo), y: 4, z: 16, core: 2. Of those that a mesh axis runs over, the one named last changes fastest.
Arguments:
- source_field: bfloat16 [8, 2, 512, 2048], P(None, None, 'lat'), may hold values from -6 to 6
- receiver_field: bfloat16 [8, 2, 512, 2048], P(None, None, 'lat'), may hold values from -6 to 6
- freq_index: int32 [8], replicated, may hold values from 0 to 63
- slowness: float32 [8, 512, 2048], P('depth', 'lat'), may hold values from 0.5 to 2
- ffd_coef: float32 [8, 512, 2048], P('depth', 'lat'), may hold values from 0.04 to 0.12
- band: bfloat16 [16, 3, 128, 128], P('depth'), may hold values from -0.3125 to 0.3125
- image_mask: int32 [8, 512, 2048], P('depth', 'lat'), may hold values 0 or 1
Outputs:
- image: float32 [8, 512, 2048], P('depth', 'lat')
- gradient: float32 [8, 512, 2048], P('depth', 'lat')
All inputs are finite; a program needn't handle non-finite values. No bound on the sum of `image_mask` on one device may be relied on, other than what follows from the above.
Results may differ from a plain program's by a relative error of at most 0.0035.
The roundings to bfloat16 on the way count: a program that leaves them out, or rounds other values in their place, can miss the bound.
Values may be sent and summed in bfloat16 or wider, within the bound.
No kernel may reach another device: no remote copies, remote signals or barrier semaphores. Data moves between devices by JAX's collectives and lax.ppermute only.
A program may use at most 64 MiB of HBM per device.

v0:
```python
import jax
import jax.numpy as jnp
from jax import lax
from jax.sharding import PartitionSpec as P

HALO = 8


def with_halo(value, sides, width):
    for axis, dim in sides:
        size, length = (lax.axis_size(axis), value.shape[dim])
        up = [(i, (i + 1) % size) for i in range(size - 1)]
        down = [(j, i) for i, j in up]
        last = lax.slice_in_dim(value, length - width, length, axis=dim)
        initial = lax.slice_in_dim(value, 0, width, axis=dim)
        before = lax.ppermute(last, axis, up)
        after = lax.ppermute(initial, axis, down)
        value = jnp.concatenate([before, value, after], axis=dim)
    return value


def passed_along(block, axis, distance):
    devices = range(lax.axis_size(axis))
    route = [(i - distance, i) for i in devices if i - distance in devices]
    return lax.ppermute(block, axis, route)


def stencil_rows(rows, padded):
    height = rows.shape[1]
    centre = rows.astype(jnp.float32)
    total = jnp.zeros_like(centre)
    for offset in range(1, HALO + 1):
        upper = lax.slice_in_dim(padded, HALO + offset, HALO + offset + height, axis=1).astype(
            jnp.float32
        )
        lower = lax.slice_in_dim(padded, HALO - offset, HALO - offset + height, axis=1).astype(
            jnp.float32
        )
        total = total + 0.25 / offset * (upper + lower - 2.0 * centre)
    return total


def band_product(rows, band):
    count, height, width = rows.shape
    nblocks = band.shape[0]
    block = band.shape[2]
    tiles = rows.reshape(count, height, nblocks, block)
    padded = jnp.pad(tiles, ((0, 0), (0, 0), (1, 1), (0, 0)))
    total = jnp.zeros(tiles.shape, jnp.float32)
    for offset in range(3):
        window = lax.slice_in_dim(padded, offset, offset + nblocks, axis=2)
        total = total + jnp.einsum(
            "acjb,jbd->acjd", window, band[:, offset], preferred_element_type=jnp.float32
        )
    return total.reshape(count, height, width)


def band_product_t(rows, band):
    count, height, width = rows.shape
    nblocks = band.shape[0]
    block = band.shape[2]
    tiles = rows.reshape(count, height, nblocks, block)
    total = jnp.zeros(tiles.shape, jnp.float32)
    for offset in range(3):
        moved = jnp.einsum(
            "acjd,jbd->acjb", tiles, band[:, offset], preferred_element_type=jnp.float32
        )
        padded = jnp.pad(moved, ((0, 0), (0, 0), (1, 1), (0, 0)))
        total = total + lax.slice_in_dim(padded, 2 - offset, 2 - offset + nblocks, axis=2)
    return total.reshape(count, height, width)


def advance(fields, omegas, slow, coef, band):
    members, comps, height, width = fields.shape
    theta = omegas[:, None, None] * slow[None]
    cosine = jnp.cos(theta)
    sine_part = jnp.sin(theta)
    phase_re = fields[:, 0] * cosine - fields[:, 1] * sine_part
    phase_im = fields[:, 0] * sine_part + fields[:, 1] * cosine
    phased = jnp.stack([phase_re, phase_im], axis=1)
    rows = phased.astype(jnp.bfloat16).reshape(members * comps, height, width)
    padded = with_halo(rows, (("lat", 1),), HALO)
    lateral = (band_product(rows, band) + stencil_rows(rows, padded)).reshape(
        members, comps, height, width
    )
    stepped = jnp.stack([phase_re - coef * lateral[:, 1], phase_im + coef * lateral[:, 0]], axis=1)
    return (phased, stepped)


def retreat(adjoint, phased, omegas, slow, coef, band):
    members, comps, height, width = adjoint.shape
    scaled = (coef * adjoint).astype(jnp.bfloat16).reshape(members * comps, height, width)
    padded = with_halo(scaled, (("lat", 1),), HALO)
    lateral = (band_product_t(scaled, band) + stencil_rows(scaled, padded)).reshape(
        members, comps, height, width
    )
    back_re = adjoint[:, 0] + lateral[:, 1]
    back_im = adjoint[:, 1] - lateral[:, 0]
    weights = omegas[:, None, None]
    term = jnp.sum(weights * (back_im * phased[:, 0] - back_re * phased[:, 1]), axis=0)
    theta = weights * slow[None]
    cosine = jnp.cos(theta)
    sine_part = jnp.sin(theta)
    upward = jnp.stack(
        [back_re * cosine + back_im * sine_part, back_im * cosine - back_re * sine_part], axis=1
    )
    return (term, upward)


def per_device(source_field, receiver_field, freq_index, slowness, ffd_coef, band, image_mask):
    position = lax.axis_index("depth")
    sections = lax.axis_size("depth")
    count = source_field.shape[0]
    layers = slowness.shape[0]
    height = slowness.shape[1]
    width = slowness.shape[2]
    omega_all = 0.1 * (freq_index.astype(jnp.float32) + 1.0)
    band = lax.all_gather(band, "depth", axis=0, tiled=True)
    ticks = count + sections - 1
    store_shape = (layers, count, 2, height, width)

    def fore_tick(tick, carry):
        inflow, image_acc, keep_s, keep_p = carry
        micro = tick - position
        active_tick = (micro >= 0) & (micro < count)
        micro_slot = jnp.clip(micro, 0, count - 1)
        first_src = lax.dynamic_index_in_dim(source_field, micro_slot, 0, keepdims=False)
        first_rcv = lax.dynamic_index_in_dim(receiver_field, micro_slot, 0, keepdims=False)
        entering = jnp.where(position == 0, jnp.stack([first_src, first_rcv]), inflow)
        fields = entering.astype(jnp.float32)
        omega_one = lax.dynamic_slice_in_dim(omega_all, micro_slot, 1)
        omega_pair = jnp.concatenate([omega_one, omega_one])
        phased, fields = advance(fields, omega_pair, slowness[0], ffd_coef[0], band)
        product = jnp.sum(fields[0] * fields[1], axis=0)
        image_acc = image_acc.at[0].add(jnp.where(active_tick, product, 0.0))
        keep_s = keep_s.at[0, micro_slot].set(
            jnp.where(active_tick, fields[0], keep_s[0, micro_slot])
        )
        keep_p = keep_p.at[0, micro_slot].set(
            jnp.where(active_tick, phased[1], keep_p[0, micro_slot])
        )
        outflow = fields.astype(jnp.bfloat16)
        inflow = passed_along(outflow, "depth", 1)
        return (inflow, image_acc, keep_s, keep_p)

    start = (
        jnp.zeros((2, 2, height, width), jnp.bfloat16),
        jnp.zeros((layers, height, width), jnp.float32),
        jnp.zeros(store_shape, jnp.float32),
        jnp.zeros(store_shape, jnp.float32),
    )
    unused, image_acc, keep_s, keep_p = lax.fori_loop(0, ticks, fore_tick, start)
    image = image_acc / count
    masked = image_mask.astype(jnp.float32) * image

    def back_tick(tick, carry):
        inflow, grad_acc = carry
        micro = tick - (sections - 1 - position)
        active_tick = (micro >= 0) & (micro < count)
        micro_slot = jnp.clip(micro, 0, count - 1)
        adjoint = jnp.where(position == sections - 1, 0.0, inflow.astype(jnp.float32))
        omega_one = lax.dynamic_slice_in_dim(omega_all, micro_slot, 1)
        for level in reversed(range(layers)):
            adjoint = adjoint + (masked[level] * keep_s[level, micro_slot])[None]
            term, adjoint = retreat(
                adjoint,
                keep_p[level, micro_slot][None],
                omega_one,
                slowness[level],
                ffd_coef[level],
                band,
            )
            grad_acc = grad_acc.at[level].add(jnp.where(active_tick, term, 0.0))
        inflow = passed_along(adjoint.astype(jnp.bfloat16), "depth", -1)
        return (inflow, grad_acc)

    start_back = (
        jnp.zeros((1, 2, height, width), jnp.bfloat16),
        jnp.zeros((layers, height, width), jnp.float32),
    )
    unused_flow, grad_acc = lax.fori_loop(0, ticks, back_tick, start_back)
    gradient = grad_acc / count
    return (image, gradient)


def solution(mesh):
    return jax.shard_map(
        per_device,
        mesh=mesh,
        in_specs=(
            P(None, None, "lat", None),
            P(None, None, "lat", None),
            P(),
            P("depth", "lat", None),
            P("depth", "lat", None),
            P("depth", None, None, None),
            P("depth", "lat", None),
        ),
        out_specs=(P("depth", "lat", None), P("depth", "lat", None)),
        check_vma=False,
    )
```

profile of v0, /device:TPU:6, one launch (start us, length us, event | category | flops | bytes accessed | tf_op | source)
XLA Modules:
  0.0 799.0 jit_solution(18386120711849431100)
XLA Ops:
  9.6 52.5 %all-gather.2.cloned.1.call-done = bf16[16,3,128,128]{3,2,0,1:T(8,128)(2,1)} async-done(((bf16[2,3,128,128]{3,2,0,1:T(8,128)(2,1)}), bf16[16,3,128,128]{3,2,0,1:T(8,128)(2,1)}) %all-gather.2.cloned.1.call-update) | async-done | bytes 1572880 | tf_op jit(solution)/shard_map/all_gather | solution.py:118
  63.9 404.6 %while.46 = (s32[]{:T(128)}, bf16[2,2,8,2048]{3,2,1,0:T(8,128)(2,1)S(1)}, f32[1,8,2048]{2,1,0:T(8,128)}, f32[1,8,2,8,2048]{4,3,2,1,0:T(8,128)}, f32[1,8,2,8,2048...) while((s32[]{:T(128)}, ...), condition=%wide.region_3.4_spmd.clone, body=%wide.region_0.3_spmd.clone.sunk | while | flops 55443484 | bytes 11142684 | solution.py:152
  69.6 7.3 collective-permute-start.1
  96.6 7.3 collective-permute-start.1
  123.5 7.3 collective-permute-start.1
  150.5 7.3 collective-permute-start.1
  177.5 7.3 collective-permute-start.1
  204.5 7.3 collective-permute-start.1
  231.4 7.3 collective-permute-start.1
  258.4 7.3 collective-permute-start.1
  285.4 7.3 collective-permute-start.1
  312.4 7.3 collective-permute-start.1
  339.3 7.3 collective-permute-start.1
  366.3 7.3 collective-permute-start.1
  393.3 7.3 collective-permute-start.1
  420.2 7.3 collective-permute-start.1
  447.2 7.3 collective-permute-start.1
  470.0 320.6 %while.47 = (s32[]{:T(128)}, bf16[1,2,8,2048]{3,2,1,0:T(8,128)(2,1)S(1)}, f32[1,8,2048]{2,1,0:T(8,128)}, pred[]{:T(512)}, f32[1,8,2048]{2,1,0:T(8,128)S(1)}, /*i...) while((s32[]{:T(128)}, ...), condition=%wide.region_5.6_spmd.clone, body=%wide.region_4.5_spmd.clone.sunk | while | flops 28868612 | bytes 6291878 | solution.py:181
  472.9 7.3 collective-permute-start.4
  512.1 7.3 collective-permute-start.4
  576.8 7.3 collective-permute-start.4
  598.5 7.3 collective-permute-start.4
  663.5 7.3 collective-permute-start.4
  685.2 7.3 collective-permute-start.4
  (749 shorter events, 577.3 us)
Async XLA Ops:
  7.2 55.0 %all-gather.2.cloned.1.call-start = ((), (), s32[]{:S(2)}) async-start(), calls=%async_computation | async-start | bytes 1769472 | tf_op jit(solution)/shard_map/all_gather | solution.py:118
  67.7 10.8 %collective-permute-start = (bf16[4,8,2048]{2,1,0:T(8,128)(2,1)S(1)}, bf16[4,8,2048]{2,1,0:T(8,128)(2,1)S(1)}, u32[]{:S(2)}, u32[]{:S(2)}) collective-permute-start(bf16[4,8,2048]{2,1,0:T(8,128)(2,1)S(1)} %bitcast.181), channel_id=1, source_target_pairs={{0,1},{1,2},{2,3},{3,4},{4,5},{5,6},{6,7},{7,8},{8,9},{9,10},{10,1... | collective-permute-start | bytes 393224 | tf_op jit(solution)/shard_map/while/body/eval_jaxpr/ppermute | solution.py:16
  94.6 10.8 %collective-permute-start = (bf16[4,8,2048]{2,1,0:T(8,128)(2,1)S(1)}, bf16[4,8,2048]{2,1,0:T(8,128)(2,1)S(1)}, u32[]{:S(2)}, u32[]{:S(2)}) collective-permute-start(bf16[4,8,2048]{2,1,0:T(8,128)(2,1)S(1)} %bitcast.181), channel_id=1, source_target_pairs={{0,1},{1,2},{2,3},{3,4},{4,5},{5,6},{6,7},{7,8},{8,9},{9,10},{10,1... | collective-permute-start | bytes 393224 | tf_op jit(solution)/shard_map/while/body/eval_jaxpr/ppermute | solution.py:16
  148.6 10.8 %collective-permute-start = (bf16[4,8,2048]{2,1,0:T(8,128)(2,1)S(1)}, bf16[4,8,2048]{2,1,0:T(8,128)(2,1)S(1)}, u32[]{:S(2)}, u32[]{:S(2)}) collective-permute-start(bf16[4,8,2048]{2,1,0:T(8,128)(2,1)S(1)} %bitcast.181), channel_id=1, source_target_pairs={{0,1},{1,2},{2,3},{3,4},{4,5},{5,6},{6,7},{7,8},{8,9},{9,10},{10,1... | collective-permute-start | bytes 393224 | tf_op jit(solution)/shard_map/while/body/eval_jaxpr/ppermute | solution.py:16
  175.6 10.8 %collective-permute-start = (bf16[4,8,2048]{2,1,0:T(8,128)(2,1)S(1)}, bf16[4,8,2048]{2,1,0:T(8,128)(2,1)S(1)}, u32[]{:S(2)}, u32[]{:S(2)}) collective-permute-start(bf16[4,8,2048]{2,1,0:T(8,128)(2,1)S(1)} %bitcast.181), channel_id=1, source_target_pairs={{0,1},{1,2},{2,3},{3,4},{4,5},{5,6},{6,7},{7,8},{8,9},{9,10},{10,1... | collective-permute-start | bytes 393224 | tf_op jit(solution)/shard_map/while/body/eval_jaxpr/ppermute | solution.py:16
  202.5 10.8 %collective-permute-start = (bf16[4,8,2048]{2,1,0:T(8,128)(2,1)S(1)}, bf16[4,8,2048]{2,1,0:T(8,128)(2,1)S(1)}, u32[]{:S(2)}, u32[]{:S(2)}) collective-permute-start(bf16[4,8,2048]{2,1,0:T(8,128)(2,1)S(1)} %bitcast.181), channel_id=1, source_target_pairs={{0,1},{1,2},{2,3},{3,4},{4,5},{5,6},{6,7},{7,8},{8,9},{9,10},{10,1... | collective-permute-start | bytes 393224 | tf_op jit(solution)/shard_map/while/body/eval_jaxpr/ppermute | solution.py:16
  256.5 10.8 %collective-permute-start = (bf16[4,8,2048]{2,1,0:T(8,128)(2,1)S(1)}, bf16[4,8,2048]{2,1,0:T(8,128)(2,1)S(1)}, u32[]{:S(2)}, u32[]{:S(2)}) collective-permute-start(bf16[4,8,2048]{2,1,0:T(8,128)(2,1)S(1)} %bitcast.181), channel_id=1, source_target_pairs={{0,1},{1,2},{2,3},{3,4},{4,5},{5,6},{6,7},{7,8},{8,9},{9,10},{10,1... | collective-permute-start | bytes 393224 | tf_op jit(solution)/shard_map/while/body/eval_jaxpr/ppermute | solution.py:16
  283.5 10.8 %collective-permute-start = (bf16[4,8,2048]{2,1,0:T(8,128)(2,1)S(1)}, bf16[4,8,2048]{2,1,0:T(8,128)(2,1)S(1)}, u32[]{:S(2)}, u32[]{:S(2)}) collective-permute-start(bf16[4,8,2048]{2,1,0:T(8,128)(2,1)S(1)} %bitcast.181), channel_id=1, source_target_pairs={{0,1},{1,2},{2,3},{3,4},{4,5},{5,6},{6,7},{7,8},{8,9},{9,10},{10,1... | collective-permute-start | bytes 393224 | tf_op jit(solution)/shard_map/while/body/eval_jaxpr/ppermute | solution.py:16
  310.4 10.8 %collective-permute-start = (bf16[4,8,2048]{2,1,0:T(8,128)(2,1)S(1)}, bf16[4,8,2048]{2,1,0:T(8,128)(2,1)S(1)}, u32[]{:S(2)}, u32[]{:S(2)}) collective-permute-start(bf16[4,8,2048]{2,1,0:T(8,128)(2,1)S(1)} %bitcast.181), channel_id=1, source_target_pairs={{0,1},{1,2},{2,3},{3,4},{4,5},{5,6},{6,7},{7,8},{8,9},{9,10},{10,1... | collective-permute-start | bytes 393224 | tf_op jit(solution)/shard_map/while/body/eval_jaxpr/ppermute | solution.py:16
  471.0 11.0 %collective-permute-start.3 = (bf16[2,8,2048]{2,1,0:T(8,128)(2,1)S(1)}, bf16[2,8,2048]{2,1,0:T(8,128)(2,1)S(1)}, u32[]{:S(2)}, u32[]{:S(2)}) collective-permute-start(bf16[2,8,2048]{2,1,0:T(8,128)(2,1)S(1)} %get-tuple-element.1043), channel_id=1, source_target_pairs={{0,1},{1,2},{2,3},{3,4},{4,5},{5,6},{6,7},{7,8},{8,9},{9,10},{10,1... | collective-permute-start | bytes 196616 | tf_op jit(solution)/shard_map/while/body/eval_jaxpr/ppermute | solution.py:16
  490.6 11.0 %collective-permute-start.3 = (bf16[2,8,2048]{2,1,0:T(8,128)(2,1)S(1)}, bf16[2,8,2048]{2,1,0:T(8,128)(2,1)S(1)}, u32[]{:S(2)}, u32[]{:S(2)}) collective-permute-start(bf16[2,8,2048]{2,1,0:T(8,128)(2,1)S(1)} %get-tuple-element.1043), channel_id=1, source_target_pairs={{0,1},{1,2},{2,3},{3,4},{4,5},{5,6},{6,7},{7,8},{8,9},{9,10},{10,1... | collective-permute-start | bytes 196616 | tf_op jit(solution)/shard_map/while/body/eval_jaxpr/ppermute | solution.py:16
  510.1 11.0 %collective-permute-start.3 = (bf16[2,8,2048]{2,1,0:T(8,128)(2,1)S(1)}, bf16[2,8,2048]{2,1,0:T(8,128)(2,1)S(1)}, u32[]{:S(2)}, u32[]{:S(2)}) collective-permute-start(bf16[2,8,2048]{2,1,0:T(8,128)(2,1)S(1)} %get-tuple-element.1043), channel_id=1, source_target_pairs={{0,1},{1,2},{2,3},{3,4},{4,5},{5,6},{6,7},{7,8},{8,9},{9,10},{10,1... | collective-permute-start | bytes 196616 | tf_op jit(solution)/shard_map/while/body/eval_jaxpr/ppermute | solution.py:16
  531.6 11.0 %collective-permute-start.3 = (bf16[2,8,2048]{2,1,0:T(8,128)(2,1)S(1)}, bf16[2,8,2048]{2,1,0:T(8,128)(2,1)S(1)}, u32[]{:S(2)}, u32[]{:S(2)}) collective-permute-start(bf16[2,8,2048]{2,1,0:T(8,128)(2,1)S(1)} %get-tuple-element.1043), channel_id=1, source_target_pairs={{0,1},{1,2},{2,3},{3,4},{4,5},{5,6},{6,7},{7,8},{8,9},{9,10},{10,1... | collective-permute-start | bytes 196616 | tf_op jit(solution)/shard_map/while/body/eval_jaxpr/ppermute | solution.py:16
  553.2 11.0 %collective-permute-start.3 = (bf16[2,8,2048]{2,1,0:T(8,128)(2,1)S(1)}, bf16[2,8,2048]{2,1,0:T(8,128)(2,1)S(1)}, u32[]{:S(2)}, u32[]{:S(2)}) collective-permute-start(bf16[2,8,2048]{2,1,0:T(8,128)(2,1)S(1)} %get-tuple-element.1043), channel_id=1, source_target_pairs={{0,1},{1,2},{2,3},{3,4},{4,5},{5,6},{6,7},{7,8},{8,9},{9,10},{10,1... | collective-permute-start | bytes 196616 | tf_op jit(solution)/shard_map/while/body/eval_jaxpr/ppermute | solution.py:16
  574.9 11.0 %collective-permute-start.3 = (bf16[2,8,2048]{2,1,0:T(8,128)(2,1)S(1)}, bf16[2,8,2048]{2,1,0:T(8,128)(2,1)S(1)}, u32[]{:S(2)}, u32[]{:S(2)}) collective-permute-start(bf16[2,8,2048]{2,1,0:T(8,128)(2,1)S(1)} %get-tuple-element.1043), channel_id=1, source_target_pairs={{0,1},{1,2},{2,3},{3,4},{4,5},{5,6},{6,7},{7,8},{8,9},{9,10},{10,1... | collective-permute-start | bytes 196616 | tf_op jit(solution)/shard_map/while/body/eval_jaxpr/ppermute | solution.py:16
  596.6 11.0 %collective-permute-start.3 = (bf16[2,8,2048]{2,1,0:T(8,128)(2,1)S(1)}, bf16[2,8,2048]{2,1,0:T(8,128)(2,1)S(1)}, u32[]{:S(2)}, u32[]{:S(2)}) collective-permute-start(bf16[2,8,2048]{2,1,0:T(8,128)(2,1)S(1)} %get-tuple-element.1043), channel_id=1, source_target_pairs={{0,1},{1,2},{2,3},{3,4},{4,5},{5,6},{6,7},{7,8},{8,9},{9,10},{10,1... | collective-permute-start | bytes 196616 | tf_op jit(solution)/shard_map/while/body/eval_jaxpr/ppermute | solution.py:16
  618.3 11.0 %collective-permute-start.3 = (bf16[2,8,2048]{2,1,0:T(8,128)(2,1)S(1)}, bf16[2,8,2048]{2,1,0:T(8,128)(2,1)S(1)}, u32[]{:S(2)}, u32[]{:S(2)}) collective-permute-start(bf16[2,8,2048]{2,1,0:T(8,128)(2,1)S(1)} %get-tuple-element.1043), channel_id=1, source_target_pairs={{0,1},{1,2},{2,3},{3,4},{4,5},{5,6},{6,7},{7,8},{8,9},{9,10},{10,1... | collective-permute-start | bytes 196616 | tf_op jit(solution)/shard_map/while/body/eval_jaxpr/ppermute | solution.py:16
  639.9 11.0 %collective-permute-start.3 = (bf16[2,8,2048]{2,1,0:T(8,128)(2,1)S(1)}, bf16[2,8,2048]{2,1,0:T(8,128)(2,1)S(1)}, u32[]{:S(2)}, u32[]{:S(2)}) collective-permute-start(bf16[2,8,2048]{2,1,0:T(8,128)(2,1)S(1)} %get-tuple-element.1043), channel_id=1, source_target_pairs={{0,1},{1,2},{2,3},{3,4},{4,5},{5,6},{6,7},{7,8},{8,9},{9,10},{10,1... | collective-permute-start | bytes 196616 | tf_op jit(solution)/shard_map/while/body/eval_jaxpr/ppermute | solution.py:16
  661.6 11.0 %collective-permute-start.3 = (bf16[2,8,2048]{2,1,0:T(8,128)(2,1)S(1)}, bf16[2,8,2048]{2,1,0:T(8,128)(2,1)S(1)}, u32[]{:S(2)}, u32[]{:S(2)}) collective-permute-start(bf16[2,8,2048]{2,1,0:T(8,128)(2,1)S(1)} %get-tuple-element.1043), channel_id=1, source_target_pairs={{0,1},{1,2},{2,3},{3,4},{4,5},{5,6},{6,7},{7,8},{8,9},{9,10},{10,1... | collective-permute-start | bytes 196616 | tf_op jit(solution)/shard_map/while/body/eval_jaxpr/ppermute | solution.py:16
  683.3 11.0 %collective-permute-start.3 = (bf16[2,8,2048]{2,1,0:T(8,128)(2,1)S(1)}, bf16[2,8,2048]{2,1,0:T(8,128)(2,1)S(1)}, u32[]{:S(2)}, u32[]{:S(2)}) collective-permute-start(bf16[2,8,2048]{2,1,0:T(8,128)(2,1)S(1)} %get-tuple-element.1043), channel_id=1, source_target_pairs={{0,1},{1,2},{2,3},{3,4},{4,5},{5,6},{6,7},{7,8},{8,9},{9,10},{10,1... | collective-permute-start | bytes 196616 | tf_op jit(solution)/shard_map/while/body/eval_jaxpr/ppermute | solution.py:16
  704.9 11.0 %collective-permute-start.3 = (bf16[2,8,2048]{2,1,0:T(8,128)(2,1)S(1)}, bf16[2,8,2048]{2,1,0:T(8,128)(2,1)S(1)}, u32[]{:S(2)}, u32[]{:S(2)}) collective-permute-start(bf16[2,8,2048]{2,1,0:T(8,128)(2,1)S(1)} %get-tuple-element.1043), channel_id=1, source_target_pairs={{0,1},{1,2},{2,3},{3,4},{4,5},{5,6},{6,7},{7,8},{8,9},{9,10},{10,1... | collective-permute-start | bytes 196616 | tf_op jit(solution)/shard_map/while/body/eval_jaxpr/ppermute | solution.py:16
  726.6 11.0 %collective-permute-start.3 = (bf16[2,8,2048]{2,1,0:T(8,128)(2,1)S(1)}, bf16[2,8,2048]{2,1,0:T(8,128)(2,1)S(1)}, u32[]{:S(2)}, u32[]{:S(2)}) collective-permute-start(bf16[2,8,2048]{2,1,0:T(8,128)(2,1)S(1)} %get-tuple-element.1043), channel_id=1, source_target_pairs={{0,1},{1,2},{2,3},{3,4},{4,5},{5,6},{6,7},{7,8},{8,9},{9,10},{10,1... | collective-permute-start | bytes 196616 | tf_op jit(solution)/shard_map/while/body/eval_jaxpr/ppermute | solution.py:16
  748.3 11.0 %collective-permute-start.3 = (bf16[2,8,2048]{2,1,0:T(8,128)(2,1)S(1)}, bf16[2,8,2048]{2,1,0:T(8,128)(2,1)S(1)}, u32[]{:S(2)}, u32[]{:S(2)}) collective-permute-start(bf16[2,8,2048]{2,1,0:T(8,128)(2,1)S(1)} %get-tuple-element.1043), channel_id=1, source_target_pairs={{0,1},{1,2},{2,3},{3,4},{4,5},{5,6},{6,7},{7,8},{8,9},{9,10},{10,1... | collective-permute-start | bytes 196616 | tf_op jit(solution)/shard_map/while/body/eval_jaxpr/ppermute | solution.py:16
  770.0 11.0 %collective-permute-start.3 = (bf16[2,8,2048]{2,1,0:T(8,128)(2,1)S(1)}, bf16[2,8,2048]{2,1,0:T(8,128)(2,1)S(1)}, u32[]{:S(2)}, u32[]{:S(2)}) collective-permute-start(bf16[2,8,2048]{2,1,0:T(8,128)(2,1)S(1)} %get-tuple-element.1043), channel_id=1, source_target_pairs={{0,1},{1,2},{2,3},{3,4},{4,5},{5,6},{6,7},{7,8},{8,9},{9,10},{10,1... | collective-permute-start | bytes 196616 | tf_op jit(solution)/shard_map/while/body/eval_jaxpr/ppermute | solution.py:16
  (131 other events, 1132.8 us)
Sparse Core Ops, SparseCore 0:
  10.1 51.9 all-gather.1
where the time goes:
time: 806 us; the launch traced here: 799 us
  starting transfers between devices  393 us (49%)
  waiting for transfers between devices  158 us (20%)
  other arithmetic  153 us (19%)
  local copies, waits for them, and re-layouts  49.8 us (6%)
  matrix products  28.6 us (4%)
  between operations  14.1 us (2%)
    ppermute x30, starting transfers between devices, with_halo(): after = lax.ppermute(initial, axis, down)  218 us
    ppermute x30, starting transfers between devices, passed_along(): return lax.ppermute(block, axis, route)  117 us
    ppermute x30, waiting for transfers between devices, passed_along(): return lax.ppermute(block, axis, route)  90.8 us
    ppermute x30, starting transfers between devices, with_halo(): before = lax.ppermute(last, axis, up)  57.6 us
    all_gather x1, waiting for transfers between devices, per_device(): band = lax.all_gather(band, 'depth', axis=0, tiled=True)  52.5 us
    add x15, other arithmetic, advance(): band_product(rows, band) + stencil_rows(rows, padded)  37.2 us
    scatter x15, other arithmetic, fore_tick(): keep_s.at[0, micro_slot]  34.2 us
    another operation x30, other arithmetic  24.4 us
  transfers between devices with their start and end apart: 91, of which 61 were waited for; matrix products, arithmetic and copies ran while one was open for 12% of the time, Pallas kernels for 0%

commit v1 on v0

v1 whole, which is shorter than its diff:
```python
import functools
import jax
import jax.numpy as jnp
import numpy as np
from jax import lax
from jax.experimental import pallas as pl
from jax.experimental.pallas import tpu as pltpu
from jax.sharding import PartitionSpec as P

HALO = 8
BLOCK = 128
PAIR = 2 * BLOCK
CENTRE, EDGE, SLOW, COEF, PACKED = 0, 256, 384, 512, 640
VMEM = pl.BlockSpec(memory_space=pltpu.VMEM)
SMEM = pl.BlockSpec(memory_space=pltpu.SMEM)
F32, BF16 = jnp.float32, jnp.bfloat16


def stencil_weight(distance):
    if distance == 0:
        return sum(-0.5 / k for k in range(1, HALO + 1))
    return 0.25 / abs(distance) if abs(distance) <= HALO else 0.0


def stencil_matrix(combos, shift):
    small = np.zeros((HALO, HALO))
    for row in range(HALO):
        for source in range(HALO):
            small[row, source] = stencil_weight(shift + source - row)
    return np.kron(np.eye(combos), small)


def split_weights(matrix):
    high = matrix.astype(jnp.bfloat16)
    low = (matrix - high.astype(np.float64)).astype(jnp.bfloat16)
    return np.concatenate([high, low], axis=0)


def own_weights(combos):
    return split_weights(stencil_matrix(combos, 0))


def side_weights(combos):
    after, before = (stencil_matrix(combos, HALO), stencil_matrix(combos, -HALO))
    even = split_weights(np.concatenate([after, before], axis=1))
    odd = split_weights(np.concatenate([before, after], axis=1))
    return np.stack([even, odd])


def cos_sin(theta):
    turns = jnp.floor(theta * 0.6366197723675814 + 0.5)
    rest = theta - turns * 1.5703125
    rest = rest - turns * 4.837512969970703e-4
    rest = rest - turns * 7.549789948768648e-8
    square = rest * rest
    sine = rest + rest * square * (
        -1.6666654611e-1 + square * (8.3321608736e-3 + square * -1.9515295891e-4)
    )
    cosine = (
        1.0
        - 0.5 * square
        + square
        * square
        * (4.166664568298827e-2 + square * (-1.388731625493765e-3 + square * 2.443315711809948e-5))
    )
    quadrant = turns.astype(jnp.int32)
    swap = (quadrant & 1) == 1
    sine_out = jnp.where(swap, cosine, sine)
    cosine_out = jnp.where(swap, sine, cosine)
    sine_out = jnp.where((quadrant & 2) == 2, -sine_out, sine_out)
    cosine_out = jnp.where(((quadrant + 1) & 2) == 2, -cosine_out, cosine_out)
    return (cosine_out, sine_out)


def dot(left, right):
    return jnp.dot(left, right, preferred_element_type=F32)


def dot_t(left, right):
    return lax.dot_general(left, right, (((1,), (1,)), ((), ())), preferred_element_type=F32)


def columns(chunk):
    return slice(chunk * PAIR, (chunk + 1) * PAIR)


def joined(packed_ref, level, base, chunk):
    start = base + chunk * 2 * HALO
    both = packed_ref[level, start : start + 2 * HALO, :].astype(F32)
    return both[:HALO] + both[HALO:]


def pack_kernel(slow_ref, coef_ref, band_ref, out_ref):
    copies = out_ref.shape[0]

    def write(rows, cols, value):
        for copy in range(copies):
            out_ref[copy, rows, cols] = value

    left, right = (slice(0, BLOCK), slice(BLOCK, PAIR))
    write(slice(0, BLOCK), left, band_ref[0, 1])
    write(slice(0, BLOCK), right, band_ref[1, 0])
    write(slice(BLOCK, PAIR), left, band_ref[0, 2])
    write(slice(BLOCK, PAIR), right, band_ref[1, 1])
    write(slice(EDGE, EDGE + BLOCK), left, band_ref[0, 0])
    write(slice(EDGE, EDGE + BLOCK), right, band_ref[1, 2])
    for ref, base in ((slow_ref, SLOW), (coef_ref, COEF)):
        for chunk in range(ref.shape[2] // PAIR):
            value = ref[0, :, columns(chunk)]
            high = value.astype(BF16).astype(F32)
            pair = jnp.concatenate([high, value - high], axis=0).astype(BF16)
            start = base + chunk * 2 * HALO
            write(slice(start, start + 2 * HALO), slice(0, PAIR), pair)


def phase(fields, cosine, sine):
    parts = []
    for member in range(fields.shape[0] // (2 * HALO)):
        base = member * 2 * HALO
        real, imag = (fields[base : base + HALO], fields[base + HALO : base + 2 * HALO])
        parts.append(real * cosine - imag * sine)
        parts.append(real * sine + imag * cosine)
    return jnp.concatenate(parts, axis=0)


def first_kernel(omega_ref, packed_ref, fields_ref, rows_ref, phased_ref, angle_ref):
    omega = omega_ref[0]
    for chunk in range(packed_ref.shape[0]):
        cols = columns(chunk)
        cosine, sine = cos_sin(omega * joined(packed_ref, 0, SLOW, chunk))
        angle_ref[0:HALO, cols] = cosine
        angle_ref[HALO : 2 * HALO, cols] = sine
        phased = phase(fields_ref[:, cols].astype(F32), cosine, sine)
        phased_ref[:, cols] = phased
        rows_ref[:, cols] = phased.astype(BF16)


def middle_kernel(level, omega_ref, packed_ref, weights_ref, rows_ref, lateral_ref, *angle_refs):
    omega = omega_ref[0]
    pairs = packed_ref.shape[0]
    height = rows_ref.shape[0]
    for pair in range(pairs):
        cols = columns(pair)
        rows = rows_ref[:, cols]
        total = dot(rows, packed_ref[pair, CENTRE : CENTRE + PAIR, :])
        spread = dot(weights_ref[...], rows)
        total = total + (spread[:height] + spread[height:])
        zero = jnp.zeros((height, BLOCK), F32)
        left, right = (zero, zero)
        if pair > 0:
            before = rows_ref[:, pair * PAIR - BLOCK : pair * PAIR]
            left = dot(before, packed_ref[pair, EDGE : EDGE + BLOCK, 0:BLOCK])
        if pair < pairs - 1:
            after = rows_ref[:, (pair + 1) * PAIR : (pair + 1) * PAIR + BLOCK]
            right = dot(after, packed_ref[pair, EDGE : EDGE + BLOCK, BLOCK:PAIR])
        lateral_ref[:, cols] = total + jnp.concatenate([left, right], axis=1)
        if angle_refs:
            cosine, sine = cos_sin(omega * joined(packed_ref, level + 1, SLOW, pair))
            angle_refs[0][0:HALO, cols] = cosine
            angle_refs[0][HALO : 2 * HALO, cols] = sine


def sides(weights_ref, first_ref, second_ref, cols):
    both = jnp.concatenate([first_ref[:, cols], second_ref[:, cols]], axis=0)
    spread = dot(weights_ref[...], both)
    height = first_ref.shape[0]
    return spread[:height] + spread[height:]


def step_kernel(level, last, *refs):
    if last:
        packed, weights, lateral, first, second, phased, state, product = refs
    else:
        packed, weights, lateral, first, second, phased, angle = refs[:7]
        state, product, rows_next, phased_next = refs[7:]
    for chunk in range(packed.shape[0]):
        cols = columns(chunk)
        total = lateral[:, cols] + sides(weights, first, second, cols)
        coef = joined(packed, level, COEF, chunk)
        value = phased[:, cols]
        part = [slice(k * HALO, (k + 1) * HALO) for k in range(4)]
        source_re = value[part[0]] - coef * total[part[1]]
        source_im = value[part[1]] + coef * total[part[0]]
        receiver_re = value[part[2]] - coef * total[part[3]]
        receiver_im = value[part[3]] + coef * total[part[2]]
        state[0:HALO, cols] = source_re
        state[HALO : 2 * HALO, cols] = source_im
        product[:, cols] = source_re * receiver_re + source_im * receiver_im
        if not last:
            stepped = jnp.concatenate([source_re, source_im, receiver_re, receiver_im], axis=0)
            entering = stepped.astype(BF16).astype(F32)
            cosine, sine = (angle[0:HALO, cols], angle[HALO : 2 * HALO, cols])
            following = phase(entering, cosine, sine)
            phased_next[:, cols] = following
            rows_next[:, cols] = following.astype(BF16)


def image_kernel(parts_ref, mask_ref, image_ref, masked_ref):
    count = parts_ref.shape[0]
    total = parts_ref[0]
    for member in range(1, count):
        total = total + parts_ref[member]
    image = total / count
    image_ref[0] = image
    masked = mask_ref[0].astype(F32) * image
    for copy in range(count):
        masked_ref[copy] = masked


def gradient_kernel(parts_ref, gradient_ref):
    count = parts_ref.shape[0]
    total = parts_ref[0]
    for member in range(1, count):
        total = total + parts_ref[member]
    gradient_ref[0] = total / count


def scaled_rows(adjoint, coef):
    return jnp.concatenate([adjoint[:HALO] * coef, adjoint[HALO:] * coef], axis=0).astype(BF16)


def weighted(masked, state):
    return jnp.concatenate([masked * state[:HALO], masked * state[HALO:]], axis=0)


def adjoint_kernel(level, packed, masked, state, adjoint, scaled):
    for chunk in range(packed.shape[0]):
        cols = columns(chunk)
        value = weighted(masked[level, :, cols], state[:, cols])
        adjoint[:, cols] = value
        scaled[:, cols] = scaled_rows(value, joined(packed, level, COEF, chunk))


def middle_back_kernel(packed_ref, weights_ref, rows_ref, lateral_ref):
    pairs = packed_ref.shape[0]
    height = rows_ref.shape[0]
    for pair in range(pairs):
        cols = columns(pair)
        rows = rows_ref[:, cols]
        total = dot_t(rows, packed_ref[pair, CENTRE : CENTRE + PAIR, :])
        spread = dot(weights_ref[...], rows)
        total = total + (spread[:height] + spread[height:])
        zero = jnp.zeros((height, BLOCK), F32)
        left, right = (zero, zero)
        if pair > 0:
            before = rows_ref[:, pair * PAIR - BLOCK : pair * PAIR]
            left = dot_t(before, packed_ref[pair - 1, EDGE : EDGE + BLOCK, BLOCK:PAIR])
        if pair < pairs - 1:
            after = rows_ref[:, (pair + 1) * PAIR : (pair + 1) * PAIR + BLOCK]
            right = dot_t(after, packed_ref[pair + 1, EDGE : EDGE + BLOCK, 0:BLOCK])
        lateral_ref[:, cols] = total + jnp.concatenate([left, right], axis=1)


def back_kernel(level, last, *refs):
    if last:
        omega, packed, weights, lateral, first, second, adjoint, phased, term = refs
    else:
        omega, packed, weights, lateral, first, second, adjoint, phased = refs[:8]
        angle, masked, state, term, adjoint_next, scaled_next = refs[8:]
    for chunk in range(packed.shape[0]):
        cols = columns(chunk)
        total = lateral[:, cols] + sides(weights, first, second, cols)
        value = adjoint[:, cols]
        back_re = value[:HALO] + total[HALO:]
        back_im = value[HALO:] - total[:HALO]
        phase_re = phased[2 * HALO : 3 * HALO, cols]
        phase_im = phased[3 * HALO : 4 * HALO, cols]
        term[:, cols] = omega[0] * (back_im * phase_re - back_re * phase_im)
        if not last:
            cosine, sine = (angle[0:HALO, cols], angle[HALO : 2 * HALO, cols])
            upward = jnp.concatenate(
                [back_re * cosine + back_im * sine, back_im * cosine - back_re * sine], axis=0
            )
            upward = upward.astype(BF16).astype(F32)
            following = weighted(masked[level - 1, :, cols], state[:, cols]) + upward
            adjoint_next[:, cols] = following
            scaled_next[:, cols] = scaled_rows(following, joined(packed, level - 1, COEF, chunk))


def call(kernel, name, outs, cost, *args):
    shapes = [jax.ShapeDtypeStruct(shape, kind) for shape, kind in outs]
    return pl.pallas_call(
        kernel,
        name=name,
        out_shape=shapes,
        in_specs=[SMEM if arg.shape == (1,) else VMEM for arg in args],
        out_specs=[VMEM] * len(shapes),
        cost_estimate=pl.CostEstimate(flops=cost, bytes_accessed=1 << 20, transcendentals=0),
    )(*args)


def swapped(rows):
    size = lax.axis_size("lat")
    received = []
    for offset in (0, 1):
        pairs = [(i, i + 1) for i in range(offset, size - 1, 2)]
        route = [(a, b) for a, b in pairs] + [(b, a) for a, b in pairs]
        received.append(lax.ppermute(rows, "lat", route))
    return received


def exchanged(parts):
    return lax.all_to_all(parts, "depth", 0, 0)


def per_device(source_field, receiver_field, freq_index, slowness, ffd_coef, band, image_mask):
    sections = lax.axis_size("depth")
    member = lax.axis_index("depth")
    height, width = slowness.shape[1:]
    levels = sections
    omega = 0.1 * (lax.dynamic_slice_in_dim(freq_index, member, 1).astype(F32) + 1.0)
    odd = lax.rem(lax.axis_index("lat"), 2)
    side_fore = jnp.where(odd == 1, *side_weights(4)[::-1])
    side_back = jnp.where(odd == 1, *side_weights(2)[::-1])
    own_fore, own_back = (jnp.asarray(own_weights(4)), jnp.asarray(own_weights(2)))
    source = lax.dynamic_index_in_dim(source_field, member, 0, keepdims=False)
    receiver = lax.dynamic_index_in_dim(receiver_field, member, 0, keepdims=False)
    fields = jnp.concatenate([source, receiver]).reshape(4 * height, width)

    wide, half, single = ((4 * height, width), (2 * height, width), (height, width))
    (packed,) = call(
        pack_kernel, "pack", [((sections, PACKED, PAIR), BF16)], 1000, slowness, ffd_coef, band
    )
    packed = exchanged(packed)
    rows, phased, angle = call(
        first_kernel, "first", [(wide, BF16), (wide, F32), (half, F32)], 1000, omega, packed, fields
    )
    states, products, phases, angles = ([], [], [phased], [angle])
    for level in range(levels):
        last = level == levels - 1
        first, second = swapped(rows)
        outs = [(wide, F32)] + ([] if last else [(half, F32)])
        lateral, *more = call(
            functools.partial(middle_kernel, level),
            "middle",
            outs,
            1 << 28,
            omega,
            packed,
            own_fore,
            rows,
        )
        angles += more
        outs = [(half, F32), (single, F32)] + ([] if last else [(wide, BF16), (wide, F32)])
        args = [packed, side_fore, lateral, first, second, phased] + more
        state, product, *more = call(
            functools.partial(step_kernel, level, last), "step", outs, 1 << 20, *args
        )
        states.append(state)
        products.append(product)
        if not last:
            rows, phased = more
            phases.append(phased)

    image, masked = call(
        image_kernel,
        "image",
        [((1,) + single, F32), ((sections,) + single, F32)],
        1000,
        exchanged(jnp.stack(products)),
        image_mask,
    )
    masked = exchanged(masked)

    level = levels - 1
    adjoint, scaled = call(
        functools.partial(adjoint_kernel, level),
        "adjoint",
        [(half, F32), (half, BF16)],
        1000,
        packed,
        masked,
        states[level],
    )
    terms = [None] * levels
    for level in reversed(range(levels)):
        last = level == 0
        first, second = swapped(scaled)
        (lateral,) = call(
            middle_back_kernel, "middle_back", [(half, F32)], 1 << 28, packed, own_back, scaled
        )
        args = [omega, packed, side_back, lateral, first, second, adjoint, phases[level]]
        outs = [(single, F32)]
        if not last:
            args += [angles[level], masked, states[level - 1]]
            outs += [(half, F32), (half, BF16)]
        terms[level], *more = call(
            functools.partial(back_kernel, level, last), "back", outs, 1 << 20, *args
        )
        if not last:
            adjoint, scaled = more
    (gradient,) = call(
        gradient_kernel, "gradient", [((1,) + single, F32)], 1000, exchanged(jnp.stack(terms))
    )
    return (image, gradient)


def solution(mesh):
    return jax.shard_map(
        per_device,
        mesh=mesh,
        in_specs=(
            P(None, None, "lat", None),
            P(None, None, "lat", None),
            P(),
            P("depth", "lat", None),
            P("depth", "lat", None),
            P("depth", None, None, None),
            P("depth", "lat", None),
        ),
        out_specs=(P("depth", "lat", None), P("depth", "lat", None)),
        check_vma=False,
    )
```

time: 806 us -> 341 us (0.42)
  starting transfers between devices: 393 us -> 135 us
  other arithmetic: 153 us -> 3.71 us
  waiting for transfers between devices: 158 us -> 37.1 us
  Pallas kernels: 0 us -> 105 us
  blocking collectives: 0 us -> 35.8 us
  local copies, waits for them, and re-layouts: 49.8 us -> 19.5 us
  matrix products: 28.6 us -> 0 us
  between operations: 14.1 us -> 1.81 us
    ppermute x90 -> x32, starting transfers between devices: 393 us -> 129 us  [swapped(): received.append(lax.ppermute(rows, 'lat', route))]
    pallas_call x0 -> x36, Pallas kernels: none -> 105 us  [call(): pl.pallas_call(kernel, name=name, out_shape=shapes, in_specs=[SMEM if arg...]
    ppermute x90 -> x32, waiting for transfers between devices: 105 us -> 8.86 us  [swapped(): received.append(lax.ppermute(rows, 'lat', route))]
    all_gather x1 -> x0, waiting for transfers between devices: 52.5 us -> none  [per_device(): band = lax.all_gather(band, 'depth', axis=0, tiled=True)]
    add x45 -> x0, other arithmetic: 48 us -> none  [the longest x15 37.2 us: advance(): band_product(rows, band) + stencil_rows(rows, padded)]
    dynamic_slice x60 -> x1, local copies, waits for them, and re-layouts: 44.2 us -> 0.59 us  [per_device(): lax.dynamic_slice_in_dim(freq_index, member, 1).astype(F32) + 1.0]
    all_to_all x0 -> x3, blocking collectives: none -> 35.8 us  [exchanged(): return lax.all_to_all(parts, 'depth', 0, 0)]
    scatter x15 -> x0, other arithmetic: 34.2 us -> none  [fore_tick(): keep_s.at[0, micro_slot]]
  transfers between devices with their start and end apart: 91 -> 33, of which waited for: 61 -> 13; matrix products, arithmetic and copies ran while one was open for 12% -> 3% of each run, Pallas kernels for 0% -> 14%
where the time goes in v1:
time: 341 us; the launch traced here: 338 us
  starting transfers between devices  135 us (40%)
  Pallas kernels  105 us (31%)
  waiting for transfers between devices  37.1 us (11%)
  blocking collectives  35.8 us (10%)
  local copies, waits for them, and re-layouts  19.5 us (6%)
  other arithmetic  3.71 us (1%)
    ppermute x32, starting transfers between devices, swapped(): received.append(lax.ppermute(rows, 'lat', route))  129 us
    pallas_call x36, Pallas kernels, call(): pl.pallas_call(kernel, name=name, out_shape=shapes, in_specs=[SMEM if arg...  105 us
    all_to_all x3, blocking collectives, exchanged(): return lax.all_to_all(parts, 'depth', 0, 0)  35.8 us
    all_to_all x1, waiting for transfers between devices, exchanged(): return lax.all_to_all(parts, 'depth', 0, 0)  28.3 us
    unnamed x106, local copies, waits for them, and re-layouts  18 us
    ppermute x32, waiting for transfers between devices, swapped(): received.append(lax.ppermute(rows, 'lat', route))  8.86 us
  transfers between devices with their start and end apart: 33, of which 13 were waited for; matrix products, arithmetic and copies ran while one was open for 3% of the time, Pallas kernels for 14%

profile of v1, /device:TPU:6, one launch (start us, length us, event | category | flops | bytes accessed | tf_op | source)
XLA Modules:
  0.0 337.9 jit_solution(4995217051041583929)
XLA Ops:
  3.4 6.1 %all-to-all-start = ((bf16[8,640,256]{2,1,0:T(8,128)(2,1)}), bf16[8,640,256]{2,1,0:T(8,128)(2,1)S(1)}, u32[]{:S(2)}, u32[]{:S(2)}) async-start(bf16[8,640,256]{2,1,0:T(8,128)(2,1)} %pack.1), calls=%async_computation | async-start | bytes 5242880 | tf_op jit(solution)/shard_map/all_to_all | solution.py:303
  12.2 28.3 %all-to-all-done.packed_ref.refs_0_.packed.refs_1_ = bf16[8,640,256]{2,1,0:T(8,128)(2,1)S(1)} async-done(((bf16[8,640,256]{2,1,0:T(8,128)(2,1)}), bf16[8,640,256]{2,1,0:T(8,128)(2,1)S(1)}, u32[]{:S(2)}, u32[]{:S(2)}) %all-to-all-start) | async-done | bytes 2621472 | tf_op jit(solution)/shard_map/all_to_all | solution.py:303
  46.6 12.3 %collective-permute-start.1 = (bf16[32,2048]{1,0:T(8,128)(2,1)}, bf16[32,2048]{1,0:T(8,128)(2,1)S(1)}, u32[]{:S(2)}, u32[]{:S(2)}) collective-permute-start(bf16[32,2048]{1,0:T(8,128)(2,1)} %get-tuple-element.73.rows_ref), channel_id=1, source_target_pairs={{1,2},{3,4},{5,6},{7,8},{9,10},{11,12},{13,14},{15,16},{17,18},{19... | collective-permute-start | bytes 393224 | tf_op jit(solution)/shard_map/ppermute | solution.py:298
  68.1 6.5 %collective-permute-start.3 = (bf16[32,2048]{1,0:T(8,128)(2,1)}, bf16[32,2048]{1,0:T(8,128)(2,1)S(1)}, u32[]{:S(2)}, u32[]{:S(2)}) collective-permute-start(bf16[32,2048]{1,0:T(8,128)(2,1)} %get-tuple-element.78.rows_ref), channel_id=1, source_target_pairs={{1,2},{3,4},{5,6},{7,8},{9,10},{11,12},{13,14},{15,16},{17,18},{19... | collective-permute-start | bytes 393224 | tf_op jit(solution)/shard_map/ppermute | solution.py:298
  84.0 6.3 %collective-permute-start.5 = (bf16[32,2048]{1,0:T(8,128)(2,1)}, bf16[32,2048]{1,0:T(8,128)(2,1)S(1)}, u32[]{:S(2)}, u32[]{:S(2)}) collective-permute-start(bf16[32,2048]{1,0:T(8,128)(2,1)} %get-tuple-element.83.rows_ref), channel_id=1, source_target_pairs={{1,2},{3,4},{5,6},{7,8},{9,10},{11,12},{13,14},{15,16},{17,18},{19... | collective-permute-start | bytes 393224 | tf_op jit(solution)/shard_map/ppermute | solution.py:298
  99.7 6.2 %collective-permute-start.7 = (bf16[32,2048]{1,0:T(8,128)(2,1)}, bf16[32,2048]{1,0:T(8,128)(2,1)S(1)}, u32[]{:S(2)}, u32[]{:S(2)}) collective-permute-start(bf16[32,2048]{1,0:T(8,128)(2,1)} %get-tuple-element.88.rows_ref), channel_id=1, source_target_pairs={{1,2},{3,4},{5,6},{7,8},{9,10},{11,12},{13,14},{15,16},{17,18},{19... | collective-permute-start | bytes 393224 | tf_op jit(solution)/shard_map/ppermute | solution.py:298
  115.4 6.2 %collective-permute-start.9 = (bf16[32,2048]{1,0:T(8,128)(2,1)}, bf16[32,2048]{1,0:T(8,128)(2,1)S(1)}, u32[]{:S(2)}, u32[]{:S(2)}) collective-permute-start(bf16[32,2048]{1,0:T(8,128)(2,1)} %get-tuple-element.93.rows_ref), channel_id=1, source_target_pairs={{1,2},{3,4},{5,6},{7,8},{9,10},{11,12},{13,14},{15,16},{17,18},{19... | collective-permute-start | bytes 393224 | tf_op jit(solution)/shard_map/ppermute | solution.py:298
  131.1 6.2 %collective-permute-start.11 = (bf16[32,2048]{1,0:T(8,128)(2,1)}, bf16[32,2048]{1,0:T(8,128)(2,1)S(1)}, u32[]{:S(2)}, u32[]{:S(2)}) collective-permute-start(bf16[32,2048]{1,0:T(8,128)(2,1)} %get-tuple-element.98.rows_ref), channel_id=1, source_target_pairs={{1,2},{3,4},{5,6},{7,8},{9,10},{11,12},{13,14},{15,16},{17,18},{19... | collective-permute-start | bytes 393224 | tf_op jit(solution)/shard_map/ppermute | solution.py:298
  146.8 6.2 %collective-permute-start.13 = (bf16[32,2048]{1,0:T(8,128)(2,1)}, bf16[32,2048]{1,0:T(8,128)(2,1)S(1)}, u32[]{:S(2)}, u32[]{:S(2)}) collective-permute-start(bf16[32,2048]{1,0:T(8,128)(2,1)} %get-tuple-element.103.rows_ref), channel_id=1, source_target_pairs={{1,2},{3,4},{5,6},{7,8},{9,10},{11,12},{13,14},{15,16},{17,18},{19... | collective-permute-start | bytes 393224 | tf_op jit(solution)/shard_map/ppermute | solution.py:298
  157.7 3.1 step.14
  162.9 6.1 %collective-permute-start.15 = (bf16[32,2048]{1,0:T(8,128)(2,1)}, bf16[32,2048]{1,0:T(8,128)(2,1)}, u32[]{:S(2)}, u32[]{:S(2)}) collective-permute-start(bf16[32,2048]{1,0:T(8,128)(2,1)} %get-tuple-element.108.rows_ref), channel_id=1, source_target_pairs={{1,2},{3,4},{5,6},{7,8},{9,10},{11,12},{13,14},{15,16},{17,18},{19... | collective-permute-start | bytes 393224 | tf_op jit(solution)/shard_map/ppermute | solution.py:298
  175.0 11.2 %all_to_all.20.parts_ref = f32[8,8,2048]{2,1,0:T(8,128)} all-to-all(f32[8,8,2048]{2,1,0:T(8,128)S(1)} %get-tuple-element.146), channel_id=1, replica_groups=mesh['depth'=8,'lat'=64] {'depth'}, dimensions={0} | all-to-all | bytes 1048576 | tf_op jit(solution)/shard_map/all_to_all | solution.py:303
  188.2 12.8 %all_to_all.21.masked.refs_9_ = f32[8,8,2048]{2,1,0:T(8,128)} all-to-all(f32[8,8,2048]{2,1,0:T(8,128)} %get-tuple-element.112), channel_id=1, replica_groups=mesh['depth'=8,'lat'=64] {'depth'}, dimensions={0} | all-to-all | bytes 1048576 | tf_op jit(solution)/shard_map/all_to_all | solution.py:303
  205.4 5.3 %collective-permute-start.17 = (bf16[16,2048]{1,0:T(8,128)(2,1)}, bf16[16,2048]{1,0:T(8,128)(2,1)S(1)}, u32[]{:S(2)}, u32[]{:S(2)}) collective-permute-start(bf16[16,2048]{1,0:T(8,128)(2,1)} %get-tuple-element.114.rows_ref), channel_id=1, source_target_pairs={{1,2},{3,4},{5,6},{7,8},{9,10},{11,12},{13,14},{15,16},{17,18},{19... | collective-permute-start | bytes 196616 | tf_op jit(solution)/shard_map/ppermute | solution.py:298
  220.5 5.3 %collective-permute-start.19 = (bf16[16,2048]{1,0:T(8,128)(2,1)}, bf16[16,2048]{1,0:T(8,128)(2,1)S(1)}, u32[]{:S(2)}, u32[]{:S(2)}) collective-permute-start(bf16[16,2048]{1,0:T(8,128)(2,1)} %get-tuple-element.117.rows_ref), channel_id=1, source_target_pairs={{1,2},{3,4},{5,6},{7,8},{9,10},{11,12},{13,14},{15,16},{17,18},{19... | collective-permute-start | bytes 196616 | tf_op jit(solution)/shard_map/ppermute | solution.py:298
  225.7 3.1 middle_back.9.refs_3_
  235.5 5.3 %collective-permute-start.21 = (bf16[16,2048]{1,0:T(8,128)(2,1)}, bf16[16,2048]{1,0:T(8,128)(2,1)S(1)}, u32[]{:S(2)}, u32[]{:S(2)}) collective-permute-start(bf16[16,2048]{1,0:T(8,128)(2,1)} %get-tuple-element.120.rows_ref), channel_id=1, source_target_pairs={{1,2},{3,4},{5,6},{7,8},{9,10},{11,12},{13,14},{15,16},{17,18},{19... | collective-permute-start | bytes 196616 | tf_op jit(solution)/shard_map/ppermute | solution.py:298
  240.7 3.1 middle_back.10.refs_3_
  250.5 5.3 %collective-permute-start.23 = (bf16[16,2048]{1,0:T(8,128)(2,1)}, bf16[16,2048]{1,0:T(8,128)(2,1)S(1)}, u32[]{:S(2)}, u32[]{:S(2)}) collective-permute-start(bf16[16,2048]{1,0:T(8,128)(2,1)} %get-tuple-element.123.rows_ref), channel_id=1, source_target_pairs={{1,2},{3,4},{5,6},{7,8},{9,10},{11,12},{13,14},{15,16},{17,18},{19... | collective-permute-start | bytes 196616 | tf_op jit(solution)/shard_map/ppermute | solution.py:298
  265.5 5.3 %collective-permute-start.25 = (bf16[16,2048]{1,0:T(8,128)(2,1)}, bf16[16,2048]{1,0:T(8,128)(2,1)S(1)}, u32[]{:S(2)}, u32[]{:S(2)}) collective-permute-start(bf16[16,2048]{1,0:T(8,128)(2,1)} %get-tuple-element.126.rows_ref), channel_id=1, source_target_pairs={{1,2},{3,4},{5,6},{7,8},{9,10},{11,12},{13,14},{15,16},{17,18},{19... | collective-permute-start | bytes 196616 | tf_op jit(solution)/shard_map/ppermute | solution.py:298
  280.5 5.3 %collective-permute-start.27 = (bf16[16,2048]{1,0:T(8,128)(2,1)}, bf16[16,2048]{1,0:T(8,128)(2,1)S(1)}, u32[]{:S(2)}, u32[]{:S(2)}) collective-permute-start(bf16[16,2048]{1,0:T(8,128)(2,1)} %get-tuple-element.129.rows_ref), channel_id=1, source_target_pairs={{1,2},{3,4},{5,6},{7,8},{9,10},{11,12},{13,14},{15,16},{17,18},{19... | collective-permute-start | bytes 196616 | tf_op jit(solution)/shard_map/ppermute | solution.py:298
  295.5 5.3 %collective-permute-start.29 = (bf16[16,2048]{1,0:T(8,128)(2,1)}, bf16[16,2048]{1,0:T(8,128)(2,1)S(1)}, u32[]{:S(2)}, u32[]{:S(2)}) collective-permute-start(bf16[16,2048]{1,0:T(8,128)(2,1)} %get-tuple-element.132.rows_ref), channel_id=1, source_target_pairs={{1,2},{3,4},{5,6},{7,8},{9,10},{11,12},{13,14},{15,16},{17,18},{19... | collective-permute-start | bytes 196616 | tf_op jit(solution)/shard_map/ppermute | solution.py:298
  310.7 5.3 %collective-permute-start.31 = (bf16[16,2048]{1,0:T(8,128)(2,1)}, bf16[16,2048]{1,0:T(8,128)(2,1)S(1)}, u32[]{:S(2)}, u32[]{:S(2)}) collective-permute-start(bf16[16,2048]{1,0:T(8,128)(2,1)} %get-tuple-element.135.rows_ref), channel_id=1, source_target_pairs={{1,2},{3,4},{5,6},{7,8},{9,10},{11,12},{13,14},{15,16},{17,18},{19... | collective-permute-start | bytes 196616 | tf_op jit(solution)/shard_map/ppermute | solution.py:298
  324.4 11.8 %all_to_all.22.parts_ref = f32[8,8,2048]{2,1,0:T(8,128)} all-to-all(f32[8,8,2048]{2,1,0:T(8,128)S(1)} %bitcast_dynamic-update-slice_fusion), channel_id=1, replica_groups=mesh['depth'=8,'lat'=64] {'depth'}, dimensions={0} | all-to-all | bytes 1048576 | tf_op jit(solution)/shard_map/all_to_all | solution.py:303
  (194 shorter events, 158.5 us)
Async XLA Ops:
  3.4 37.2 %all-to-all-start = ((bf16[8,640,256]{2,1,0:T(8,128)(2,1)}), bf16[8,640,256]{2,1,0:T(8,128)(2,1)S(1)}, u32[]{:S(2)}, u32[]{:S(2)}) async-start(bf16[8,640,256]{2,1,0:T(8,128)(2,1)} %pack.1), calls=%async_computation | async-start | bytes 5242880 | tf_op jit(solution)/shard_map/all_to_all | solution.py:303
  44.7 17.8 %collective-permute-start = (bf16[32,2048]{1,0:T(8,128)(2,1)}, bf16[32,2048]{1,0:T(8,128)(2,1)S(1)}, u32[]{:S(2)}, u32[]{:S(2)}) collective-permute-start(bf16[32,2048]{1,0:T(8,128)(2,1)} %get-tuple-element.73.rows_ref), channel_id=1, source_target_pairs={{0,1},{2,3},{4,5},{6,7},{8,9},{10,11},{12,13},{14,15},{16,17},{18,... | collective-permute-start | bytes 393224 | tf_op jit(solution)/shard_map/ppermute | solution.py:298
  46.6 15.9 %collective-permute-start.1 = (bf16[32,2048]{1,0:T(8,128)(2,1)}, bf16[32,2048]{1,0:T(8,128)(2,1)S(1)}, u32[]{:S(2)}, u32[]{:S(2)}) collective-permute-start(bf16[32,2048]{1,0:T(8,128)(2,1)} %get-tuple-element.73.rows_ref), channel_id=1, source_target_pairs={{1,2},{3,4},{5,6},{7,8},{9,10},{11,12},{13,14},{15,16},{17,18},{19... | collective-permute-start | bytes 393224 | tf_op jit(solution)/shard_map/ppermute | solution.py:298
  66.2 12.2 %collective-permute-start.2 = (bf16[32,2048]{1,0:T(8,128)(2,1)}, bf16[32,2048]{1,0:T(8,128)(2,1)S(1)}, u32[]{:S(2)}, u32[]{:S(2)}) collective-permute-start(bf16[32,2048]{1,0:T(8,128)(2,1)} %get-tuple-element.78.rows_ref), channel_id=1, source_target_pairs={{0,1},{2,3},{4,5},{6,7},{8,9},{10,11},{12,13},{14,15},{16,17},{18,... | collective-permute-start | bytes 393224 | tf_op jit(solution)/shard_map/ppermute | solution.py:298
  68.1 10.3 %collective-permute-start.3 = (bf16[32,2048]{1,0:T(8,128)(2,1)}, bf16[32,2048]{1,0:T(8,128)(2,1)S(1)}, u32[]{:S(2)}, u32[]{:S(2)}) collective-permute-start(bf16[32,2048]{1,0:T(8,128)(2,1)} %get-tuple-element.78.rows_ref), channel_id=1, source_target_pairs={{1,2},{3,4},{5,6},{7,8},{9,10},{11,12},{13,14},{15,16},{17,18},{19... | collective-permute-start | bytes 393224 | tf_op jit(solution)/shard_map/ppermute | solution.py:298
  82.1 12.0 %collective-permute-start.4 = (bf16[32,2048]{1,0:T(8,128)(2,1)}, bf16[32,2048]{1,0:T(8,128)(2,1)S(1)}, u32[]{:S(2)}, u32[]{:S(2)}) collective-permute-start(bf16[32,2048]{1,0:T(8,128)(2,1)} %get-tuple-element.83.rows_ref), channel_id=1, source_target_pairs={{0,1},{2,3},{4,5},{6,7},{8,9},{10,11},{12,13},{14,15},{16,17},{18,... | collective-permute-start | bytes 393224 | tf_op jit(solution)/shard_map/ppermute | solution.py:298
  84.0 10.1 %collective-permute-start.5 = (bf16[32,2048]{1,0:T(8,128)(2,1)}, bf16[32,2048]{1,0:T(8,128)(2,1)S(1)}, u32[]{:S(2)}, u32[]{:S(2)}) collective-permute-start(bf16[32,2048]{1,0:T(8,128)(2,1)} %get-tuple-element.83.rows_ref), channel_id=1, source_target_pairs={{1,2},{3,4},{5,6},{7,8},{9,10},{11,12},{13,14},{15,16},{17,18},{19... | collective-permute-start | bytes 393224 | tf_op jit(solution)/shard_map/ppermute | solution.py:298
  97.8 11.9 %collective-permute-start.6 = (bf16[32,2048]{1,0:T(8,128)(2,1)}, bf16[32,2048]{1,0:T(8,128)(2,1)S(1)}, u32[]{:S(2)}, u32[]{:S(2)}) collective-permute-start(bf16[32,2048]{1,0:T(8,128)(2,1)} %get-tuple-element.88.rows_ref), channel_id=1, source_target_pairs={{0,1},{2,3},{4,5},{6,7},{8,9},{10,11},{12,13},{14,15},{16,17},{18,... | collective-permute-start | bytes 393224 | tf_op jit(solution)/shard_map/ppermute | solution.py:298
  99.7 10.1 %collective-permute-start.7 = (bf16[32,2048]{1,0:T(8,128)(2,1)}, bf16[32,2048]{1,0:T(8,128)(2,1)S(1)}, u32[]{:S(2)}, u32[]{:S(2)}) collective-permute-start(bf16[32,2048]{1,0:T(8,128)(2,1)} %get-tuple-element.88.rows_ref), channel_id=1, source_target_pairs={{1,2},{3,4},{5,6},{7,8},{9,10},{11,12},{13,14},{15,16},{17,18},{19... | collective-permute-start | bytes 393224 | tf_op jit(solution)/shard_map/ppermute | solution.py:298
  113.5 12.0 %collective-permute-start.8 = (bf16[32,2048]{1,0:T(8,128)(2,1)}, bf16[32,2048]{1,0:T(8,128)(2,1)S(1)}, u32[]{:S(2)}, u32[]{:S(2)}) collective-permute-start(bf16[32,2048]{1,0:T(8,128)(2,1)} %get-tuple-element.93.rows_ref), channel_id=1, source_target_pairs={{0,1},{2,3},{4,5},{6,7},{8,9},{10,11},{12,13},{14,15},{16,17},{18,... | collective-permute-start | bytes 393224 | tf_op jit(solution)/shard_map/ppermute | solution.py:298
  129.2 11.9 %collective-permute-start.10 = (bf16[32,2048]{1,0:T(8,128)(2,1)}, bf16[32,2048]{1,0:T(8,128)(2,1)S(1)}, u32[]{:S(2)}, u32[]{:S(2)}) collective-permute-start(bf16[32,2048]{1,0:T(8,128)(2,1)} %get-tuple-element.98.rows_ref), channel_id=1, source_target_pairs={{0,1},{2,3},{4,5},{6,7},{8,9},{10,11},{12,13},{14,15},{16,17},{18,... | collective-permute-start | bytes 393224 | tf_op jit(solution)/shard_map/ppermute | solution.py:298
  131.1 10.1 %collective-permute-start.11 = (bf16[32,2048]{1,0:T(8,128)(2,1)}, bf16[32,2048]{1,0:T(8,128)(2,1)S(1)}, u32[]{:S(2)}, u32[]{:S(2)}) collective-permute-start(bf16[32,2048]{1,0:T(8,128)(2,1)} %get-tuple-element.98.rows_ref), channel_id=1, source_target_pairs={{1,2},{3,4},{5,6},{7,8},{9,10},{11,12},{13,14},{15,16},{17,18},{19... | collective-permute-start | bytes 393224 | tf_op jit(solution)/shard_map/ppermute | solution.py:298
  144.9 11.9 %collective-permute-start.12 = (bf16[32,2048]{1,0:T(8,128)(2,1)}, bf16[32,2048]{1,0:T(8,128)(2,1)S(1)}, u32[]{:S(2)}, u32[]{:S(2)}) collective-permute-start(bf16[32,2048]{1,0:T(8,128)(2,1)} %get-tuple-element.103.rows_ref), channel_id=1, source_target_pairs={{0,1},{2,3},{4,5},{6,7},{8,9},{10,11},{12,13},{14,15},{16,17},{18,... | collective-permute-start | bytes 393224 | tf_op jit(solution)/shard_map/ppermute | solution.py:298
  146.8 10.2 %collective-permute-start.13 = (bf16[32,2048]{1,0:T(8,128)(2,1)}, bf16[32,2048]{1,0:T(8,128)(2,1)S(1)}, u32[]{:S(2)}, u32[]{:S(2)}) collective-permute-start(bf16[32,2048]{1,0:T(8,128)(2,1)} %get-tuple-element.103.rows_ref), channel_id=1, source_target_pairs={{1,2},{3,4},{5,6},{7,8},{9,10},{11,12},{13,14},{15,16},{17,18},{19... | collective-permute-start | bytes 393224 | tf_op jit(solution)/shard_map/ppermute | solution.py:298
  160.8 11.9 %collective-permute-start.14 = (bf16[32,2048]{1,0:T(8,128)(2,1)}, bf16[32,2048]{1,0:T(8,128)(2,1)S(1)}, u32[]{:S(2)}, u32[]{:S(2)}) collective-permute-start(bf16[32,2048]{1,0:T(8,128)(2,1)} %get-tuple-element.108.rows_ref), channel_id=1, source_target_pairs={{0,1},{2,3},{4,5},{6,7},{8,9},{10,11},{12,13},{14,15},{16,17},{18,... | collective-permute-start | bytes 393224 | tf_op jit(solution)/shard_map/ppermute | solution.py:298
  162.9 10.3 %collective-permute-start.15 = (bf16[32,2048]{1,0:T(8,128)(2,1)}, bf16[32,2048]{1,0:T(8,128)(2,1)}, u32[]{:S(2)}, u32[]{:S(2)}) collective-permute-start(bf16[32,2048]{1,0:T(8,128)(2,1)} %get-tuple-element.108.rows_ref), channel_id=1, source_target_pairs={{1,2},{3,4},{5,6},{7,8},{9,10},{11,12},{13,14},{15,16},{17,18},{19... | collective-permute-start | bytes 393224 | tf_op jit(solution)/shard_map/ppermute | solution.py:298
  203.5 10.9 %collective-permute-start.16 = (bf16[16,2048]{1,0:T(8,128)(2,1)}, bf16[16,2048]{1,0:T(8,128)(2,1)S(1)}, u32[]{:S(2)}, u32[]{:S(2)}) collective-permute-start(bf16[16,2048]{1,0:T(8,128)(2,1)} %get-tuple-element.114.rows_ref), channel_id=1, source_target_pairs={{0,1},{2,3},{4,5},{6,7},{8,9},{10,11},{12,13},{14,15},{16,17},{18,... | collective-permute-start | bytes 196616 | tf_op jit(solution)/shard_map/ppermute | solution.py:298
  218.6 10.3 %collective-permute-start.18 = (bf16[16,2048]{1,0:T(8,128)(2,1)}, bf16[16,2048]{1,0:T(8,128)(2,1)S(1)}, u32[]{:S(2)}, u32[]{:S(2)}) collective-permute-start(bf16[16,2048]{1,0:T(8,128)(2,1)} %get-tuple-element.117.rows_ref), channel_id=1, source_target_pairs={{0,1},{2,3},{4,5},{6,7},{8,9},{10,11},{12,13},{14,15},{16,17},{18,... | collective-permute-start | bytes 196616 | tf_op jit(solution)/shard_map/ppermute | solution.py:298
  233.6 10.3 %collective-permute-start.20 = (bf16[16,2048]{1,0:T(8,128)(2,1)}, bf16[16,2048]{1,0:T(8,128)(2,1)S(1)}, u32[]{:S(2)}, u32[]{:S(2)}) collective-permute-start(bf16[16,2048]{1,0:T(8,128)(2,1)} %get-tuple-element.120.rows_ref), channel_id=1, source_target_pairs={{0,1},{2,3},{4,5},{6,7},{8,9},{10,11},{12,13},{14,15},{16,17},{18,... | collective-permute-start | bytes 196616 | tf_op jit(solution)/shard_map/ppermute | solution.py:298
  248.6 10.3 %collective-permute-start.22 = (bf16[16,2048]{1,0:T(8,128)(2,1)}, bf16[16,2048]{1,0:T(8,128)(2,1)S(1)}, u32[]{:S(2)}, u32[]{:S(2)}) collective-permute-start(bf16[16,2048]{1,0:T(8,128)(2,1)} %get-tuple-element.123.rows_ref), channel_id=1, source_target_pairs={{0,1},{2,3},{4,5},{6,7},{8,9},{10,11},{12,13},{14,15},{16,17},{18,... | collective-permute-start | bytes 196616 | tf_op jit(solution)/shard_map/ppermute | solution.py:298
  263.6 10.2 %collective-permute-start.24 = (bf16[16,2048]{1,0:T(8,128)(2,1)}, bf16[16,2048]{1,0:T(8,128)(2,1)S(1)}, u32[]{:S(2)}, u32[]{:S(2)}) collective-permute-start(bf16[16,2048]{1,0:T(8,128)(2,1)} %get-tuple-element.126.rows_ref), channel_id=1, source_target_pairs={{0,1},{2,3},{4,5},{6,7},{8,9},{10,11},{12,13},{14,15},{16,17},{18,... | collective-permute-start | bytes 196616 | tf_op jit(solution)/shard_map/ppermute | solution.py:298
  278.6 10.2 %collective-permute-start.26 = (bf16[16,2048]{1,0:T(8,128)(2,1)}, bf16[16,2048]{1,0:T(8,128)(2,1)S(1)}, u32[]{:S(2)}, u32[]{:S(2)}) collective-permute-start(bf16[16,2048]{1,0:T(8,128)(2,1)} %get-tuple-element.129.rows_ref), channel_id=1, source_target_pairs={{0,1},{2,3},{4,5},{6,7},{8,9},{10,11},{12,13},{14,15},{16,17},{18,... | collective-permute-start | bytes 196616 | tf_op jit(solution)/shard_map/ppermute | solution.py:298
  293.6 10.2 %collective-permute-start.28 = (bf16[16,2048]{1,0:T(8,128)(2,1)}, bf16[16,2048]{1,0:T(8,128)(2,1)S(1)}, u32[]{:S(2)}, u32[]{:S(2)}) collective-permute-start(bf16[16,2048]{1,0:T(8,128)(2,1)} %get-tuple-element.132.rows_ref), channel_id=1, source_target_pairs={{0,1},{2,3},{4,5},{6,7},{8,9},{10,11},{12,13},{14,15},{16,17},{18,... | collective-permute-start | bytes 196616 | tf_op jit(solution)/shard_map/ppermute | solution.py:298
  308.6 10.4 %collective-permute-start.30 = (bf16[16,2048]{1,0:T(8,128)(2,1)}, bf16[16,2048]{1,0:T(8,128)(2,1)S(1)}, u32[]{:S(2)}, u32[]{:S(2)}) collective-permute-start(bf16[16,2048]{1,0:T(8,128)(2,1)} %get-tuple-element.135.rows_ref), channel_id=1, source_target_pairs={{0,1},{2,3},{4,5},{6,7},{8,9},{10,11},{12,13},{14,15},{16,17},{18,... | collective-permute-start | bytes 196616 | tf_op jit(solution)/shard_map/ppermute | solution.py:298
  (55 other events, 375.1 us)

commit v2 on v1

--- a/solution.py
+++ b/solution.py
@@ -10,7 +10,7 @@
 HALO = 8
 BLOCK = 128
 PAIR = 2 * BLOCK
-CENTRE, EDGE, SLOW, COEF, PACKED = 0, 256, 384, 512, 640
+CENTRE, EDGE, SLOW, COEF, PACKED = 0, 256, 384, 640, 704
 VMEM = pl.BlockSpec(memory_space=pltpu.VMEM)
 SMEM = pl.BlockSpec(memory_space=pltpu.SMEM)
 F32, BF16 = jnp.float32, jnp.bfloat16
@@ -42,8 +42,8 @@
 
 def side_weights(combos):
     after, before = (stencil_matrix(combos, HALO), stencil_matrix(combos, -HALO))
-    even = split_weights(np.concatenate([after, before], axis=1))
-    odd = split_weights(np.concatenate([before, after], axis=1))
+    even = split_weights(np.concatenate([before, after], axis=1))
+    odd = split_weights(np.concatenate([after, before], axis=1))
     return np.stack([even, odd])
 
 
@@ -84,10 +84,22 @@
     return slice(chunk * PAIR, (chunk + 1) * PAIR)
 
 
-def joined(packed_ref, level, base, chunk):
-    start = base + chunk * 2 * HALO
-    both = packed_ref[level, start : start + 2 * HALO, :].astype(F32)
-    return both[:HALO] + both[HALO:]
+def slowness_of(packed_ref, level, chunk):
+    start = SLOW + chunk * 4 * HALO
+    value = packed_ref[level, start : start + 4 * HALO, :].astype(F32)
+    return value[:HALO] + value[HALO : 2 * HALO] + value[2 * HALO : 3 * HALO]
+
+
+def coef_of(packed_ref, level, chunk):
+    start = SLOW + chunk * 4 * HALO + 2 * HALO
+    high = packed_ref[level, start : start + 2 * HALO, :].astype(F32)[HALO:]
+    start = COEF + chunk // 2 * 2 * HALO
+    low = packed_ref[level, start : start + 2 * HALO, :].astype(F32)
+    return high + (low[:HALO] if chunk % 2 == 0 else low[HALO:])
+
+
+def rounded(value):
+    return value.astype(BF16).astype(F32)
 
 
 def pack_kernel(slow_ref, coef_ref, band_ref, out_ref):
@@ -104,13 +116,21 @@
     write(slice(BLOCK, PAIR), right, band_ref[1, 1])
     write(slice(EDGE, EDGE + BLOCK), left, band_ref[0, 0])
     write(slice(EDGE, EDGE + BLOCK), right, band_ref[1, 2])
-    for ref, base in ((slow_ref, SLOW), (coef_ref, COEF)):
-        for chunk in range(ref.shape[2] // PAIR):
-            value = ref[0, :, columns(chunk)]
-            high = value.astype(BF16).astype(F32)
-            pair = jnp.concatenate([high, value - high], axis=0).astype(BF16)
-            start = base + chunk * 2 * HALO
-            write(slice(start, start + 2 * HALO), slice(0, PAIR), pair)
+    lows = []
+    for chunk in range(slow_ref.shape[2] // PAIR):
+        slow = slow_ref[0, :, columns(chunk)]
+        coef = coef_ref[0, :, columns(chunk)]
+        high = rounded(slow)
+        middle = rounded(slow - high)
+        coef_high = rounded(coef)
+        lows.append(coef - coef_high)
+        pieces = jnp.concatenate([high, middle, slow - high - middle, coef_high], axis=0)
+        start = SLOW + chunk * 4 * HALO
+        write(slice(start, start + 4 * HALO), slice(0, PAIR), pieces.astype(BF16))
+    for half in range(len(lows) // 2):
+        start = COEF + half * 2 * HALO
+        pieces = jnp.concatenate(lows[2 * half : 2 * half + 2], axis=0)
+        write(slice(start, start + 2 * HALO), slice(0, PAIR), pieces.astype(BF16))
 
 
 def phase(fields, cosine, sine):
@@ -127,7 +147,7 @@
     omega = omega_ref[0]
     for chunk in range(packed_ref.shape[0]):
         cols = columns(chunk)
-        cosine, sine = cos_sin(omega * joined(packed_ref, 0, SLOW, chunk))
+        cosine, sine = cos_sin(omega * slowness_of(packed_ref, 0, chunk))
         angle_ref[0:HALO, cols] = cosine
         angle_ref[HALO : 2 * HALO, cols] = sine
         phased = phase(fields_ref[:, cols].astype(F32), cosine, sine)
@@ -155,7 +175,7 @@
             right = dot(after, packed_ref[pair, EDGE : EDGE + BLOCK, BLOCK:PAIR])
         lateral_ref[:, cols] = total + jnp.concatenate([left, right], axis=1)
         if angle_refs:
-            cosine, sine = cos_sin(omega * joined(packed_ref, level + 1, SLOW, pair))
+            cosine, sine = cos_sin(omega * slowness_of(packed_ref, level + 1, pair))
             angle_refs[0][0:HALO, cols] = cosine
             angle_refs[0][HALO : 2 * HALO, cols] = sine
 
@@ -176,7 +196,7 @@
     for chunk in range(packed.shape[0]):
         cols = columns(chunk)
         total = lateral[:, cols] + sides(weights, first, second, cols)
-        coef = joined(packed, level, COEF, chunk)
+        coef = coef_of(packed, level, chunk)
         value = phased[:, cols]
         part = [slice(k * HALO, (k + 1) * HALO) for k in range(4)]
         source_re = value[part[0]] - coef * total[part[1]]
@@ -228,7 +248,7 @@
         cols = columns(chunk)
         value = weighted(masked[level, :, cols], state[:, cols])
         adjoint[:, cols] = value
-        scaled[:, cols] = scaled_rows(value, joined(packed, level, COEF, chunk))
+        scaled[:, cols] = scaled_rows(value, coef_of(packed, level, chunk))
 
 
 def middle_back_kernel(packed_ref, weights_ref, rows_ref, lateral_ref):
@@ -274,28 +294,55 @@
             upward = upward.astype(BF16).astype(F32)
             following = weighted(masked[level - 1, :, cols], state[:, cols]) + upward
             adjoint_next[:, cols] = following
-            scaled_next[:, cols] = scaled_rows(following, joined(packed, level - 1, COEF, chunk))
-
-
-def call(kernel, name, outs, cost, *args):
-    shapes = [jax.ShapeDtypeStruct(shape, kind) for shape, kind in outs]
+            scaled_next[:, cols] = scaled_rows(following, coef_of(packed, level - 1, chunk))
+
+
+def call(kernel, name, outs, cost, *args, local=True):
+    kind_of = pltpu.VMEM if local else jax.ShapeDtypeStruct
+    placed = []
+    for arg in args:
+        scalar = arg.shape == (1,)
+        placed.append(arg if scalar else pltpu.with_memory_space_constraint(arg, pltpu.VMEM))
     return pl.pallas_call(
         kernel,
         name=name,
-        out_shape=shapes,
+        out_shape=[kind_of(shape, kind) for shape, kind in outs],
         in_specs=[SMEM if arg.shape == (1,) else VMEM for arg in args],
-        out_specs=[VMEM] * len(shapes),
+        out_specs=[VMEM] * len(outs),
         cost_estimate=pl.CostEstimate(flops=cost, bytes_accessed=1 << 20, transcendentals=0),
-    )(*args)
+        compiler_params=pltpu.CompilerParams(vmem_limit_bytes=8 << 20),
+    )(*placed)
+
+
+def stack_kernel(*refs):
+    for index, ref in enumerate(refs[:-1]):
+        refs[-1][index] = ref[...]
+
+
+def stacked(parts):
+    shape = (len(parts),) + parts[0].shape
+    return call(stack_kernel, "stack", [(shape, F32)], 1000, *parts)[0]
+
+
+def frequency_of(depth, lat, sections, size):
+    upper = lat >= size // 2
+    return (depth + upper * (sections // 2)) % sections
 
 
 def swapped(rows):
-    size = lax.axis_size("lat")
+    sections, size = (lax.axis_size("depth"), lax.axis_size("lat"))
+    place = {}
+    for depth in range(sections):
+        for lat in range(size):
+            place[frequency_of(depth, lat, sections, size), lat] = depth * size + lat
     received = []
-    for offset in (0, 1):
-        pairs = [(i, i + 1) for i in range(offset, size - 1, 2)]
-        route = [(a, b) for a, b in pairs] + [(b, a) for a, b in pairs]
-        received.append(lax.ppermute(rows, "lat", route))
+    for offset in (1, 0):
+        route = []
+        for member in range(sections):
+            for lat in range(offset, size - 1, 2):
+                one, other = (place[member, lat], place[member, lat + 1])
+                route += [(one, other), (other, one)]
+        received.append(lax.ppermute(rows, ("depth", "lat"), route))
     return received
 
 
@@ -305,11 +352,12 @@
 
 def per_device(source_field, receiver_field, freq_index, slowness, ffd_coef, band, image_mask):
     sections = lax.axis_size("depth")
-    member = lax.axis_index("depth")
+    lat, size = (lax.axis_index("lat"), lax.axis_size("lat"))
+    member = frequency_of(lax.axis_index("depth"), lat, sections, size)
     height, width = slowness.shape[1:]
     levels = sections
     omega = 0.1 * (lax.dynamic_slice_in_dim(freq_index, member, 1).astype(F32) + 1.0)
-    odd = lax.rem(lax.axis_index("lat"), 2)
+    odd = lax.rem(lat, 2)
     side_fore = jnp.where(odd == 1, *side_weights(4)[::-1])
     side_back = jnp.where(odd == 1, *side_weights(2)[::-1])
     own_fore, own_back = (jnp.asarray(own_weights(4)), jnp.asarray(own_weights(2)))
@@ -357,7 +405,7 @@
         "image",
         [((1,) + single, F32), ((sections,) + single, F32)],
         1000,
-        exchanged(jnp.stack(products)),
+        exchanged(stacked(products)),
         image_mask,
     )
     masked = exchanged(masked)
@@ -390,7 +438,8 @@
         if not last:
             adjoint, scaled = more
     (gradient,) = call(
-        gradient_kernel, "gradient", [((1,) + single, F32)], 1000, exchanged(jnp.stack(terms))
+        gradient_kernel, "gradient", [((1,) + single, F32)], 1000, exchanged(stacked(terms)),
+        local=False,
     )
     return (image, gradient)
 

time: 341 us -> 241 us (0.71)
  Pallas kernels: 105 us -> 14.6 us
  waiting for transfers between devices: 37.1 us -> 71.4 us
  starting transfers between devices: 135 us -> 121 us
  local copies, waits for them, and re-layouts: 19.5 us -> 6.28 us
  blocking collectives: 35.8 us -> 24.7 us
  other arithmetic: 3.71 us -> 0.04 us
    pallas_call x36 -> x39, Pallas kernels: 105 us -> 14.6 us  [call(): pl.pallas_call(kernel, name=name, out_shape=[kind_of(shape, kind) for sha...]
    ppermute x32, waiting for transfers between devices: 8.86 us -> 33.1 us  [swapped(): received.append(lax.ppermute(rows, ('depth', 'lat'), route))]
    ppermute x32, starting transfers between devices: 129 us -> 110 us  [swapped(): received.append(lax.ppermute(rows, ('depth', 'lat'), route))]
    unnamed x106 -> x25, local copies, waits for them, and re-layouts: 18 us -> 4.8 us
    all_to_all x3 -> x2, blocking collectives: 35.8 us -> 24.7 us  [exchanged(): return lax.all_to_all(parts, 'depth', 0, 0)]
    all_to_all x1 -> x2, waiting for transfers between devices: 28.3 us -> 38.3 us  [exchanged(): return lax.all_to_all(parts, 'depth', 0, 0)]
    all_to_all x1 -> x2, starting transfers between devices: 6.06 us -> 10.3 us  [exchanged(): return lax.all_to_all(parts, 'depth', 0, 0)]
  transfers between devices with their start and end apart: 33 -> 34, of which waited for: 13 -> 19; matrix products, arithmetic and copies ran while one was open for 3% -> 1% of each run, Pallas kernels for 14% -> 4%
where the time goes in v2:
time: 241 us; the launch traced here: 240 us
  starting transfers between devices  121 us (50%)
  waiting for transfers between devices  71.4 us (30%)
  blocking collectives  24.7 us (10%)
  Pallas kernels  14.6 us (6%)
  local copies, waits for them, and re-layouts  6.28 us (3%)
    ppermute x32, starting transfers between devices, swapped(): received.append(lax.ppermute(rows, ('depth', 'lat'), route))  110 us
    all_to_all x2, waiting for transfers between devices, exchanged(): return lax.all_to_all(parts, 'depth', 0, 0)  38.3 us
    ppermute x32, waiting for transfers between devices, swapped(): received.append(lax.ppermute(rows, ('depth', 'lat'), route))  33.1 us
    all_to_all x2, blocking collectives, exchanged(): return lax.all_to_all(parts, 'depth', 0, 0)  24.7 us
    pallas_call x39, Pallas kernels, call(): pl.pallas_call(kernel, name=name, out_shape=[kind_of(shape, kind) for sha...  14.6 us
    all_to_all x2, starting transfers between devices, exchanged(): return lax.all_to_all(parts, 'depth', 0, 0)  10.3 us
  transfers between devices with their start and end apart: 34, of which 19 were waited for; matrix products, arithmetic and copies ran while one was open for 1% of the time, Pallas kernels for 4%

profile of v2, /device:TPU:6, one launch (start us, length us, event | category | flops | bytes accessed | tf_op | source)
XLA Modules:
  0.0 239.5 jit_solution(13038183989492097944)
XLA Ops:
  5.1 6.1 %all-to-all-start = ((bf16[8,704,256]{2,1,0:T(8,128)(2,1)}), bf16[8,704,256]{2,1,0:T(8,128)(2,1)S(1)}, u32[]{:S(2)}, u32[]{:S(2)}) async-start(bf16[8,704,256]{2,1,0:T(8,128)(2,1)} %copy-done), calls=%async_computation | async-start | bytes 5767168 | tf_op jit(solution)/shard_map/all_to_all | solution.py:350
  13.4 31.7 %all-to-all-done.packed_ref.refs_0_.packed.refs_1_ = bf16[8,704,256]{2,1,0:T(8,128)(2,1)S(1)} async-done(((bf16[8,704,256]{2,1,0:T(8,128)(2,1)}), bf16[8,704,256]{2,1,0:T(8,128)(2,1)S(1)}, u32[]{:S(2)}, u32[]{:S(2)}) %all-to-all-start) | async-done | bytes 2883616 | tf_op jit(solution)/shard_map/all_to_all | solution.py:350
  45.8 10.6 %collective-permute-start = (bf16[32,2048]{1,0:T(8,128)(2,1)S(1)}, bf16[32,2048]{1,0:T(8,128)(2,1)S(1)}, u32[]{:S(2)}, u32[]{:S(2)}) collective-permute-start(bf16[32,2048]{1,0:T(8,128)(2,1)S(1)} %get-tuple-element.73.rows_ref), channel_id=1, source_target_pairs={{1,2},{2,1},{3,4},{4,3},{5,6},{6,5},{7,8},{8,7},{9,10},{10,9},{11,... | collective-permute-start | bytes 393224 | tf_op jit(solution)/shard_map/ppermute | solution.py:345
  59.9 6.4 %collective-permute-start.2 = (bf16[32,2048]{1,0:T(8,128)(2,1)S(1)}, bf16[32,2048]{1,0:T(8,128)(2,1)S(1)}, u32[]{:S(2)}, u32[]{:S(2)}) collective-permute-start(bf16[32,2048]{1,0:T(8,128)(2,1)S(1)} %get-tuple-element.78.rows_ref), channel_id=1, source_target_pairs={{1,2},{2,1},{3,4},{4,3},{5,6},{6,5},{7,8},{8,7},{9,10},{10,9},{11,... | collective-permute-start | bytes 393224 | tf_op jit(solution)/shard_map/ppermute | solution.py:345
  69.8 6.4 %collective-permute-start.4 = (bf16[32,2048]{1,0:T(8,128)(2,1)S(1)}, bf16[32,2048]{1,0:T(8,128)(2,1)S(1)}, u32[]{:S(2)}, u32[]{:S(2)}) collective-permute-start(bf16[32,2048]{1,0:T(8,128)(2,1)S(1)} %get-tuple-element.83.rows_ref), channel_id=1, source_target_pairs={{1,2},{2,1},{3,4},{4,3},{5,6},{6,5},{7,8},{8,7},{9,10},{10,9},{11,... | collective-permute-start | bytes 393224 | tf_op jit(solution)/shard_map/ppermute | solution.py:345
  79.6 6.4 %collective-permute-start.6 = (bf16[32,2048]{1,0:T(8,128)(2,1)S(1)}, bf16[32,2048]{1,0:T(8,128)(2,1)S(1)}, u32[]{:S(2)}, u32[]{:S(2)}) collective-permute-start(bf16[32,2048]{1,0:T(8,128)(2,1)S(1)} %get-tuple-element.88.rows_ref), channel_id=1, source_target_pairs={{1,2},{2,1},{3,4},{4,3},{5,6},{6,5},{7,8},{8,7},{9,10},{10,9},{11,... | collective-permute-start | bytes 393224 | tf_op jit(solution)/shard_map/ppermute | solution.py:345
  89.5 6.4 %collective-permute-start.8 = (bf16[32,2048]{1,0:T(8,128)(2,1)S(1)}, bf16[32,2048]{1,0:T(8,128)(2,1)S(1)}, u32[]{:S(2)}, u32[]{:S(2)}) collective-permute-start(bf16[32,2048]{1,0:T(8,128)(2,1)S(1)} %get-tuple-element.93.rows_ref), channel_id=1, source_target_pairs={{1,2},{2,1},{3,4},{4,3},{5,6},{6,5},{7,8},{8,7},{9,10},{10,9},{11,... | collective-permute-start | bytes 393224 | tf_op jit(solution)/shard_map/ppermute | solution.py:345
  99.3 6.4 %collective-permute-start.10 = (bf16[32,2048]{1,0:T(8,128)(2,1)S(1)}, bf16[32,2048]{1,0:T(8,128)(2,1)S(1)}, u32[]{:S(2)}, u32[]{:S(2)}) collective-permute-start(bf16[32,2048]{1,0:T(8,128)(2,1)S(1)} %get-tuple-element.98.rows_ref), channel_id=1, source_target_pairs={{1,2},{2,1},{3,4},{4,3},{5,6},{6,5},{7,8},{8,7},{9,10},{10,9},{11,... | collective-permute-start | bytes 393224 | tf_op jit(solution)/shard_map/ppermute | solution.py:345
  109.2 6.4 %collective-permute-start.12 = (bf16[32,2048]{1,0:T(8,128)(2,1)S(1)}, bf16[32,2048]{1,0:T(8,128)(2,1)S(1)}, u32[]{:S(2)}, u32[]{:S(2)}) collective-permute-start(bf16[32,2048]{1,0:T(8,128)(2,1)S(1)} %get-tuple-element.103.rows_ref), channel_id=1, source_target_pairs={{1,2},{2,1},{3,4},{4,3},{5,6},{6,5},{7,8},{8,7},{9,10},{10,9},{11,... | collective-permute-start | bytes 393224 | tf_op jit(solution)/shard_map/ppermute | solution.py:345
  119.0 6.4 %collective-permute-start.14 = (bf16[32,2048]{1,0:T(8,128)(2,1)S(1)}, bf16[32,2048]{1,0:T(8,128)(2,1)S(1)}, u32[]{:S(2)}, u32[]{:S(2)}) collective-permute-start(bf16[32,2048]{1,0:T(8,128)(2,1)S(1)} %get-tuple-element.108.rows_ref), channel_id=1, source_target_pairs={{1,2},{2,1},{3,4},{4,3},{5,6},{6,5},{7,8},{8,7},{9,10},{10,9},{11,... | collective-permute-start | bytes 393224 | tf_op jit(solution)/shard_map/ppermute | solution.py:345
  128.9 12.5 %all_to_all.20.parts_ref = f32[8,8,2048]{2,1,0:T(8,128)S(1)} all-to-all(f32[8,8,2048]{2,1,0:T(8,128)S(1)} %stack.2), channel_id=1, replica_groups=mesh['depth'=8,'lat'=64] {'depth'}, dimensions={0} | all-to-all | bytes 1048576 | tf_op jit(solution)/shard_map/all_to_all | solution.py:350
  141.5 12.2 %all_to_all.21.masked.refs_9_ = f32[8,8,2048]{2,1,0:T(8,128)S(1)} all-to-all(f32[8,8,2048]{2,1,0:T(8,128)S(1)} %get-tuple-element.112), channel_id=1, replica_groups=mesh['depth'=8,'lat'=64] {'depth'}, dimensions={0} | all-to-all | bytes 1048576 | tf_op jit(solution)/shard_map/all_to_all | solution.py:350
  159.0 3.7 %collective-permute-done.16.refs_4_ = bf16[16,2048]{1,0:T(8,128)(2,1)S(1)} collective-permute-done((bf16[16,2048]{1,0:T(8,128)(2,1)S(1)}, bf16[16,2048]{1,0:T(8,128)(2,1)S(1)}, u32[]{:S(2)}, u32[]{:S(2)}) %collective-permute-start.16) | collective-permute-done | bytes 65568 | tf_op jit(solution)/shard_map/ppermute | solution.py:345
  168.6 3.2 %collective-permute-done.18.refs_4_ = bf16[16,2048]{1,0:T(8,128)(2,1)S(1)} collective-permute-done((bf16[16,2048]{1,0:T(8,128)(2,1)S(1)}, bf16[16,2048]{1,0:T(8,128)(2,1)S(1)}, u32[]{:S(2)}, u32[]{:S(2)}) %collective-permute-start.18) | collective-permute-done | bytes 65568 | tf_op jit(solution)/shard_map/ppermute | solution.py:345
  177.7 3.2 %collective-permute-done.20.refs_4_ = bf16[16,2048]{1,0:T(8,128)(2,1)S(1)} collective-permute-done((bf16[16,2048]{1,0:T(8,128)(2,1)S(1)}, bf16[16,2048]{1,0:T(8,128)(2,1)S(1)}, u32[]{:S(2)}, u32[]{:S(2)}) %collective-permute-start.20) | collective-permute-done | bytes 65568 | tf_op jit(solution)/shard_map/ppermute | solution.py:345
  186.8 3.2 %collective-permute-done.22.refs_4_ = bf16[16,2048]{1,0:T(8,128)(2,1)S(1)} collective-permute-done((bf16[16,2048]{1,0:T(8,128)(2,1)S(1)}, bf16[16,2048]{1,0:T(8,128)(2,1)S(1)}, u32[]{:S(2)}, u32[]{:S(2)}) %collective-permute-start.22) | collective-permute-done | bytes 65568 | tf_op jit(solution)/shard_map/ppermute | solution.py:345
  190.2 3.1 %collective-permute-start.24 = (bf16[16,2048]{1,0:T(8,128)(2,1)S(1)}, bf16[16,2048]{1,0:T(8,128)(2,1)S(1)}, u32[]{:S(2)}, u32[]{:S(2)}) collective-permute-start(bf16[16,2048]{1,0:T(8,128)(2,1)S(1)} %get-tuple-element.126.rows_ref), channel_id=1, source_target_pairs={{1,2},{2,1},{3,4},{4,3},{5,6},{6,5},{7,8},{8,7},{9,10},{10,9},{11,... | collective-permute-start | bytes 196616 | tf_op jit(solution)/shard_map/ppermute | solution.py:345
  195.9 3.2 %collective-permute-done.24.refs_4_ = bf16[16,2048]{1,0:T(8,128)(2,1)S(1)} collective-permute-done((bf16[16,2048]{1,0:T(8,128)(2,1)S(1)}, bf16[16,2048]{1,0:T(8,128)(2,1)S(1)}, u32[]{:S(2)}, u32[]{:S(2)}) %collective-permute-start.24) | collective-permute-done | bytes 65568 | tf_op jit(solution)/shard_map/ppermute | solution.py:345
  199.3 3.1 %collective-permute-start.26 = (bf16[16,2048]{1,0:T(8,128)(2,1)S(1)}, bf16[16,2048]{1,0:T(8,128)(2,1)S(1)}, u32[]{:S(2)}, u32[]{:S(2)}) collective-permute-start(bf16[16,2048]{1,0:T(8,128)(2,1)S(1)} %get-tuple-element.129.rows_ref), channel_id=1, source_target_pairs={{1,2},{2,1},{3,4},{4,3},{5,6},{6,5},{7,8},{8,7},{9,10},{10,9},{11,... | collective-permute-start | bytes 196616 | tf_op jit(solution)/shard_map/ppermute | solution.py:345
  205.0 3.2 %collective-permute-done.26.refs_4_ = bf16[16,2048]{1,0:T(8,128)(2,1)S(1)} collective-permute-done((bf16[16,2048]{1,0:T(8,128)(2,1)S(1)}, bf16[16,2048]{1,0:T(8,128)(2,1)S(1)}, u32[]{:S(2)}, u32[]{:S(2)}) %collective-permute-start.26) | collective-permute-done | bytes 65568 | tf_op jit(solution)/shard_map/ppermute | solution.py:345
  214.1 3.2 %collective-permute-done.28.refs_4_ = bf16[16,2048]{1,0:T(8,128)(2,1)S(1)} collective-permute-done((bf16[16,2048]{1,0:T(8,128)(2,1)S(1)}, bf16[16,2048]{1,0:T(8,128)(2,1)S(1)}, u32[]{:S(2)}, u32[]{:S(2)}) %collective-permute-start.28) | collective-permute-done | bytes 65568 | tf_op jit(solution)/shard_map/ppermute | solution.py:345
  223.2 3.2 %collective-permute-done.30.refs_4_ = bf16[16,2048]{1,0:T(8,128)(2,1)S(1)} collective-permute-done((bf16[16,2048]{1,0:T(8,128)(2,1)S(1)}, bf16[16,2048]{1,0:T(8,128)(2,1)S(1)}, u32[]{:S(2)}, u32[]{:S(2)}) %collective-permute-start.30) | collective-permute-done | bytes 65568 | tf_op jit(solution)/shard_map/ppermute | solution.py:345
  227.5 4.2 %all-to-all-start.3 = ((f32[8,8,2048]{2,1,0:T(8,128)}), f32[8,8,2048]{2,1,0:T(8,128)S(1)}, u32[]{:S(2)}, u32[]{:S(2)}) async-start(f32[8,8,2048]{2,1,0:T(8,128)} %stack.3), calls=%async_computation.3 | async-start | bytes 1048576 | tf_op jit(solution)/shard_map/all_to_all | solution.py:350
  232.3 6.6 %all-to-all-done.3.parts_ref = f32[8,8,2048]{2,1,0:T(8,128)S(1)} async-done(((f32[8,8,2048]{2,1,0:T(8,128)}), f32[8,8,2048]{2,1,0:T(8,128)S(1)}, u32[]{:S(2)}, u32[]{:S(2)}) %all-to-all-start.3) | async-done | bytes 524320 | tf_op jit(solution)/shard_map/all_to_all | solution.py:350
  (115 shorter events, 76.9 us)
Async XLA Ops:
  5.1 40.0 %all-to-all-start = ((bf16[8,704,256]{2,1,0:T(8,128)(2,1)}), bf16[8,704,256]{2,1,0:T(8,128)(2,1)S(1)}, u32[]{:S(2)}, u32[]{:S(2)}) async-start(bf16[8,704,256]{2,1,0:T(8,128)(2,1)} %copy-done), calls=%async_computation | async-start | bytes 5767168 | tf_op jit(solution)/shard_map/all_to_all | solution.py:350
  45.8 13.2 %collective-permute-start = (bf16[32,2048]{1,0:T(8,128)(2,1)S(1)}, bf16[32,2048]{1,0:T(8,128)(2,1)S(1)}, u32[]{:S(2)}, u32[]{:S(2)}) collective-permute-start(bf16[32,2048]{1,0:T(8,128)(2,1)S(1)} %get-tuple-element.73.rows_ref), channel_id=1, source_target_pairs={{1,2},{2,1},{3,4},{4,3},{5,6},{6,5},{7,8},{8,7},{9,10},{10,9},{11,... | collective-permute-start | bytes 393224 | tf_op jit(solution)/shard_map/ppermute | solution.py:345
  59.9 9.6 %collective-permute-start.2 = (bf16[32,2048]{1,0:T(8,128)(2,1)S(1)}, bf16[32,2048]{1,0:T(8,128)(2,1)S(1)}, u32[]{:S(2)}, u32[]{:S(2)}) collective-permute-start(bf16[32,2048]{1,0:T(8,128)(2,1)S(1)} %get-tuple-element.78.rows_ref), channel_id=1, source_target_pairs={{1,2},{2,1},{3,4},{4,3},{5,6},{6,5},{7,8},{8,7},{9,10},{10,9},{11,... | collective-permute-start | bytes 393224 | tf_op jit(solution)/shard_map/ppermute | solution.py:345
  69.8 9.6 %collective-permute-start.4 = (bf16[32,2048]{1,0:T(8,128)(2,1)S(1)}, bf16[32,2048]{1,0:T(8,128)(2,1)S(1)}, u32[]{:S(2)}, u32[]{:S(2)}) collective-permute-start(bf16[32,2048]{1,0:T(8,128)(2,1)S(1)} %get-tuple-element.83.rows_ref), channel_id=1, source_target_pairs={{1,2},{2,1},{3,4},{4,3},{5,6},{6,5},{7,8},{8,7},{9,10},{10,9},{11,... | collective-permute-start | bytes 393224 | tf_op jit(solution)/shard_map/ppermute | solution.py:345
  79.6 9.6 %collective-permute-start.6 = (bf16[32,2048]{1,0:T(8,128)(2,1)S(1)}, bf16[32,2048]{1,0:T(8,128)(2,1)S(1)}, u32[]{:S(2)}, u32[]{:S(2)}) collective-permute-start(bf16[32,2048]{1,0:T(8,128)(2,1)S(1)} %get-tuple-element.88.rows_ref), channel_id=1, source_target_pairs={{1,2},{2,1},{3,4},{4,3},{5,6},{6,5},{7,8},{8,7},{9,10},{10,9},{11,... | collective-permute-start | bytes 393224 | tf_op jit(solution)/shard_map/ppermute | solution.py:345
  89.5 9.6 %collective-permute-start.8 = (bf16[32,2048]{1,0:T(8,128)(2,1)S(1)}, bf16[32,2048]{1,0:T(8,128)(2,1)S(1)}, u32[]{:S(2)}, u32[]{:S(2)}) collective-permute-start(bf16[32,2048]{1,0:T(8,128)(2,1)S(1)} %get-tuple-element.93.rows_ref), channel_id=1, source_target_pairs={{1,2},{2,1},{3,4},{4,3},{5,6},{6,5},{7,8},{8,7},{9,10},{10,9},{11,... | collective-permute-start | bytes 393224 | tf_op jit(solution)/shard_map/ppermute | solution.py:345
  99.3 9.6 %collective-permute-start.10 = (bf16[32,2048]{1,0:T(8,128)(2,1)S(1)}, bf16[32,2048]{1,0:T(8,128)(2,1)S(1)}, u32[]{:S(2)}, u32[]{:S(2)}) collective-permute-start(bf16[32,2048]{1,0:T(8,128)(2,1)S(1)} %get-tuple-element.98.rows_ref), channel_id=1, source_target_pairs={{1,2},{2,1},{3,4},{4,3},{5,6},{6,5},{7,8},{8,7},{9,10},{10,9},{11,... | collective-permute-start | bytes 393224 | tf_op jit(solution)/shard_map/ppermute | solution.py:345
  109.2 9.6 %collective-permute-start.12 = (bf16[32,2048]{1,0:T(8,128)(2,1)S(1)}, bf16[32,2048]{1,0:T(8,128)(2,1)S(1)}, u32[]{:S(2)}, u32[]{:S(2)}) collective-permute-start(bf16[32,2048]{1,0:T(8,128)(2,1)S(1)} %get-tuple-element.103.rows_ref), channel_id=1, source_target_pairs={{1,2},{2,1},{3,4},{4,3},{5,6},{6,5},{7,8},{8,7},{9,10},{10,9},{11,... | collective-permute-start | bytes 393224 | tf_op jit(solution)/shard_map/ppermute | solution.py:345
  119.0 9.6 %collective-permute-start.14 = (bf16[32,2048]{1,0:T(8,128)(2,1)S(1)}, bf16[32,2048]{1,0:T(8,128)(2,1)S(1)}, u32[]{:S(2)}, u32[]{:S(2)}) collective-permute-start(bf16[32,2048]{1,0:T(8,128)(2,1)S(1)} %get-tuple-element.108.rows_ref), channel_id=1, source_target_pairs={{1,2},{2,1},{3,4},{4,3},{5,6},{6,5},{7,8},{8,7},{9,10},{10,9},{11,... | collective-permute-start | bytes 393224 | tf_op jit(solution)/shard_map/ppermute | solution.py:345
  153.8 8.9 %collective-permute-start.16 = (bf16[16,2048]{1,0:T(8,128)(2,1)S(1)}, bf16[16,2048]{1,0:T(8,128)(2,1)S(1)}, u32[]{:S(2)}, u32[]{:S(2)}) collective-permute-start(bf16[16,2048]{1,0:T(8,128)(2,1)S(1)} %get-tuple-element.114.rows_ref), channel_id=1, source_target_pairs={{1,2},{2,1},{3,4},{4,3},{5,6},{6,5},{7,8},{8,7},{9,10},{10,9},{11,... | collective-permute-start | bytes 196616 | tf_op jit(solution)/shard_map/ppermute | solution.py:345
  156.4 6.3 %collective-permute-start.17 = (bf16[16,2048]{1,0:T(8,128)(2,1)S(1)}, bf16[16,2048]{1,0:T(8,128)(2,1)S(1)}, u32[]{:S(2)}, u32[]{:S(2)}) collective-permute-start(bf16[16,2048]{1,0:T(8,128)(2,1)S(1)} %get-tuple-element.114.rows_ref), channel_id=1, source_target_pairs={{0,1},{1,0},{2,3},{3,2},{4,5},{5,4},{6,7},{7,6},{8,9},{9,8},{10,11... | collective-permute-start | bytes 196616 | tf_op jit(solution)/shard_map/ppermute | solution.py:345
  162.9 8.9 %collective-permute-start.18 = (bf16[16,2048]{1,0:T(8,128)(2,1)S(1)}, bf16[16,2048]{1,0:T(8,128)(2,1)S(1)}, u32[]{:S(2)}, u32[]{:S(2)}) collective-permute-start(bf16[16,2048]{1,0:T(8,128)(2,1)S(1)} %get-tuple-element.117.rows_ref), channel_id=1, source_target_pairs={{1,2},{2,1},{3,4},{4,3},{5,6},{6,5},{7,8},{8,7},{9,10},{10,9},{11,... | collective-permute-start | bytes 196616 | tf_op jit(solution)/shard_map/ppermute | solution.py:345
  166.0 5.8 %collective-permute-start.19 = (bf16[16,2048]{1,0:T(8,128)(2,1)S(1)}, bf16[16,2048]{1,0:T(8,128)(2,1)S(1)}, u32[]{:S(2)}, u32[]{:S(2)}) collective-permute-start(bf16[16,2048]{1,0:T(8,128)(2,1)S(1)} %get-tuple-element.117.rows_ref), channel_id=1, source_target_pairs={{0,1},{1,0},{2,3},{3,2},{4,5},{5,4},{6,7},{7,6},{8,9},{9,8},{10,11... | collective-permute-start | bytes 196616 | tf_op jit(solution)/shard_map/ppermute | solution.py:345
  172.0 8.9 %collective-permute-start.20 = (bf16[16,2048]{1,0:T(8,128)(2,1)S(1)}, bf16[16,2048]{1,0:T(8,128)(2,1)S(1)}, u32[]{:S(2)}, u32[]{:S(2)}) collective-permute-start(bf16[16,2048]{1,0:T(8,128)(2,1)S(1)} %get-tuple-element.120.rows_ref), channel_id=1, source_target_pairs={{1,2},{2,1},{3,4},{4,3},{5,6},{6,5},{7,8},{8,7},{9,10},{10,9},{11,... | collective-permute-start | bytes 196616 | tf_op jit(solution)/shard_map/ppermute | solution.py:345
  175.1 5.8 %collective-permute-start.21 = (bf16[16,2048]{1,0:T(8,128)(2,1)S(1)}, bf16[16,2048]{1,0:T(8,128)(2,1)S(1)}, u32[]{:S(2)}, u32[]{:S(2)}) collective-permute-start(bf16[16,2048]{1,0:T(8,128)(2,1)S(1)} %get-tuple-element.120.rows_ref), channel_id=1, source_target_pairs={{0,1},{1,0},{2,3},{3,2},{4,5},{5,4},{6,7},{7,6},{8,9},{9,8},{10,11... | collective-permute-start | bytes 196616 | tf_op jit(solution)/shard_map/ppermute | solution.py:345
  181.1 8.9 %collective-permute-start.22 = (bf16[16,2048]{1,0:T(8,128)(2,1)S(1)}, bf16[16,2048]{1,0:T(8,128)(2,1)S(1)}, u32[]{:S(2)}, u32[]{:S(2)}) collective-permute-start(bf16[16,2048]{1,0:T(8,128)(2,1)S(1)} %get-tuple-element.123.rows_ref), channel_id=1, source_target_pairs={{1,2},{2,1},{3,4},{4,3},{5,6},{6,5},{7,8},{8,7},{9,10},{10,9},{11,... | collective-permute-start | bytes 196616 | tf_op jit(solution)/shard_map/ppermute | solution.py:345
  184.2 5.8 %collective-permute-start.23 = (bf16[16,2048]{1,0:T(8,128)(2,1)S(1)}, bf16[16,2048]{1,0:T(8,128)(2,1)S(1)}, u32[]{:S(2)}, u32[]{:S(2)}) collective-permute-start(bf16[16,2048]{1,0:T(8,128)(2,1)S(1)} %get-tuple-element.123.rows_ref), channel_id=1, source_target_pairs={{0,1},{1,0},{2,3},{3,2},{4,5},{5,4},{6,7},{7,6},{8,9},{9,8},{10,11... | collective-permute-start | bytes 196616 | tf_op jit(solution)/shard_map/ppermute | solution.py:345
  190.2 8.9 %collective-permute-start.24 = (bf16[16,2048]{1,0:T(8,128)(2,1)S(1)}, bf16[16,2048]{1,0:T(8,128)(2,1)S(1)}, u32[]{:S(2)}, u32[]{:S(2)}) collective-permute-start(bf16[16,2048]{1,0:T(8,128)(2,1)S(1)} %get-tuple-element.126.rows_ref), channel_id=1, source_target_pairs={{1,2},{2,1},{3,4},{4,3},{5,6},{6,5},{7,8},{8,7},{9,10},{10,9},{11,... | collective-permute-start | bytes 196616 | tf_op jit(solution)/shard_map/ppermute | solution.py:345
  193.3 5.8 %collective-permute-start.25 = (bf16[16,2048]{1,0:T(8,128)(2,1)S(1)}, bf16[16,2048]{1,0:T(8,128)(2,1)S(1)}, u32[]{:S(2)}, u32[]{:S(2)}) collective-permute-start(bf16[16,2048]{1,0:T(8,128)(2,1)S(1)} %get-tuple-element.126.rows_ref), channel_id=1, source_target_pairs={{0,1},{1,0},{2,3},{3,2},{4,5},{5,4},{6,7},{7,6},{8,9},{9,8},{10,11... | collective-permute-start | bytes 196616 | tf_op jit(solution)/shard_map/ppermute | solution.py:345
  199.3 8.9 %collective-permute-start.26 = (bf16[16,2048]{1,0:T(8,128)(2,1)S(1)}, bf16[16,2048]{1,0:T(8,128)(2,1)S(1)}, u32[]{:S(2)}, u32[]{:S(2)}) collective-permute-start(bf16[16,2048]{1,0:T(8,128)(2,1)S(1)} %get-tuple-element.129.rows_ref), channel_id=1, source_target_pairs={{1,2},{2,1},{3,4},{4,3},{5,6},{6,5},{7,8},{8,7},{9,10},{10,9},{11,... | collective-permute-start | bytes 196616 | tf_op jit(solution)/shard_map/ppermute | solution.py:345
  202.4 5.8 %collective-permute-start.27 = (bf16[16,2048]{1,0:T(8,128)(2,1)S(1)}, bf16[16,2048]{1,0:T(8,128)(2,1)S(1)}, u32[]{:S(2)}, u32[]{:S(2)}) collective-permute-start(bf16[16,2048]{1,0:T(8,128)(2,1)S(1)} %get-tuple-element.129.rows_ref), channel_id=1, source_target_pairs={{0,1},{1,0},{2,3},{3,2},{4,5},{5,4},{6,7},{7,6},{8,9},{9,8},{10,11... | collective-permute-start | bytes 196616 | tf_op jit(solution)/shard_map/ppermute | solution.py:345
  208.4 8.9 %collective-permute-start.28 = (bf16[16,2048]{1,0:T(8,128)(2,1)S(1)}, bf16[16,2048]{1,0:T(8,128)(2,1)S(1)}, u32[]{:S(2)}, u32[]{:S(2)}) collective-permute-start(bf16[16,2048]{1,0:T(8,128)(2,1)S(1)} %get-tuple-element.132.rows_ref), channel_id=1, source_target_pairs={{1,2},{2,1},{3,4},{4,3},{5,6},{6,5},{7,8},{8,7},{9,10},{10,9},{11,... | collective-permute-start | bytes 196616 | tf_op jit(solution)/shard_map/ppermute | solution.py:345
  217.5 8.9 %collective-permute-start.30 = (bf16[16,2048]{1,0:T(8,128)(2,1)S(1)}, bf16[16,2048]{1,0:T(8,128)(2,1)S(1)}, u32[]{:S(2)}, u32[]{:S(2)}) collective-permute-start(bf16[16,2048]{1,0:T(8,128)(2,1)S(1)} %get-tuple-element.135.rows_ref), channel_id=1, source_target_pairs={{1,2},{2,1},{3,4},{4,3},{5,6},{6,5},{7,8},{8,7},{9,10},{10,9},{11,... | collective-permute-start | bytes 196616 | tf_op jit(solution)/shard_map/ppermute | solution.py:345
  227.5 11.4 %all-to-all-start.3 = ((f32[8,8,2048]{2,1,0:T(8,128)}), f32[8,8,2048]{2,1,0:T(8,128)S(1)}, u32[]{:S(2)}, u32[]{:S(2)}) async-start(f32[8,8,2048]{2,1,0:T(8,128)} %stack.3), calls=%async_computation.3 | async-start | bytes 1048576 | tf_op jit(solution)/shard_map/all_to_all | solution.py:350
  (22 other events, 290.4 us)

commit v3 on v2

--- a/solution.py
+++ b/solution.py
@@ -10,7 +10,7 @@
 HALO = 8
 BLOCK = 128
 PAIR = 2 * BLOCK
-CENTRE, EDGE, SLOW, COEF, PACKED = 0, 256, 384, 640, 704
+PIECE = BLOCK + BLOCK // 2
 VMEM = pl.BlockSpec(memory_space=pltpu.VMEM)
 SMEM = pl.BlockSpec(memory_space=pltpu.SMEM)
 F32, BF16 = jnp.float32, jnp.bfloat16
@@ -84,53 +84,38 @@
     return slice(chunk * PAIR, (chunk + 1) * PAIR)
 
 
-def slowness_of(packed_ref, level, chunk):
-    start = SLOW + chunk * 4 * HALO
-    value = packed_ref[level, start : start + 4 * HALO, :].astype(F32)
-    return value[:HALO] + value[HALO : 2 * HALO] + value[2 * HALO : 3 * HALO]
-
-
-def coef_of(packed_ref, level, chunk):
-    start = SLOW + chunk * 4 * HALO + 2 * HALO
-    high = packed_ref[level, start : start + 2 * HALO, :].astype(F32)[HALO:]
-    start = COEF + chunk // 2 * 2 * HALO
-    low = packed_ref[level, start : start + 2 * HALO, :].astype(F32)
-    return high + (low[:HALO] if chunk % 2 == 0 else low[HALO:])
+def centre_of(band_ref, pair):
+    return jnp.concatenate([band_ref[half, pair, 0:BLOCK, :] for half in (0, 1)], axis=0)
+
+
+def edge_of(band_ref, pair, side):
+    cols = slice(side * BLOCK, (side + 1) * BLOCK)
+    return jnp.concatenate([band_ref[half, pair, BLOCK:PIECE, cols] for half in (0, 1)], axis=0)
 
 
 def rounded(value):
     return value.astype(BF16).astype(F32)
 
 
-def pack_kernel(slow_ref, coef_ref, band_ref, out_ref):
-    copies = out_ref.shape[0]
-
-    def write(rows, cols, value):
-        for copy in range(copies):
-            out_ref[copy, rows, cols] = value
-
-    left, right = (slice(0, BLOCK), slice(BLOCK, PAIR))
-    write(slice(0, BLOCK), left, band_ref[0, 1])
-    write(slice(0, BLOCK), right, band_ref[1, 0])
-    write(slice(BLOCK, PAIR), left, band_ref[0, 2])
-    write(slice(BLOCK, PAIR), right, band_ref[1, 1])
-    write(slice(EDGE, EDGE + BLOCK), left, band_ref[0, 0])
-    write(slice(EDGE, EDGE + BLOCK), right, band_ref[1, 2])
-    lows = []
-    for chunk in range(slow_ref.shape[2] // PAIR):
-        slow = slow_ref[0, :, columns(chunk)]
-        coef = coef_ref[0, :, columns(chunk)]
-        high = rounded(slow)
-        middle = rounded(slow - high)
-        coef_high = rounded(coef)
-        lows.append(coef - coef_high)
-        pieces = jnp.concatenate([high, middle, slow - high - middle, coef_high], axis=0)
-        start = SLOW + chunk * 4 * HALO
-        write(slice(start, start + 4 * HALO), slice(0, PAIR), pieces.astype(BF16))
-    for half in range(len(lows) // 2):
-        start = COEF + half * 2 * HALO
-        pieces = jnp.concatenate(lows[2 * half : 2 * half + 2], axis=0)
-        write(slice(start, start + 2 * HALO), slice(0, PAIR), pieces.astype(BF16))
+def band_kernel(half_ref, band_ref, out_ref):
+    half = half_ref[0]
+    rows = pl.ds(pl.multiple_of(half * (BLOCK // 2), BLOCK // 2), BLOCK // 2)
+    centre = jnp.concatenate([band_ref[0, 1 + half], band_ref[1, half]], axis=1)
+    edge = jnp.concatenate([band_ref[0, 0, rows, :], band_ref[1, 2, rows, :]], axis=1)
+    for copy in range(out_ref.shape[0]):
+        out_ref[copy, 0:BLOCK, :] = centre
+        out_ref[copy, BLOCK:PIECE, :] = edge
+
+
+def merge_kernel(half_ref, own_ref, other_ref, out_ref):
+    half = half_ref[0]
+    out_ref[half] = own_ref[...]
+    out_ref[1 - half] = other_ref[...]
+
+
+def copies_kernel(value_ref, out_ref):
+    for copy in range(out_ref.shape[0]):
+        out_ref[copy] = value_ref[...]
 
 
 def phase(fields, cosine, sine):
@@ -143,11 +128,11 @@
     return jnp.concatenate(parts, axis=0)
 
 
-def first_kernel(omega_ref, packed_ref, fields_ref, rows_ref, phased_ref, angle_ref):
+def first_kernel(omega_ref, params_ref, fields_ref, rows_ref, phased_ref, angle_ref):
     omega = omega_ref[0]
-    for chunk in range(packed_ref.shape[0]):
+    for chunk in range(params_ref.shape[3] // PAIR):
         cols = columns(chunk)
-        cosine, sine = cos_sin(omega * slowness_of(packed_ref, 0, chunk))
+        cosine, sine = cos_sin(omega * params_ref[0, 0, :, cols])
         angle_ref[0:HALO, cols] = cosine
         angle_ref[HALO : 2 * HALO, cols] = sine
         phased = phase(fields_ref[:, cols].astype(F32), cosine, sine)
@@ -155,27 +140,27 @@
         rows_ref[:, cols] = phased.astype(BF16)
 
 
-def middle_kernel(level, omega_ref, packed_ref, weights_ref, rows_ref, lateral_ref, *angle_refs):
+def middle_kernel(level, omega_ref, params_ref, band_ref, weights_ref, rows_ref, lateral_ref, *angle_refs):
     omega = omega_ref[0]
-    pairs = packed_ref.shape[0]
+    pairs = band_ref.shape[1]
     height = rows_ref.shape[0]
     for pair in range(pairs):
         cols = columns(pair)
         rows = rows_ref[:, cols]
-        total = dot(rows, packed_ref[pair, CENTRE : CENTRE + PAIR, :])
+        total = dot(rows, centre_of(band_ref, pair))
         spread = dot(weights_ref[...], rows)
         total = total + (spread[:height] + spread[height:])
         zero = jnp.zeros((height, BLOCK), F32)
         left, right = (zero, zero)
         if pair > 0:
             before = rows_ref[:, pair * PAIR - BLOCK : pair * PAIR]
-            left = dot(before, packed_ref[pair, EDGE : EDGE + BLOCK, 0:BLOCK])
+            left = dot(before, edge_of(band_ref, pair, 0))
         if pair < pairs - 1:
             after = rows_ref[:, (pair + 1) * PAIR : (pair + 1) * PAIR + BLOCK]
-            right = dot(after, packed_ref[pair, EDGE : EDGE + BLOCK, BLOCK:PAIR])
+            right = dot(after, edge_of(band_ref, pair, 1))
         lateral_ref[:, cols] = total + jnp.concatenate([left, right], axis=1)
         if angle_refs:
-            cosine, sine = cos_sin(omega * slowness_of(packed_ref, level + 1, pair))
+            cosine, sine = cos_sin(omega * params_ref[level + 1, 0, :, cols])
             angle_refs[0][0:HALO, cols] = cosine
             angle_refs[0][HALO : 2 * HALO, cols] = sine
 
@@ -189,14 +174,14 @@
 
 def step_kernel(level, last, *refs):
     if last:
-        packed, weights, lateral, first, second, phased, state, product = refs
+        params, weights, lateral, first, second, phased, state, product = refs
     else:
-        packed, weights, lateral, first, second, phased, angle = refs[:7]
+        params, weights, lateral, first, second, phased, angle = refs[:7]
         state, product, rows_next, phased_next = refs[7:]
-    for chunk in range(packed.shape[0]):
+    for chunk in range(params.shape[3] // PAIR):
         cols = columns(chunk)
         total = lateral[:, cols] + sides(weights, first, second, cols)
-        coef = coef_of(packed, level, chunk)
+        coef = params[level, 1, :, cols]
         value = phased[:, cols]
         part = [slice(k * HALO, (k + 1) * HALO) for k in range(4)]
         source_re = value[part[0]] - coef * total[part[1]]
@@ -221,8 +206,8 @@
     for member in range(1, count):
         total = total + parts_ref[member]
     image = total / count
-    image_ref[0] = image
-    masked = mask_ref[0].astype(F32) * image
+    image_ref[...] = image
+    masked = mask_ref[...].astype(F32) * image
     for copy in range(count):
         masked_ref[copy] = masked
 
@@ -232,7 +217,7 @@
     total = parts_ref[0]
     for member in range(1, count):
         total = total + parts_ref[member]
-    gradient_ref[0] = total / count
+    gradient_ref[...] = total / count
 
 
 def scaled_rows(adjoint, coef):
@@ -243,41 +228,41 @@
     return jnp.concatenate([masked * state[:HALO], masked * state[HALO:]], axis=0)
 
 
-def adjoint_kernel(level, packed, masked, state, adjoint, scaled):
-    for chunk in range(packed.shape[0]):
+def adjoint_kernel(level, params, masked, state, adjoint, scaled):
+    for chunk in range(params.shape[3] // PAIR):
         cols = columns(chunk)
         value = weighted(masked[level, :, cols], state[:, cols])
         adjoint[:, cols] = value
-        scaled[:, cols] = scaled_rows(value, coef_of(packed, level, chunk))
-
-
-def middle_back_kernel(packed_ref, weights_ref, rows_ref, lateral_ref):
-    pairs = packed_ref.shape[0]
+        scaled[:, cols] = scaled_rows(value, params[level, 1, :, cols])
+
+
+def middle_back_kernel(band_ref, weights_ref, rows_ref, lateral_ref):
+    pairs = band_ref.shape[1]
     height = rows_ref.shape[0]
     for pair in range(pairs):
         cols = columns(pair)
         rows = rows_ref[:, cols]
-        total = dot_t(rows, packed_ref[pair, CENTRE : CENTRE + PAIR, :])
+        total = dot_t(rows, centre_of(band_ref, pair))
         spread = dot(weights_ref[...], rows)
         total = total + (spread[:height] + spread[height:])
         zero = jnp.zeros((height, BLOCK), F32)
         left, right = (zero, zero)
         if pair > 0:
             before = rows_ref[:, pair * PAIR - BLOCK : pair * PAIR]
-            left = dot_t(before, packed_ref[pair - 1, EDGE : EDGE + BLOCK, BLOCK:PAIR])
+            left = dot_t(before, edge_of(band_ref, pair - 1, 1))
         if pair < pairs - 1:
             after = rows_ref[:, (pair + 1) * PAIR : (pair + 1) * PAIR + BLOCK]
-            right = dot_t(after, packed_ref[pair + 1, EDGE : EDGE + BLOCK, 0:BLOCK])
+            right = dot_t(after, edge_of(band_ref, pair + 1, 0))
         lateral_ref[:, cols] = total + jnp.concatenate([left, right], axis=1)
 
 
 def back_kernel(level, last, *refs):
     if last:
-        omega, packed, weights, lateral, first, second, adjoint, phased, term = refs
+        omega, params, weights, lateral, first, second, adjoint, phased, term = refs
     else:
-        omega, packed, weights, lateral, first, second, adjoint, phased = refs[:8]
+        omega, params, weights, lateral, first, second, adjoint, phased = refs[:8]
         angle, masked, state, term, adjoint_next, scaled_next = refs[8:]
-    for chunk in range(packed.shape[0]):
+    for chunk in range(params.shape[3] // PAIR):
         cols = columns(chunk)
         total = lateral[:, cols] + sides(weights, first, second, cols)
         value = adjoint[:, cols]
@@ -294,11 +279,10 @@
             upward = upward.astype(BF16).astype(F32)
             following = weighted(masked[level - 1, :, cols], state[:, cols]) + upward
             adjoint_next[:, cols] = following
-            scaled_next[:, cols] = scaled_rows(following, coef_of(packed, level - 1, chunk))
-
-
-def call(kernel, name, outs, cost, *args, local=True):
-    kind_of = pltpu.VMEM if local else jax.ShapeDtypeStruct
+            scaled_next[:, cols] = scaled_rows(following, params[level - 1, 1, :, cols])
+
+
+def call(kernel, name, outs, cost, *args):
     placed = []
     for arg in args:
         scalar = arg.shape == (1,)
@@ -306,7 +290,7 @@
     return pl.pallas_call(
         kernel,
         name=name,
-        out_shape=[kind_of(shape, kind) for shape, kind in outs],
+        out_shape=[pltpu.VMEM(shape, kind) for shape, kind in outs],
         in_specs=[SMEM if arg.shape == (1,) else VMEM for arg in args],
         out_specs=[VMEM] * len(outs),
         cost_estimate=pl.CostEstimate(flops=cost, bytes_accessed=1 << 20, transcendentals=0),
@@ -329,18 +313,30 @@
     return (depth + upper * (sections // 2)) % sections
 
 
+def home_of(row, size):
+    half = size // 2
+    return row if row < half else half + (row - half - 2) % half
+
+
+def moved(value, inward=True):
+    size = lax.axis_size("lat")
+    route = [(row, home_of(row, size)) for row in range(size)]
+    return lax.ppermute(value, "lat", route if inward else [(b, a) for a, b in route])
+
+
 def swapped(rows):
     sections, size = (lax.axis_size("depth"), lax.axis_size("lat"))
     place = {}
-    for depth in range(sections):
-        for lat in range(size):
-            place[frequency_of(depth, lat, sections, size), lat] = depth * size + lat
+    for row in range(size):
+        lat = home_of(row, size)
+        for depth in range(sections):
+            place[frequency_of(depth, lat, sections, size), row] = depth * size + lat
     received = []
     for offset in (1, 0):
         route = []
         for member in range(sections):
-            for lat in range(offset, size - 1, 2):
-                one, other = (place[member, lat], place[member, lat + 1])
+            for row in range(offset, size - 1, 2):
+                one, other = (place[member, row], place[member, row + 1])
                 route += [(one, other), (other, one)]
         received.append(lax.ppermute(rows, ("depth", "lat"), route))
     return received
@@ -366,12 +362,24 @@
     fields = jnp.concatenate([source, receiver]).reshape(4 * height, width)
 
     wide, half, single = ((4 * height, width), (2 * height, width), (height, width))
-    (packed,) = call(
-        pack_kernel, "pack", [((sections, PACKED, PAIR), BF16)], 1000, slowness, ffd_coef, band
-    )
-    packed = exchanged(packed)
+    own = moved(jnp.stack([slowness[0], ffd_coef[0]]))
+    fields = moved(fields)
+    mask = moved(image_mask[0])
+    half_index = odd.astype(jnp.int32).reshape(1)
+    (pieces,) = call(
+        band_kernel, "band", [((sections, PIECE, PAIR), BF16)], 1000, half_index, band
+    )
+    pieces = exchanged(pieces)
+    (params,) = call(copies_kernel, "copies", [((sections, 2) + single, F32)], 1000, own)
+    pieces, _ = lax.optimization_barrier((pieces, params))
+    params = exchanged(params)
+    route = [(lat, lat + 1 - lat % 2 * 2) for lat in range(size)]
+    other = lax.ppermute(pieces, "lat", route)
+    (band,) = call(
+        merge_kernel, "merge", [((2,) + pieces.shape, BF16)], 1000, half_index, pieces, other
+    )
     rows, phased, angle = call(
-        first_kernel, "first", [(wide, BF16), (wide, F32), (half, F32)], 1000, omega, packed, fields
+        first_kernel, "first", [(wide, BF16), (wide, F32), (half, F32)], 1000, omega, params, fields
     )
     states, products, phases, angles = ([], [], [phased], [angle])
     for level in range(levels):
@@ -384,13 +392,14 @@
             outs,
             1 << 28,
             omega,
-            packed,
+            params,
+            band,
             own_fore,
             rows,
         )
         angles += more
         outs = [(half, F32), (single, F32)] + ([] if last else [(wide, BF16), (wide, F32)])
-        args = [packed, side_fore, lateral, first, second, phased] + more
+        args = [params, side_fore, lateral, first, second, phased] + more
         state, product, *more = call(
             functools.partial(step_kernel, level, last), "step", outs, 1 << 20, *args
         )
@@ -403,12 +412,13 @@
     image, masked = call(
         image_kernel,
         "image",
-        [((1,) + single, F32), ((sections,) + single, F32)],
+        [(single, F32), ((sections,) + single, F32)],
         1000,
         exchanged(stacked(products)),
-        image_mask,
+        mask,
     )
     masked = exchanged(masked)
+    image = moved(image, False)
 
     level = levels - 1
     adjoint, scaled = call(
@@ -416,7 +426,7 @@
         "adjoint",
         [(half, F32), (half, BF16)],
         1000,
-        packed,
+        params,
         masked,
         states[level],
     )
@@ -425,9 +435,9 @@
         last = level == 0
         first, second = swapped(scaled)
         (lateral,) = call(
-            middle_back_kernel, "middle_back", [(half, F32)], 1 << 28, packed, own_back, scaled
+            middle_back_kernel, "middle_back", [(half, F32)], 1 << 28, band, own_back, scaled
         )
-        args = [omega, packed, side_back, lateral, first, second, adjoint, phases[level]]
+        args = [omega, params, side_back, lateral, first, second, adjoint, phases[level]]
         outs = [(single, F32)]
         if not last:
             args += [angles[level], masked, states[level - 1]]
@@ -438,10 +448,9 @@
         if not last:
             adjoint, scaled = more
     (gradient,) = call(
-        gradient_kernel, "gradient", [((1,) + single, F32)], 1000, exchanged(stacked(terms)),
-        local=False,
-    )
-    return (image, gradient)
+        gradient_kernel, "gradient", [(single, F32)], 1000, exchanged(stacked(terms))
+    )
+    return (image[None], moved(gradient, False)[None])
 
 
 def solution(mesh):

time: 241 us -> 221 us (0.917)
  waiting for transfers between devices: 71.4 us -> 40.7 us
  starting transfers between devices: 121 us -> 139 us
  blocking collectives: 24.7 us -> 12.2 us
    all_to_all x2 -> x4, waiting for transfers between devices: 38.3 us -> 8.33 us  [exchanged(): return lax.all_to_all(parts, 'depth', 0, 0)]
    ppermute x0 -> x6, starting transfers between devices: none -> 26.9 us  [the longest x5 25 us: moved(): lax.ppermute(value, 'lat', route if inward else [(b, a) for a, b in route])]
    ppermute x32, starting transfers between devices: 110 us -> 91.3 us  [swapped(): received.append(lax.ppermute(rows, ('depth', 'lat'), route))]
    ppermute x32, waiting for transfers between devices: 33.1 us -> 19.4 us  [swapped(): received.append(lax.ppermute(rows, ('depth', 'lat'), route))]
    ppermute x0 -> x6, waiting for transfers between devices: none -> 13 us  [the longest x5 13 us: moved(): lax.ppermute(value, 'lat', route if inward else [(b, a) for a, b in route])]
    all_to_all x2 -> x1, blocking collectives: 24.7 us -> 12.2 us  [exchanged(): return lax.all_to_all(parts, 'depth', 0, 0)]
    all_to_all x2 -> x4, starting transfers between devices: 10.3 us -> 20.6 us  [exchanged(): return lax.all_to_all(parts, 'depth', 0, 0)]
    unnamed x25 -> x118, local copies, waits for them, and re-layouts: 4.8 us -> 7.18 us
  transfers between devices with their start and end apart: 34 -> 42, of which waited for: 19 -> 24; matrix products, arithmetic and copies ran while one was open for 1% -> 1% of each run, Pallas kernels for 4% -> 5%
where the time goes in v3:
time: 221 us; the launch traced here: 219 us
  starting transfers between devices  139 us (63%)
  waiting for transfers between devices  40.7 us (18%)
  Pallas kernels  16.5 us (7%)
  blocking collectives  12.2 us (6%)
  local copies, waits for them, and re-layouts  8.66 us (4%)
  between operations  2.41 us (1%)
    ppermute x32, starting transfers between devices, swapped(): received.append(lax.ppermute(rows, ('depth', 'lat'), route))  91.3 us
    ppermute x5, starting transfers between devices, moved(): lax.ppermute(value, 'lat', route if inward else [(b, a) for a, b in route])  25 us
    all_to_all x4, starting transfers between devices, exchanged(): return lax.all_to_all(parts, 'depth', 0, 0)  20.6 us
    ppermute x32, waiting for transfers between devices, swapped(): received.append(lax.ppermute(rows, ('depth', 'lat'), route))  19.4 us
    pallas_call x41, Pallas kernels, call(): pl.pallas_call(kernel, name=name, out_shape=[pltpu.VMEM(shape, kind) for...  16.5 us
    ppermute x5, waiting for transfers between devices, moved(): lax.ppermute(value, 'lat', route if inward else [(b, a) for a, b in route])  13 us
    all_to_all x1, blocking collectives, exchanged(): return lax.all_to_all(parts, 'depth', 0, 0)  12.2 us
    all_to_all x4, waiting for transfers between devices, exchanged(): return lax.all_to_all(parts, 'depth', 0, 0)  8.33 us
  transfers between devices with their start and end apart: 42, of which 24 were waited for; matrix products, arithmetic and copies ran while one was open for 1% of the time, Pallas kernels for 5%

profile of v3, /device:TPU:6, one launch (start us, length us, event | category | flops | bytes accessed | tf_op | source)
XLA Modules:
  0.0 219.3 jit_solution(12565794889008269286)
XLA Ops:
  2.5 5.9 %all-to-all-start.1 = ((bf16[8,192,256]{2,1,0:T(8,128)(2,1)}), bf16[8,192,256]{2,1,0:T(8,128)(2,1)S(1)}, u32[]{:S(2)}, u32[]{:S(2)}) async-start(bf16[8,192,256]{2,1,0:T(8,128)(2,1)} %band.1), calls=%async_computation.1 | async-start | bytes 1572864 | tf_op jit(solution)/shard_map/all_to_all | solution.py:346
  8.4 11.4 %collective-permute-start = (f32[2,8,2048]{2,1,0:T(8,128)S(1)}, f32[2,8,2048]{2,1,0:T(8,128)S(1)}, u32[]{:S(2)}, u32[]{:S(2)}) collective-permute-start(f32[2,8,2048]{2,1,0:T(8,128)S(1)} %pad_maximum_fusion), channel_id=1, source_target_pairs={{0,0},{1,1},{2,2},{3,3},{4,4},{5,5},{6,6},{7,7},{8,8},{9,9},{10,10... | collective-permute-start | bytes 393224 | tf_op jit(solution)/shard_map/ppermute | solution.py:324
  23.4 5.8 %all-to-all-start = ((f32[8,2,8,2048]{3,2,1,0:T(8,128)}), f32[8,2,8,2048]{3,2,1,0:T(8,128)S(1)}, u32[]{:S(2)}, u32[]{:S(2)}) async-start(f32[8,2,8,2048]{3,2,1,0:T(8,128)} %copies.1), calls=%async_computation | async-start | bytes 2097152 | tf_op jit(solution)/shard_map/all_to_all | solution.py:346
  32.1 6.2 %collective-permute-start.2 = (bf16[32,2048]{1,0:T(8,128)(2,1)S(1)}, bf16[32,2048]{1,0:T(8,128)(2,1)S(1)}, u32[]{:S(2)}, u32[]{:S(2)}) collective-permute-start(bf16[32,2048]{1,0:T(8,128)(2,1)S(1)} %maximum_bitcast_fusion), channel_id=1, source_target_pairs={{0,0},{1,1},{2,2},{3,3},{4,4},{5,5},{6,6},{7,7},{8,8},{9,9},{10,10... | collective-permute-start | bytes 393224 | tf_op jit(solution)/shard_map/ppermute | solution.py:324
  42.9 7.1 %collective-permute-start.3 = (bf16[32,2048]{1,0:T(8,128)(2,1)S(1)}, bf16[32,2048]{1,0:T(8,128)(2,1)S(1)}, u32[]{:S(2)}, u32[]{:S(2)}) collective-permute-start(bf16[32,2048]{1,0:T(8,128)(2,1)S(1)} %get-tuple-element.75.rows_ref), channel_id=1, source_target_pairs={{1,2},{2,1},{3,4},{4,3},{5,6},{6,5},{7,8},{8,7},{9,10},{10,9},{11,... | collective-permute-start | bytes 393224 | tf_op jit(solution)/shard_map/ppermute | solution.py:341
  62.6 3.3 %collective-permute-start.7 = (bf16[32,2048]{1,0:T(8,128)(2,1)S(1)}, bf16[32,2048]{1,0:T(8,128)(2,1)S(1)}, u32[]{:S(2)}, u32[]{:S(2)}) collective-permute-start(bf16[32,2048]{1,0:T(8,128)(2,1)S(1)} %get-tuple-element.85.rows_ref), channel_id=1, source_target_pairs={{1,2},{2,1},{3,4},{4,3},{5,6},{6,5},{7,8},{8,7},{9,10},{10,9},{11,... | collective-permute-start | bytes 393224 | tf_op jit(solution)/shard_map/ppermute | solution.py:341
  72.3 3.7 %collective-permute-start.9 = (bf16[32,2048]{1,0:T(8,128)(2,1)S(1)}, bf16[32,2048]{1,0:T(8,128)(2,1)S(1)}, u32[]{:S(2)}, u32[]{:S(2)}) collective-permute-start(bf16[32,2048]{1,0:T(8,128)(2,1)S(1)} %get-tuple-element.90.rows_ref), channel_id=1, source_target_pairs={{1,2},{2,1},{3,4},{4,3},{5,6},{6,5},{7,8},{8,7},{9,10},{10,9},{11,... | collective-permute-start | bytes 393224 | tf_op jit(solution)/shard_map/ppermute | solution.py:341
  76.4 3.4 %collective-permute-done.9.refs_3_ = bf16[32,2048]{1,0:T(8,128)(2,1)S(1)} collective-permute-done((bf16[32,2048]{1,0:T(8,128)(2,1)S(1)}, bf16[32,2048]{1,0:T(8,128)(2,1)S(1)}, u32[]{:S(2)}, u32[]{:S(2)}) %collective-permute-start.9) | collective-permute-done | bytes 131104 | tf_op jit(solution)/shard_map/ppermute | solution.py:341
  80.0 3.7 %collective-permute-start.11 = (bf16[32,2048]{1,0:T(8,128)(2,1)S(1)}, bf16[32,2048]{1,0:T(8,128)(2,1)S(1)}, u32[]{:S(2)}, u32[]{:S(2)}) collective-permute-start(bf16[32,2048]{1,0:T(8,128)(2,1)S(1)} %get-tuple-element.95.rows_ref), channel_id=1, source_target_pairs={{1,2},{2,1},{3,4},{4,3},{5,6},{6,5},{7,8},{8,7},{9,10},{10,9},{11,... | collective-permute-start | bytes 393224 | tf_op jit(solution)/shard_map/ppermute | solution.py:341
  87.8 3.7 %collective-permute-start.13 = (bf16[32,2048]{1,0:T(8,128)(2,1)S(1)}, bf16[32,2048]{1,0:T(8,128)(2,1)S(1)}, u32[]{:S(2)}, u32[]{:S(2)}) collective-permute-start(bf16[32,2048]{1,0:T(8,128)(2,1)S(1)} %get-tuple-element.100.rows_ref), channel_id=1, source_target_pairs={{1,2},{2,1},{3,4},{4,3},{5,6},{6,5},{7,8},{8,7},{9,10},{10,9},{11,... | collective-permute-start | bytes 393224 | tf_op jit(solution)/shard_map/ppermute | solution.py:341
  95.6 3.7 %collective-permute-start.15 = (bf16[32,2048]{1,0:T(8,128)(2,1)S(1)}, bf16[32,2048]{1,0:T(8,128)(2,1)S(1)}, u32[]{:S(2)}, u32[]{:S(2)}) collective-permute-start(bf16[32,2048]{1,0:T(8,128)(2,1)S(1)} %get-tuple-element.105.rows_ref), channel_id=1, source_target_pairs={{1,2},{2,1},{3,4},{4,3},{5,6},{6,5},{7,8},{8,7},{9,10},{10,9},{11,... | collective-permute-start | bytes 393224 | tf_op jit(solution)/shard_map/ppermute | solution.py:341
  104.0 3.7 %collective-permute-start.17 = (bf16[32,2048]{1,0:T(8,128)(2,1)S(1)}, bf16[32,2048]{1,0:T(8,128)(2,1)S(1)}, u32[]{:S(2)}, u32[]{:S(2)}) collective-permute-start(bf16[32,2048]{1,0:T(8,128)(2,1)S(1)} %get-tuple-element.110.rows_ref), channel_id=1, source_target_pairs={{1,2},{2,1},{3,4},{4,3},{5,6},{6,5},{7,8},{8,7},{9,10},{10,9},{11,... | collective-permute-start | bytes 393224 | tf_op jit(solution)/shard_map/ppermute | solution.py:341
  113.2 4.7 %all-to-all-start.2 = ((f32[8,8,2048]{2,1,0:T(8,128)}), f32[8,8,2048]{2,1,0:T(8,128)S(1)}, u32[]{:S(2)}, u32[]{:S(2)}) async-start(f32[8,8,2048]{2,1,0:T(8,128)} %stack.6), calls=%async_computation.2 | async-start | bytes 1048576 | tf_op jit(solution)/shard_map/all_to_all | solution.py:346
  117.9 3.5 %collective-permute-start.19 = (s32[8,2048]{1,0:T(8,128)}, s32[8,2048]{1,0:T(8,128)S(1)}, u32[]{:S(2)}, u32[]{:S(2)}) collective-permute-start(s32[8,2048]{1,0:T(8,128)} %bitcast.12), channel_id=1, source_target_pairs={{0,0},{1,1},{2,2},{3,3},{4,4},{5,5},{6,6},{7,7},{8,8},{9,9},{10,10... | collective-permute-start | bytes 196616 | tf_op jit(solution)/shard_map/ppermute | solution.py:324
  126.8 12.2 %all_to_all.25.masked.refs_9_ = f32[8,8,2048]{2,1,0:T(8,128)S(1)} all-to-all(f32[8,8,2048]{2,1,0:T(8,128)S(1)} %get-tuple-element.114), channel_id=1, replica_groups=mesh['depth'=8,'lat'=64] {'depth'}, dimensions={0} | all-to-all | bytes 1048576 | tf_op jit(solution)/shard_map/all_to_all | solution.py:346
  153.3 4.4 %collective-permute-start.25 = (bf16[16,2048]{1,0:T(8,128)(2,1)S(1)}, bf16[16,2048]{1,0:T(8,128)(2,1)S(1)}, u32[]{:S(2)}, u32[]{:S(2)}) collective-permute-start(bf16[16,2048]{1,0:T(8,128)(2,1)S(1)} %get-tuple-element.122.rows_ref), channel_id=1, source_target_pairs={{1,2},{2,1},{3,4},{4,3},{5,6},{6,5},{7,8},{8,7},{9,10},{10,9},{11,... | collective-permute-start | bytes 196616 | tf_op jit(solution)/shard_map/ppermute | solution.py:341
  161.1 3.9 %collective-permute-start.27 = (bf16[16,2048]{1,0:T(8,128)(2,1)S(1)}, bf16[16,2048]{1,0:T(8,128)(2,1)S(1)}, u32[]{:S(2)}, u32[]{:S(2)}) collective-permute-start(bf16[16,2048]{1,0:T(8,128)(2,1)S(1)} %get-tuple-element.125.rows_ref), channel_id=1, source_target_pairs={{1,2},{2,1},{3,4},{4,3},{5,6},{6,5},{7,8},{8,7},{9,10},{10,9},{11,... | collective-permute-start | bytes 196616 | tf_op jit(solution)/shard_map/ppermute | solution.py:341
  168.4 3.8 %collective-permute-start.29 = (bf16[16,2048]{1,0:T(8,128)(2,1)S(1)}, bf16[16,2048]{1,0:T(8,128)(2,1)S(1)}, u32[]{:S(2)}, u32[]{:S(2)}) collective-permute-start(bf16[16,2048]{1,0:T(8,128)(2,1)S(1)} %get-tuple-element.128.rows_ref), channel_id=1, source_target_pairs={{1,2},{2,1},{3,4},{4,3},{5,6},{6,5},{7,8},{8,7},{9,10},{10,9},{11,... | collective-permute-start | bytes 196616 | tf_op jit(solution)/shard_map/ppermute | solution.py:341
  175.7 3.6 %collective-permute-start.31 = (bf16[16,2048]{1,0:T(8,128)(2,1)S(1)}, bf16[16,2048]{1,0:T(8,128)(2,1)S(1)}, u32[]{:S(2)}, u32[]{:S(2)}) collective-permute-start(bf16[16,2048]{1,0:T(8,128)(2,1)S(1)} %get-tuple-element.131.rows_ref), channel_id=1, source_target_pairs={{1,2},{2,1},{3,4},{4,3},{5,6},{6,5},{7,8},{8,7},{9,10},{10,9},{11,... | collective-permute-start | bytes 196616 | tf_op jit(solution)/shard_map/ppermute | solution.py:341
  182.7 3.6 %collective-permute-start.33 = (bf16[16,2048]{1,0:T(8,128)(2,1)S(1)}, bf16[16,2048]{1,0:T(8,128)(2,1)S(1)}, u32[]{:S(2)}, u32[]{:S(2)}) collective-permute-start(bf16[16,2048]{1,0:T(8,128)(2,1)S(1)} %get-tuple-element.134.rows_ref), channel_id=1, source_target_pairs={{1,2},{2,1},{3,4},{4,3},{5,6},{6,5},{7,8},{8,7},{9,10},{10,9},{11,... | collective-permute-start | bytes 196616 | tf_op jit(solution)/shard_map/ppermute | solution.py:341
  189.7 3.6 %collective-permute-start.35 = (bf16[16,2048]{1,0:T(8,128)(2,1)S(1)}, bf16[16,2048]{1,0:T(8,128)(2,1)S(1)}, u32[]{:S(2)}, u32[]{:S(2)}) collective-permute-start(bf16[16,2048]{1,0:T(8,128)(2,1)S(1)} %get-tuple-element.137.rows_ref), channel_id=1, source_target_pairs={{1,2},{2,1},{3,4},{4,3},{5,6},{6,5},{7,8},{8,7},{9,10},{10,9},{11,... | collective-permute-start | bytes 196616 | tf_op jit(solution)/shard_map/ppermute | solution.py:341
  197.5 4.2 %all-to-all-start.4 = ((f32[8,8,2048]{2,1,0:T(8,128)}), f32[8,8,2048]{2,1,0:T(8,128)S(1)}, u32[]{:S(2)}, u32[]{:S(2)}) async-start(f32[8,8,2048]{2,1,0:T(8,128)} %stack.7), calls=%async_computation.4 | async-start | bytes 1048576 | tf_op jit(solution)/shard_map/all_to_all | solution.py:346
  203.7 7.0 %all-to-all-done.4.parts_ref = f32[8,8,2048]{2,1,0:T(8,128)S(1)} async-done(((f32[8,8,2048]{2,1,0:T(8,128)}), f32[8,8,2048]{2,1,0:T(8,128)S(1)}, u32[]{:S(2)}, u32[]{:S(2)}) %all-to-all-start.4) | async-done | bytes 524320 | tf_op jit(solution)/shard_map/all_to_all | solution.py:346
  212.7 5.4 %collective-permute-done.37 = f32[8,2048]{1,0:T(8,128)S(1)} collective-permute-done((f32[8,2048]{1,0:T(8,128)S(1)}, f32[8,2048]{1,0:T(8,128)S(1)}, u32[]{:S(2)}, u32[]{:S(2)}) %collective-permute-start.37) | collective-permute-done | bytes 65568 | tf_op jit(solution)/shard_map/ppermute | solution.py:324
  (226 shorter events, 95.4 us)
Async XLA Ops:
  2.5 20.9 %all-to-all-start.1 = ((bf16[8,192,256]{2,1,0:T(8,128)(2,1)}), bf16[8,192,256]{2,1,0:T(8,128)(2,1)S(1)}, u32[]{:S(2)}, u32[]{:S(2)}) async-start(bf16[8,192,256]{2,1,0:T(8,128)(2,1)} %band.1), calls=%async_computation.1 | async-start | bytes 1572864 | tf_op jit(solution)/shard_map/all_to_all | solution.py:346
  8.4 13.9 %collective-permute-start = (f32[2,8,2048]{2,1,0:T(8,128)S(1)}, f32[2,8,2048]{2,1,0:T(8,128)S(1)}, u32[]{:S(2)}, u32[]{:S(2)}) collective-permute-start(f32[2,8,2048]{2,1,0:T(8,128)S(1)} %pad_maximum_fusion), channel_id=1, source_target_pairs={{0,0},{1,1},{2,2},{3,3},{4,4},{5,5},{6,6},{7,7},{8,8},{9,9},{10,10... | collective-permute-start | bytes 393224 | tf_op jit(solution)/shard_map/ppermute | solution.py:324
  23.4 18.7 %all-to-all-start = ((f32[8,2,8,2048]{3,2,1,0:T(8,128)}), f32[8,2,8,2048]{3,2,1,0:T(8,128)S(1)}, u32[]{:S(2)}, u32[]{:S(2)}) async-start(f32[8,2,8,2048]{3,2,1,0:T(8,128)} %copies.1), calls=%async_computation | async-start | bytes 2097152 | tf_op jit(solution)/shard_map/all_to_all | solution.py:346
  29.3 22.6 %collective-permute-start.1 = (bf16[8,192,256]{2,1,0:T(8,128)(2,1)S(1)}, bf16[8,192,256]{2,1,0:T(8,128)(2,1)S(1)}, u32[]{:S(2)}, u32[]{:S(2)}) collective-permute-start(bf16[8,192,256]{2,1,0:T(8,128)(2,1)S(1)} %all-to-all-done.1.own_ref), channel_id=1, source_target_pairs={{0,1},{1,0},{2,3},{3,2},{4,5},{5,4},{6,7},{7,6},{8,9},{9,8},{10,11... | collective-permute-start | bytes 2359304 | tf_op jit(solution)/shard_map/ppermute | solution.py:377
  32.1 9.6 %collective-permute-start.2 = (bf16[32,2048]{1,0:T(8,128)(2,1)S(1)}, bf16[32,2048]{1,0:T(8,128)(2,1)S(1)}, u32[]{:S(2)}, u32[]{:S(2)}) collective-permute-start(bf16[32,2048]{1,0:T(8,128)(2,1)S(1)} %maximum_bitcast_fusion), channel_id=1, source_target_pairs={{0,0},{1,1},{2,2},{3,3},{4,4},{5,5},{6,6},{7,7},{8,8},{9,9},{10,10... | collective-permute-start | bytes 393224 | tf_op jit(solution)/shard_map/ppermute | solution.py:324
  42.9 11.6 %collective-permute-start.3 = (bf16[32,2048]{1,0:T(8,128)(2,1)S(1)}, bf16[32,2048]{1,0:T(8,128)(2,1)S(1)}, u32[]{:S(2)}, u32[]{:S(2)}) collective-permute-start(bf16[32,2048]{1,0:T(8,128)(2,1)S(1)} %get-tuple-element.75.rows_ref), channel_id=1, source_target_pairs={{1,2},{2,1},{3,4},{4,3},{5,6},{6,5},{7,8},{8,7},{9,10},{10,9},{11,... | collective-permute-start | bytes 393224 | tf_op jit(solution)/shard_map/ppermute | solution.py:341
  54.8 7.5 %collective-permute-start.5 = (bf16[32,2048]{1,0:T(8,128)(2,1)S(1)}, bf16[32,2048]{1,0:T(8,128)(2,1)S(1)}, u32[]{:S(2)}, u32[]{:S(2)}) collective-permute-start(bf16[32,2048]{1,0:T(8,128)(2,1)S(1)} %get-tuple-element.80.rows_ref), channel_id=1, source_target_pairs={{1,2},{2,1},{3,4},{4,3},{5,6},{6,5},{7,8},{8,7},{9,10},{10,9},{11,... | collective-permute-start | bytes 393224 | tf_op jit(solution)/shard_map/ppermute | solution.py:341
  62.6 7.5 %collective-permute-start.7 = (bf16[32,2048]{1,0:T(8,128)(2,1)S(1)}, bf16[32,2048]{1,0:T(8,128)(2,1)S(1)}, u32[]{:S(2)}, u32[]{:S(2)}) collective-permute-start(bf16[32,2048]{1,0:T(8,128)(2,1)S(1)} %get-tuple-element.85.rows_ref), channel_id=1, source_target_pairs={{1,2},{2,1},{3,4},{4,3},{5,6},{6,5},{7,8},{8,7},{9,10},{10,9},{11,... | collective-permute-start | bytes 393224 | tf_op jit(solution)/shard_map/ppermute | solution.py:341
  72.3 7.5 %collective-permute-start.9 = (bf16[32,2048]{1,0:T(8,128)(2,1)S(1)}, bf16[32,2048]{1,0:T(8,128)(2,1)S(1)}, u32[]{:S(2)}, u32[]{:S(2)}) collective-permute-start(bf16[32,2048]{1,0:T(8,128)(2,1)S(1)} %get-tuple-element.90.rows_ref), channel_id=1, source_target_pairs={{1,2},{2,1},{3,4},{4,3},{5,6},{6,5},{7,8},{8,7},{9,10},{10,9},{11,... | collective-permute-start | bytes 393224 | tf_op jit(solution)/shard_map/ppermute | solution.py:341
  80.0 7.5 %collective-permute-start.11 = (bf16[32,2048]{1,0:T(8,128)(2,1)S(1)}, bf16[32,2048]{1,0:T(8,128)(2,1)S(1)}, u32[]{:S(2)}, u32[]{:S(2)}) collective-permute-start(bf16[32,2048]{1,0:T(8,128)(2,1)S(1)} %get-tuple-element.95.rows_ref), channel_id=1, source_target_pairs={{1,2},{2,1},{3,4},{4,3},{5,6},{6,5},{7,8},{8,7},{9,10},{10,9},{11,... | collective-permute-start | bytes 393224 | tf_op jit(solution)/shard_map/ppermute | solution.py:341
  87.8 7.5 %collective-permute-start.13 = (bf16[32,2048]{1,0:T(8,128)(2,1)S(1)}, bf16[32,2048]{1,0:T(8,128)(2,1)S(1)}, u32[]{:S(2)}, u32[]{:S(2)}) collective-permute-start(bf16[32,2048]{1,0:T(8,128)(2,1)S(1)} %get-tuple-element.100.rows_ref), channel_id=1, source_target_pairs={{1,2},{2,1},{3,4},{4,3},{5,6},{6,5},{7,8},{8,7},{9,10},{10,9},{11,... | collective-permute-start | bytes 393224 | tf_op jit(solution)/shard_map/ppermute | solution.py:341
  95.6 7.5 %collective-permute-start.15 = (bf16[32,2048]{1,0:T(8,128)(2,1)S(1)}, bf16[32,2048]{1,0:T(8,128)(2,1)S(1)}, u32[]{:S(2)}, u32[]{:S(2)}) collective-permute-start(bf16[32,2048]{1,0:T(8,128)(2,1)S(1)} %get-tuple-element.105.rows_ref), channel_id=1, source_target_pairs={{1,2},{2,1},{3,4},{4,3},{5,6},{6,5},{7,8},{8,7},{9,10},{10,9},{11,... | collective-permute-start | bytes 393224 | tf_op jit(solution)/shard_map/ppermute | solution.py:341
  104.0 7.5 %collective-permute-start.17 = (bf16[32,2048]{1,0:T(8,128)(2,1)S(1)}, bf16[32,2048]{1,0:T(8,128)(2,1)S(1)}, u32[]{:S(2)}, u32[]{:S(2)}) collective-permute-start(bf16[32,2048]{1,0:T(8,128)(2,1)S(1)} %get-tuple-element.110.rows_ref), channel_id=1, source_target_pairs={{1,2},{2,1},{3,4},{4,3},{5,6},{6,5},{7,8},{8,7},{9,10},{10,9},{11,... | collective-permute-start | bytes 393224 | tf_op jit(solution)/shard_map/ppermute | solution.py:341
  113.2 12.7 %all-to-all-start.2 = ((f32[8,8,2048]{2,1,0:T(8,128)}), f32[8,8,2048]{2,1,0:T(8,128)S(1)}, u32[]{:S(2)}, u32[]{:S(2)}) async-start(f32[8,8,2048]{2,1,0:T(8,128)} %stack.6), calls=%async_computation.2 | async-start | bytes 1048576 | tf_op jit(solution)/shard_map/all_to_all | solution.py:346
  139.1 6.9 %collective-permute-start.21 = (bf16[16,2048]{1,0:T(8,128)(2,1)S(1)}, bf16[16,2048]{1,0:T(8,128)(2,1)S(1)}, u32[]{:S(2)}, u32[]{:S(2)}) collective-permute-start(bf16[16,2048]{1,0:T(8,128)(2,1)S(1)} %get-tuple-element.116.rows_ref), channel_id=1, source_target_pairs={{1,2},{2,1},{3,4},{4,3},{5,6},{6,5},{7,8},{8,7},{9,10},{10,9},{11,... | collective-permute-start | bytes 196616 | tf_op jit(solution)/shard_map/ppermute | solution.py:341
  146.3 6.8 %collective-permute-start.23 = (bf16[16,2048]{1,0:T(8,128)(2,1)S(1)}, bf16[16,2048]{1,0:T(8,128)(2,1)S(1)}, u32[]{:S(2)}, u32[]{:S(2)}) collective-permute-start(bf16[16,2048]{1,0:T(8,128)(2,1)S(1)} %get-tuple-element.119.rows_ref), channel_id=1, source_target_pairs={{1,2},{2,1},{3,4},{4,3},{5,6},{6,5},{7,8},{8,7},{9,10},{10,9},{11,... | collective-permute-start | bytes 196616 | tf_op jit(solution)/shard_map/ppermute | solution.py:341
  153.3 6.9 %collective-permute-start.25 = (bf16[16,2048]{1,0:T(8,128)(2,1)S(1)}, bf16[16,2048]{1,0:T(8,128)(2,1)S(1)}, u32[]{:S(2)}, u32[]{:S(2)}) collective-permute-start(bf16[16,2048]{1,0:T(8,128)(2,1)S(1)} %get-tuple-element.122.rows_ref), channel_id=1, source_target_pairs={{1,2},{2,1},{3,4},{4,3},{5,6},{6,5},{7,8},{8,7},{9,10},{10,9},{11,... | collective-permute-start | bytes 196616 | tf_op jit(solution)/shard_map/ppermute | solution.py:341
  161.1 6.8 %collective-permute-start.27 = (bf16[16,2048]{1,0:T(8,128)(2,1)S(1)}, bf16[16,2048]{1,0:T(8,128)(2,1)S(1)}, u32[]{:S(2)}, u32[]{:S(2)}) collective-permute-start(bf16[16,2048]{1,0:T(8,128)(2,1)S(1)} %get-tuple-element.125.rows_ref), channel_id=1, source_target_pairs={{1,2},{2,1},{3,4},{4,3},{5,6},{6,5},{7,8},{8,7},{9,10},{10,9},{11,... | collective-permute-start | bytes 196616 | tf_op jit(solution)/shard_map/ppermute | solution.py:341
  168.4 6.8 %collective-permute-start.29 = (bf16[16,2048]{1,0:T(8,128)(2,1)S(1)}, bf16[16,2048]{1,0:T(8,128)(2,1)S(1)}, u32[]{:S(2)}, u32[]{:S(2)}) collective-permute-start(bf16[16,2048]{1,0:T(8,128)(2,1)S(1)} %get-tuple-element.128.rows_ref), channel_id=1, source_target_pairs={{1,2},{2,1},{3,4},{4,3},{5,6},{6,5},{7,8},{8,7},{9,10},{10,9},{11,... | collective-permute-start | bytes 196616 | tf_op jit(solution)/shard_map/ppermute | solution.py:341
  175.7 6.8 %collective-permute-start.31 = (bf16[16,2048]{1,0:T(8,128)(2,1)S(1)}, bf16[16,2048]{1,0:T(8,128)(2,1)S(1)}, u32[]{:S(2)}, u32[]{:S(2)}) collective-permute-start(bf16[16,2048]{1,0:T(8,128)(2,1)S(1)} %get-tuple-element.131.rows_ref), channel_id=1, source_target_pairs={{1,2},{2,1},{3,4},{4,3},{5,6},{6,5},{7,8},{8,7},{9,10},{10,9},{11,... | collective-permute-start | bytes 196616 | tf_op jit(solution)/shard_map/ppermute | solution.py:341
  182.7 6.8 %collective-permute-start.33 = (bf16[16,2048]{1,0:T(8,128)(2,1)S(1)}, bf16[16,2048]{1,0:T(8,128)(2,1)S(1)}, u32[]{:S(2)}, u32[]{:S(2)}) collective-permute-start(bf16[16,2048]{1,0:T(8,128)(2,1)S(1)} %get-tuple-element.134.rows_ref), channel_id=1, source_target_pairs={{1,2},{2,1},{3,4},{4,3},{5,6},{6,5},{7,8},{8,7},{9,10},{10,9},{11,... | collective-permute-start | bytes 196616 | tf_op jit(solution)/shard_map/ppermute | solution.py:341
  197.5 13.1 %all-to-all-start.4 = ((f32[8,8,2048]{2,1,0:T(8,128)}), f32[8,8,2048]{2,1,0:T(8,128)S(1)}, u32[]{:S(2)}, u32[]{:S(2)}) async-start(f32[8,8,2048]{2,1,0:T(8,128)} %stack.7), calls=%async_computation.4 | async-start | bytes 1048576 | tf_op jit(solution)/shard_map/all_to_all | solution.py:346
  201.7 10.9 %collective-permute-start.20 = (f32[8,2048]{1,0:T(8,128)S(1)}, f32[8,2048]{1,0:T(8,128)S(1)}, u32[]{:S(2)}, u32[]{:S(2)}) collective-permute-start(f32[8,2048]{1,0:T(8,128)S(1)} %copy-done.50), channel_id=1, source_target_pairs={{0,0},{1,1},{2,2},{3,3},{4,4},{5,5},{6,6},{7,7},{8,8},{9,9},{10,10... | collective-permute-start | bytes 196616 | tf_op jit(solution)/shard_map/ppermute | solution.py:324
  210.7 7.4 %collective-permute-start.37 = (f32[8,2048]{1,0:T(8,128)S(1)}, f32[8,2048]{1,0:T(8,128)S(1)}, u32[]{:S(2)}, u32[]{:S(2)}) collective-permute-start(f32[8,2048]{1,0:T(8,128)S(1)} %gradient.1), channel_id=1, source_target_pairs={{0,0},{1,1},{2,2},{3,3},{4,4},{5,5},{6,6},{7,7},{8,8},{9,9},{10,10... | collective-permute-start | bytes 196616 | tf_op jit(solution)/shard_map/ppermute | solution.py:324
  (76 other events, 561.5 us)

commit v4 on v3

--- a/solution.py
+++ b/solution.py
@@ -93,10 +93,6 @@
     return jnp.concatenate([band_ref[half, pair, BLOCK:PIECE, cols] for half in (0, 1)], axis=0)
 
 
-def rounded(value):
-    return value.astype(BF16).astype(F32)
-
-
 def band_kernel(half_ref, band_ref, out_ref):
     half = half_ref[0]
     rows = pl.ds(pl.multiple_of(half * (BLOCK // 2), BLOCK // 2), BLOCK // 2)
@@ -116,6 +112,14 @@
 def copies_kernel(value_ref, out_ref):
     for copy in range(out_ref.shape[0]):
         out_ref[copy] = value_ref[...]
+
+
+def coef_of(params, level, cols):
+    return jnp.abs(params[level, 1, :, cols])
+
+
+def visible(params, level, cols, image):
+    return jnp.where(params[level, 1, :, cols] > 0.0, image, 0.0)
 
 
 def phase(fields, cosine, sine):
@@ -173,51 +177,65 @@
 
 
 def step_kernel(level, last, *refs):
+    params, weights, lateral, first, second, phased = refs[:6]
     if last:
-        params, weights, lateral, first, second, phased, state, product = refs
+        state, products = refs[-2:]
     else:
-        params, weights, lateral, first, second, phased, angle = refs[:7]
-        state, product, rows_next, phased_next = refs[7:]
-    for chunk in range(params.shape[3] // PAIR):
-        cols = columns(chunk)
-        total = lateral[:, cols] + sides(weights, first, second, cols)
-        coef = params[level, 1, :, cols]
-        value = phased[:, cols]
-        part = [slice(k * HALO, (k + 1) * HALO) for k in range(4)]
-        source_re = value[part[0]] - coef * total[part[1]]
-        source_im = value[part[1]] + coef * total[part[0]]
-        receiver_re = value[part[2]] - coef * total[part[3]]
-        receiver_im = value[part[3]] + coef * total[part[2]]
-        state[0:HALO, cols] = source_re
-        state[HALO : 2 * HALO, cols] = source_im
-        product[:, cols] = source_re * receiver_re + source_im * receiver_im
-        if not last:
-            stepped = jnp.concatenate([source_re, source_im, receiver_re, receiver_im], axis=0)
-            entering = stepped.astype(BF16).astype(F32)
-            cosine, sine = (angle[0:HALO, cols], angle[HALO : 2 * HALO, cols])
-            following = phase(entering, cosine, sine)
-            phased_next[:, cols] = following
-            rows_next[:, cols] = following.astype(BF16)
-
-
-def image_kernel(parts_ref, mask_ref, image_ref, masked_ref):
+        angle = refs[6]
+        state, products, rows_next, phased_next = refs[-4:]
+    halves = products.shape[2] // PAIR
+    for index in range(halves):
+        pieces = []
+        for chunk in (index, index + halves):
+            cols = columns(chunk)
+            total = lateral[:, cols] + sides(weights, first, second, cols)
+            coef = coef_of(params, level, cols)
+            value = phased[:, cols]
+            part = [slice(k * HALO, (k + 1) * HALO) for k in range(4)]
+            source_re = value[part[0]] - coef * total[part[1]]
+            source_im = value[part[1]] + coef * total[part[0]]
+            receiver_re = value[part[2]] - coef * total[part[3]]
+            receiver_im = value[part[3]] + coef * total[part[2]]
+            state[0:HALO, cols] = source_re
+            state[HALO : 2 * HALO, cols] = source_im
+            pieces.append(source_re * receiver_re + source_im * receiver_im)
+            if not last:
+                stepped = jnp.concatenate(
+                    [source_re, source_im, receiver_re, receiver_im], axis=0
+                )
+                entering = stepped.astype(BF16).astype(F32)
+                cosine, sine = (angle[0:HALO, cols], angle[HALO : 2 * HALO, cols])
+                following = phase(entering, cosine, sine)
+                phased_next[:, cols] = following
+                rows_next[:, cols] = following.astype(BF16)
+        products[level, :, columns(index)] = jnp.concatenate(pieces, axis=0).astype(BF16)
+
+
+def mean_of(parts_ref, cols):
     count = parts_ref.shape[0]
-    total = parts_ref[0]
+    total = parts_ref[0, :, cols].astype(F32)
     for member in range(1, count):
-        total = total + parts_ref[member]
-    image = total / count
-    image_ref[...] = image
-    masked = mask_ref[...].astype(F32) * image
-    for copy in range(count):
-        masked_ref[copy] = masked
+        total = total + parts_ref[member, :, cols].astype(F32)
+    return total / count
+
+
+def image_kernel(parts_ref, image_ref, copies_ref):
+    halves = parts_ref.shape[2] // PAIR
+    for index in range(halves):
+        cols = columns(index)
+        image = mean_of(parts_ref, cols)
+        image_ref[:, cols] = image[:HALO]
+        image_ref[:, columns(index + halves)] = image[HALO:]
+        for copy in range(copies_ref.shape[0]):
+            copies_ref[copy, :, cols] = image.astype(BF16)
 
 
 def gradient_kernel(parts_ref, gradient_ref):
-    count = parts_ref.shape[0]
-    total = parts_ref[0]
-    for member in range(1, count):
-        total = total + parts_ref[member]
-    gradient_ref[...] = total / count
+    halves = parts_ref.shape[2] // PAIR
+    for index in range(halves):
+        gradient = mean_of(parts_ref, columns(index))
+        gradient_ref[:, columns(index)] = gradient[:HALO]
+        gradient_ref[:, columns(index + halves)] = gradient[HALO:]
 
 
 def scaled_rows(adjoint, coef):
@@ -228,12 +246,15 @@
     return jnp.concatenate([masked * state[:HALO], masked * state[HALO:]], axis=0)
 
 
-def adjoint_kernel(level, params, masked, state, adjoint, scaled):
-    for chunk in range(params.shape[3] // PAIR):
-        cols = columns(chunk)
-        value = weighted(masked[level, :, cols], state[:, cols])
-        adjoint[:, cols] = value
-        scaled[:, cols] = scaled_rows(value, params[level, 1, :, cols])
+def adjoint_kernel(level, params, images, state, adjoint, scaled):
+    halves = images.shape[2] // PAIR
+    for index in range(halves):
+        image = images[level, :, columns(index)].astype(F32)
+        for chunk, part in ((index, image[:HALO]), (index + halves, image[HALO:])):
+            cols = columns(chunk)
+            value = weighted(visible(params, level, cols, part), state[:, cols])
+            adjoint[:, cols] = value
+            scaled[:, cols] = scaled_rows(value, coef_of(params, level, cols))
 
 
 def middle_back_kernel(band_ref, weights_ref, rows_ref, lateral_ref):
@@ -257,32 +278,43 @@
 
 
 def back_kernel(level, last, *refs):
+    omega, params, weights, lateral, first, second, adjoint, phased = refs[:8]
     if last:
-        omega, params, weights, lateral, first, second, adjoint, phased, term = refs
+        term = refs[-1].at[0]
+        for later, ref in enumerate(refs[8:-1]):
+            refs[-1][later + 1] = ref[...]
     else:
-        omega, params, weights, lateral, first, second, adjoint, phased = refs[:8]
-        angle, masked, state, term, adjoint_next, scaled_next = refs[8:]
-    for chunk in range(params.shape[3] // PAIR):
-        cols = columns(chunk)
-        total = lateral[:, cols] + sides(weights, first, second, cols)
-        value = adjoint[:, cols]
-        back_re = value[:HALO] + total[HALO:]
-        back_im = value[HALO:] - total[:HALO]
-        phase_re = phased[2 * HALO : 3 * HALO, cols]
-        phase_im = phased[3 * HALO : 4 * HALO, cols]
-        term[:, cols] = omega[0] * (back_im * phase_re - back_re * phase_im)
+        angle, images, state, term, adjoint_next, scaled_next = refs[8:]
+    halves = term.shape[1] // PAIR
+    for index in range(halves):
+        pieces = []
         if not last:
-            cosine, sine = (angle[0:HALO, cols], angle[HALO : 2 * HALO, cols])
-            upward = jnp.concatenate(
-                [back_re * cosine + back_im * sine, back_im * cosine - back_re * sine], axis=0
-            )
-            upward = upward.astype(BF16).astype(F32)
-            following = weighted(masked[level - 1, :, cols], state[:, cols]) + upward
-            adjoint_next[:, cols] = following
-            scaled_next[:, cols] = scaled_rows(following, params[level - 1, 1, :, cols])
-
-
-def call(kernel, name, outs, cost, *args):
+            image = images[level - 1, :, columns(index)].astype(F32)
+        for place, chunk in enumerate((index, index + halves)):
+            cols = columns(chunk)
+            total = lateral[:, cols] + sides(weights, first, second, cols)
+            value = adjoint[:, cols]
+            back_re = value[:HALO] + total[HALO:]
+            back_im = value[HALO:] - total[:HALO]
+            phase_re = phased[2 * HALO : 3 * HALO, cols]
+            phase_im = phased[3 * HALO : 4 * HALO, cols]
+            pieces.append(omega[0] * (back_im * phase_re - back_re * phase_im))
+            if not last:
+                cosine, sine = (angle[0:HALO, cols], angle[HALO : 2 * HALO, cols])
+                upward = jnp.concatenate(
+                    [back_re * cosine + back_im * sine, back_im * cosine - back_re * sine],
+                    axis=0,
+                )
+                upward = upward.astype(BF16).astype(F32)
+                part = image[place * HALO : (place + 1) * HALO]
+                masked = visible(params, level - 1, cols, part)
+                following = weighted(masked, state[:, cols]) + upward
+                adjoint_next[:, cols] = following
+                scaled_next[:, cols] = scaled_rows(following, coef_of(params, level - 1, cols))
+        term[:, columns(index)] = jnp.concatenate(pieces, axis=0).astype(BF16)
+
+
+def call(kernel, name, outs, cost, *args, reuse=None):
     placed = []
     for arg in args:
         scalar = arg.shape == (1,)
@@ -293,19 +325,10 @@
         out_shape=[pltpu.VMEM(shape, kind) for shape, kind in outs],
         in_specs=[SMEM if arg.shape == (1,) else VMEM for arg in args],
         out_specs=[VMEM] * len(outs),
+        input_output_aliases=reuse or {},
         cost_estimate=pl.CostEstimate(flops=cost, bytes_accessed=1 << 20, transcendentals=0),
         compiler_params=pltpu.CompilerParams(vmem_limit_bytes=8 << 20),
     )(*placed)
-
-
-def stack_kernel(*refs):
-    for index, ref in enumerate(refs[:-1]):
-        refs[-1][index] = ref[...]
-
-
-def stacked(parts):
-    shape = (len(parts),) + parts[0].shape
-    return call(stack_kernel, "stack", [(shape, F32)], 1000, *parts)[0]
 
 
 def frequency_of(depth, lat, sections, size):
@@ -362,9 +385,9 @@
     fields = jnp.concatenate([source, receiver]).reshape(4 * height, width)
 
     wide, half, single = ((4 * height, width), (2 * height, width), (height, width))
-    own = moved(jnp.stack([slowness[0], ffd_coef[0]]))
+    signed = jnp.where(image_mask[0] > 0, ffd_coef[0], -ffd_coef[0])
+    own = moved(jnp.stack([slowness[0], signed]))
     fields = moved(fields)
-    mask = moved(image_mask[0])
     half_index = odd.astype(jnp.int32).reshape(1)
     (pieces,) = call(
         band_kernel, "band", [((sections, PIECE, PAIR), BF16)], 1000, half_index, band
@@ -381,7 +404,9 @@
     rows, phased, angle = call(
         first_kernel, "first", [(wide, BF16), (wide, F32), (half, F32)], 1000, omega, params, fields
     )
-    states, products, phases, angles = ([], [], [phased], [angle])
+    folded = (sections, 2 * height, width // 2)
+    states, phases, angles = ([], [phased], [angle])
+    products = []
     for level in range(levels):
         last = level == levels - 1
         first, second = swapped(rows)
@@ -398,26 +423,27 @@
             rows,
         )
         angles += more
-        outs = [(half, F32), (single, F32)] + ([] if last else [(wide, BF16), (wide, F32)])
-        args = [params, side_fore, lateral, first, second, phased] + more
-        state, product, *more = call(
-            functools.partial(step_kernel, level, last), "step", outs, 1 << 20, *args
+        outs = [(half, F32), (folded, BF16)]
+        outs += [] if last else [(wide, BF16), (wide, F32)]
+        args = [params, side_fore, lateral, first, second, phased] + more + products
+        state, products, *more = call(
+            functools.partial(step_kernel, level, last),
+            "step",
+            outs,
+            1 << 20,
+            *args,
+            reuse={len(args) - 1: 1} if products else None,
         )
+        products = [products]
         states.append(state)
-        products.append(product)
         if not last:
             rows, phased = more
             phases.append(phased)
 
-    image, masked = call(
-        image_kernel,
-        "image",
-        [(single, F32), ((sections,) + single, F32)],
-        1000,
-        exchanged(stacked(products)),
-        mask,
-    )
-    masked = exchanged(masked)
+    image, images = call(
+        image_kernel, "image", [(single, F32), (folded, BF16)], 1000, exchanged(products[0])
+    )
+    images = exchanged(images)
     image = moved(image, False)
 
     level = levels - 1
@@ -427,10 +453,10 @@
         [(half, F32), (half, BF16)],
         1000,
         params,
-        masked,
+        images,
         states[level],
     )
-    terms = [None] * levels
+    terms = []
     for level in reversed(range(levels)):
         last = level == 0
         first, second = swapped(scaled)
@@ -438,17 +464,24 @@
             middle_back_kernel, "middle_back", [(half, F32)], 1 << 28, band, own_back, scaled
         )
         args = [omega, params, side_back, lateral, first, second, adjoint, phases[level]]
-        outs = [(single, F32)]
-        if not last:
-            args += [angles[level], masked, states[level - 1]]
-            outs += [(half, F32), (half, BF16)]
-        terms[level], *more = call(
-            functools.partial(back_kernel, level, last), "back", outs, 1 << 20, *args
+        if last:
+            args += terms
+            outs = [(folded, BF16)]
+        else:
+            args += [angles[level], images, states[level - 1]]
+            outs = [(folded[1:], BF16), (half, F32), (half, BF16)]
+        term, *more = call(
+            functools.partial(back_kernel, level, last),
+            "back",
+            outs,
+            1 << 20,
+            *args,
         )
+        terms = [term] + terms
         if not last:
             adjoint, scaled = more
     (gradient,) = call(
-        gradient_kernel, "gradient", [(single, F32)], 1000, exchanged(stacked(terms))
+        gradient_kernel, "gradient", [(single, F32)], 1000, exchanged(terms[0])
     )
     return (image[None], moved(gradient, False)[None])
 

time: 221 us -> 209 us (0.946)
  waiting for transfers between devices: 40.7 us -> 28.7 us
  blocking collectives: 12.2 us -> 20.1 us
  local copies, waits for them, and re-layouts: 8.66 us -> 4.29 us
  starting transfers between devices: 139 us -> 136 us
    all_to_all x1 -> x2, blocking collectives: 12.2 us -> 20.1 us  [exchanged(): return lax.all_to_all(parts, 'depth', 0, 0)]
    ppermute x32, starting transfers between devices: 91.3 us -> 96.8 us  [swapped(): received.append(lax.ppermute(rows, ('depth', 'lat'), route))]
    ppermute x32, waiting for transfers between devices: 19.4 us -> 14.1 us  [swapped(): received.append(lax.ppermute(rows, ('depth', 'lat'), route))]
    all_to_all x4 -> x3, starting transfers between devices: 20.6 us -> 16 us  [exchanged(): return lax.all_to_all(parts, 'depth', 0, 0)]
    unnamed x118 -> x24, local copies, waits for them, and re-layouts: 7.18 us -> 2.81 us
    all_to_all x4 -> x3, waiting for transfers between devices: 8.33 us -> 4.63 us  [exchanged(): return lax.all_to_all(parts, 'depth', 0, 0)]
    ppermute x5 -> x4, starting transfers between devices: 25 us -> 21.5 us  [moved(): lax.ppermute(value, 'lat', route if inward else [(b, a) for a, b in route])]
    ppermute x5 -> x4, waiting for transfers between devices: 13 us -> 10 us  [moved(): lax.ppermute(value, 'lat', route if inward else [(b, a) for a, b in route])]
  transfers between devices with their start and end apart: 42 -> 40, of which waited for: 24 -> 27; matrix products, arithmetic and copies ran while one was open for 1% -> 1% of each run, Pallas kernels for 5% -> 5%
where the time goes in v4:
time: 209 us; the launch traced here: 207 us
  starting transfers between devices  136 us (65%)
  waiting for transfers between devices  28.7 us (14%)
  blocking collectives  20.1 us (10%)
  Pallas kernels  15.7 us (8%)
  local copies, waits for them, and re-layouts  4.29 us (2%)
    ppermute x32, starting transfers between devices, swapped(): received.append(lax.ppermute(rows, ('depth', 'lat'), route))  96.8 us
    ppermute x4, starting transfers between devices, moved(): lax.ppermute(value, 'lat', route if inward else [(b, a) for a, b in route])  21.5 us
    all_to_all x2, blocking collectives, exchanged(): return lax.all_to_all(parts, 'depth', 0, 0)  20.1 us
    all_to_all x3, starting transfers between devices, exchanged(): return lax.all_to_all(parts, 'depth', 0, 0)  16 us
    pallas_call x39, Pallas kernels, call(): pl.pallas_call(kernel, name=name, out_shape=[pltpu.VMEM(shape, kind) for...  15.7 us
    ppermute x32, waiting for transfers between devices, swapped(): received.append(lax.ppermute(rows, ('depth', 'lat'), route))  14.1 us
    ppermute x4, waiting for transfers between devices, moved(): lax.ppermute(value, 'lat', route if inward else [(b, a) for a, b in route])  10 us
    all_to_all x3, waiting for transfers between devices, exchanged(): return lax.all_to_all(parts, 'depth', 0, 0)  4.63 us
  transfers between devices with their start and end apart: 40, of which 27 were waited for; matrix products, arithmetic and copies ran while one was open for 1% of the time, Pallas kernels for 5%

profile of v4, /device:TPU:6, one launch (start us, length us, event | category | flops | bytes accessed | tf_op | source)
XLA Modules:
  0.0 206.9 jit_solution(7063598791983962157)
XLA Ops:
  2.5 5.9 %all-to-all-start.1 = ((bf16[8,192,256]{2,1,0:T(8,128)(2,1)}), bf16[8,192,256]{2,1,0:T(8,128)(2,1)S(1)}, u32[]{:S(2)}, u32[]{:S(2)}) async-start(bf16[8,192,256]{2,1,0:T(8,128)(2,1)} %band.1), calls=%async_computation.1 | async-start | bytes 1572864 | tf_op jit(solution)/shard_map/all_to_all | solution.py:369
  8.5 11.4 %collective-permute-start = (f32[2,8,2048]{2,1,0:T(8,128)S(1)}, f32[2,8,2048]{2,1,0:T(8,128)S(1)}, u32[]{:S(2)}, u32[]{:S(2)}) collective-permute-start(f32[2,8,2048]{2,1,0:T(8,128)S(1)} %pad_maximum_fusion), channel_id=1, source_target_pairs={{0,0},{1,1},{2,2},{3,3},{4,4},{5,5},{6,6},{7,7},{8,8},{9,9},{10,10... | collective-permute-start | bytes 393224 | tf_op jit(solution)/shard_map/ppermute | solution.py:347
  23.5 5.8 %all-to-all-start = ((f32[8,2,8,2048]{3,2,1,0:T(8,128)}), f32[8,2,8,2048]{3,2,1,0:T(8,128)S(1)}, u32[]{:S(2)}, u32[]{:S(2)}) async-start(f32[8,2,8,2048]{3,2,1,0:T(8,128)} %copies.1), calls=%async_computation | async-start | bytes 2097152 | tf_op jit(solution)/shard_map/all_to_all | solution.py:369
  32.2 6.1 %collective-permute-start.2 = (bf16[32,2048]{1,0:T(8,128)(2,1)S(1)}, bf16[32,2048]{1,0:T(8,128)(2,1)S(1)}, u32[]{:S(2)}, u32[]{:S(2)}) collective-permute-start(bf16[32,2048]{1,0:T(8,128)(2,1)S(1)} %maximum_bitcast_fusion), channel_id=1, source_target_pairs={{0,0},{1,1},{2,2},{3,3},{4,4},{5,5},{6,6},{7,7},{8,8},{9,9},{10,10... | collective-permute-start | bytes 393224 | tf_op jit(solution)/shard_map/ppermute | solution.py:347
  42.9 7.0 %collective-permute-start.3 = (bf16[32,2048]{1,0:T(8,128)(2,1)S(1)}, bf16[32,2048]{1,0:T(8,128)(2,1)S(1)}, u32[]{:S(2)}, u32[]{:S(2)}) collective-permute-start(bf16[32,2048]{1,0:T(8,128)(2,1)S(1)} %get-tuple-element.75.rows_ref), channel_id=1, source_target_pairs={{1,2},{2,1},{3,4},{4,3},{5,6},{6,5},{7,8},{8,7},{9,10},{10,9},{11,... | collective-permute-start | bytes 393224 | tf_op jit(solution)/shard_map/ppermute | solution.py:364
  53.4 4.5 %collective-permute-start.5 = (bf16[32,2048]{1,0:T(8,128)(2,1)S(1)}, bf16[32,2048]{1,0:T(8,128)(2,1)S(1)}, u32[]{:S(2)}, u32[]{:S(2)}) collective-permute-start(bf16[32,2048]{1,0:T(8,128)(2,1)S(1)} %get-tuple-element.79.rows_ref), channel_id=1, source_target_pairs={{1,2},{2,1},{3,4},{4,3},{5,6},{6,5},{7,8},{8,7},{9,10},{10,9},{11,... | collective-permute-start | bytes 393224 | tf_op jit(solution)/shard_map/ppermute | solution.py:364
  61.5 4.4 %collective-permute-start.7 = (bf16[32,2048]{1,0:T(8,128)(2,1)S(1)}, bf16[32,2048]{1,0:T(8,128)(2,1)S(1)}, u32[]{:S(2)}, u32[]{:S(2)}) collective-permute-start(bf16[32,2048]{1,0:T(8,128)(2,1)S(1)} %get-tuple-element.84.rows_ref), channel_id=1, source_target_pairs={{1,2},{2,1},{3,4},{4,3},{5,6},{6,5},{7,8},{8,7},{9,10},{10,9},{11,... | collective-permute-start | bytes 393224 | tf_op jit(solution)/shard_map/ppermute | solution.py:364
  71.4 4.5 %collective-permute-start.9 = (bf16[32,2048]{1,0:T(8,128)(2,1)S(1)}, bf16[32,2048]{1,0:T(8,128)(2,1)S(1)}, u32[]{:S(2)}, u32[]{:S(2)}) collective-permute-start(bf16[32,2048]{1,0:T(8,128)(2,1)S(1)} %get-tuple-element.89.rows_ref), channel_id=1, source_target_pairs={{1,2},{2,1},{3,4},{4,3},{5,6},{6,5},{7,8},{8,7},{9,10},{10,9},{11,... | collective-permute-start | bytes 393224 | tf_op jit(solution)/shard_map/ppermute | solution.py:364
  79.1 4.5 %collective-permute-start.11 = (bf16[32,2048]{1,0:T(8,128)(2,1)S(1)}, bf16[32,2048]{1,0:T(8,128)(2,1)S(1)}, u32[]{:S(2)}, u32[]{:S(2)}) collective-permute-start(bf16[32,2048]{1,0:T(8,128)(2,1)S(1)} %get-tuple-element.94.rows_ref), channel_id=1, source_target_pairs={{1,2},{2,1},{3,4},{4,3},{5,6},{6,5},{7,8},{8,7},{9,10},{10,9},{11,... | collective-permute-start | bytes 393224 | tf_op jit(solution)/shard_map/ppermute | solution.py:364
  87.1 4.3 %collective-permute-start.13 = (bf16[32,2048]{1,0:T(8,128)(2,1)S(1)}, bf16[32,2048]{1,0:T(8,128)(2,1)S(1)}, u32[]{:S(2)}, u32[]{:S(2)}) collective-permute-start(bf16[32,2048]{1,0:T(8,128)(2,1)S(1)} %get-tuple-element.99.rows_ref), channel_id=1, source_target_pairs={{1,2},{2,1},{3,4},{4,3},{5,6},{6,5},{7,8},{8,7},{9,10},{10,9},{11,... | collective-permute-start | bytes 393224 | tf_op jit(solution)/shard_map/ppermute | solution.py:364
  94.9 4.3 %collective-permute-start.15 = (bf16[32,2048]{1,0:T(8,128)(2,1)S(1)}, bf16[32,2048]{1,0:T(8,128)(2,1)S(1)}, u32[]{:S(2)}, u32[]{:S(2)}) collective-permute-start(bf16[32,2048]{1,0:T(8,128)(2,1)S(1)} %get-tuple-element.104.rows_ref), channel_id=1, source_target_pairs={{1,2},{2,1},{3,4},{4,3},{5,6},{6,5},{7,8},{8,7},{9,10},{10,9},{11,... | collective-permute-start | bytes 393224 | tf_op jit(solution)/shard_map/ppermute | solution.py:364
  102.6 4.3 %collective-permute-start.17 = (bf16[32,2048]{1,0:T(8,128)(2,1)S(1)}, bf16[32,2048]{1,0:T(8,128)(2,1)S(1)}, u32[]{:S(2)}, u32[]{:S(2)}) collective-permute-start(bf16[32,2048]{1,0:T(8,128)(2,1)S(1)} %get-tuple-element.109.rows_ref), channel_id=1, source_target_pairs={{1,2},{2,1},{3,4},{4,3},{5,6},{6,5},{7,8},{8,7},{9,10},{10,9},{11,... | collective-permute-start | bytes 393224 | tf_op jit(solution)/shard_map/ppermute | solution.py:364
  110.4 10.2 %all_to_all.25.parts_ref = bf16[8,16,1024]{2,1,0:T(8,128)(2,1)S(1)} all-to-all(bf16[8,16,1024]{2,1,0:T(8,128)(2,1)S(1)} %get-tuple-element.112), channel_id=1, replica_groups=mesh['depth'=8,'lat'=64] {'depth'}, dimensions={0} | all-to-all | bytes 524288 | tf_op jit(solution)/shard_map/all_to_all | solution.py:369
  120.7 9.8 %all_to_all.26.images.refs_9_ = bf16[8,16,1024]{2,1,0:T(8,128)(2,1)S(1)} all-to-all(bf16[8,16,1024]{2,1,0:T(8,128)(2,1)S(1)} %get-tuple-element.114), channel_id=1, replica_groups=mesh['depth'=8,'lat'=64] {'depth'}, dimensions={0} | all-to-all | bytes 524288 | tf_op jit(solution)/shard_map/all_to_all | solution.py:369
  137.5 3.1 %collective-permute-start.22 = (bf16[16,2048]{1,0:T(8,128)(2,1)S(1)}, bf16[16,2048]{1,0:T(8,128)(2,1)S(1)}, u32[]{:S(2)}, u32[]{:S(2)}) collective-permute-start(bf16[16,2048]{1,0:T(8,128)(2,1)S(1)} %get-tuple-element.119.rows_ref), channel_id=1, source_target_pairs={{1,2},{2,1},{3,4},{4,3},{5,6},{6,5},{7,8},{8,7},{9,10},{10,9},{11,... | collective-permute-start | bytes 196616 | tf_op jit(solution)/shard_map/ppermute | solution.py:364
  144.5 3.8 %collective-permute-start.24 = (bf16[16,2048]{1,0:T(8,128)(2,1)S(1)}, bf16[16,2048]{1,0:T(8,128)(2,1)S(1)}, u32[]{:S(2)}, u32[]{:S(2)}) collective-permute-start(bf16[16,2048]{1,0:T(8,128)(2,1)S(1)} %get-tuple-element.122.rows_ref), channel_id=1, source_target_pairs={{1,2},{2,1},{3,4},{4,3},{5,6},{6,5},{7,8},{8,7},{9,10},{10,9},{11,... | collective-permute-start | bytes 196616 | tf_op jit(solution)/shard_map/ppermute | solution.py:364
  151.7 3.9 %collective-permute-start.26 = (bf16[16,2048]{1,0:T(8,128)(2,1)S(1)}, bf16[16,2048]{1,0:T(8,128)(2,1)S(1)}, u32[]{:S(2)}, u32[]{:S(2)}) collective-permute-start(bf16[16,2048]{1,0:T(8,128)(2,1)S(1)} %get-tuple-element.125.rows_ref), channel_id=1, source_target_pairs={{1,2},{2,1},{3,4},{4,3},{5,6},{6,5},{7,8},{8,7},{9,10},{10,9},{11,... | collective-permute-start | bytes 196616 | tf_op jit(solution)/shard_map/ppermute | solution.py:364
  159.0 3.8 %collective-permute-start.28 = (bf16[16,2048]{1,0:T(8,128)(2,1)S(1)}, bf16[16,2048]{1,0:T(8,128)(2,1)S(1)}, u32[]{:S(2)}, u32[]{:S(2)}) collective-permute-start(bf16[16,2048]{1,0:T(8,128)(2,1)S(1)} %get-tuple-element.128.rows_ref), channel_id=1, source_target_pairs={{1,2},{2,1},{3,4},{4,3},{5,6},{6,5},{7,8},{8,7},{9,10},{10,9},{11,... | collective-permute-start | bytes 196616 | tf_op jit(solution)/shard_map/ppermute | solution.py:364
  166.2 3.6 %collective-permute-start.30 = (bf16[16,2048]{1,0:T(8,128)(2,1)S(1)}, bf16[16,2048]{1,0:T(8,128)(2,1)S(1)}, u32[]{:S(2)}, u32[]{:S(2)}) collective-permute-start(bf16[16,2048]{1,0:T(8,128)(2,1)S(1)} %get-tuple-element.131.rows_ref), channel_id=1, source_target_pairs={{1,2},{2,1},{3,4},{4,3},{5,6},{6,5},{7,8},{8,7},{9,10},{10,9},{11,... | collective-permute-start | bytes 196616 | tf_op jit(solution)/shard_map/ppermute | solution.py:364
  173.2 3.6 %collective-permute-start.32 = (bf16[16,2048]{1,0:T(8,128)(2,1)S(1)}, bf16[16,2048]{1,0:T(8,128)(2,1)S(1)}, u32[]{:S(2)}, u32[]{:S(2)}) collective-permute-start(bf16[16,2048]{1,0:T(8,128)(2,1)S(1)} %get-tuple-element.134.rows_ref), channel_id=1, source_target_pairs={{1,2},{2,1},{3,4},{4,3},{5,6},{6,5},{7,8},{8,7},{9,10},{10,9},{11,... | collective-permute-start | bytes 196616 | tf_op jit(solution)/shard_map/ppermute | solution.py:364
  180.2 3.6 %collective-permute-start.34 = (bf16[16,2048]{1,0:T(8,128)(2,1)S(1)}, bf16[16,2048]{1,0:T(8,128)(2,1)S(1)}, u32[]{:S(2)}, u32[]{:S(2)}) collective-permute-start(bf16[16,2048]{1,0:T(8,128)(2,1)S(1)} %get-tuple-element.137.rows_ref), channel_id=1, source_target_pairs={{1,2},{2,1},{3,4},{4,3},{5,6},{6,5},{7,8},{8,7},{9,10},{10,9},{11,... | collective-permute-start | bytes 196616 | tf_op jit(solution)/shard_map/ppermute | solution.py:364
  187.9 4.2 %all-to-all-start.4 = ((bf16[8,16,1024]{2,1,0:T(8,128)(2,1)}), bf16[8,16,1024]{2,1,0:T(8,128)(2,1)S(1)}, u32[]{:S(2)}, u32[]{:S(2)}) async-start(bf16[8,16,1024]{2,1,0:T(8,128)(2,1)} %back.15), calls=%async_computation.4 | async-start | bytes 524288 | tf_op jit(solution)/shard_map/all_to_all | solution.py:369
  194.0 4.2 %all-to-all-done.4.parts_ref = bf16[8,16,1024]{2,1,0:T(8,128)(2,1)S(1)} async-done(((bf16[8,16,1024]{2,1,0:T(8,128)(2,1)}), bf16[8,16,1024]{2,1,0:T(8,128)(2,1)S(1)}, u32[]{:S(2)}, u32[]{:S(2)}) %all-to-all-start.4) | async-done | bytes 262176 | tf_op jit(solution)/shard_map/all_to_all | solution.py:369
  200.3 5.4 %collective-permute-done.36 = f32[8,2048]{1,0:T(8,128)S(1)} collective-permute-done((f32[8,2048]{1,0:T(8,128)S(1)}, f32[8,2048]{1,0:T(8,128)S(1)}, u32[]{:S(2)}, u32[]{:S(2)}) %collective-permute-start.36) | collective-permute-done | bytes 65568 | tf_op jit(solution)/shard_map/ppermute | solution.py:347
  (128 shorter events, 78.5 us)
Async XLA Ops:
  2.5 21.0 %all-to-all-start.1 = ((bf16[8,192,256]{2,1,0:T(8,128)(2,1)}), bf16[8,192,256]{2,1,0:T(8,128)(2,1)S(1)}, u32[]{:S(2)}, u32[]{:S(2)}) async-start(bf16[8,192,256]{2,1,0:T(8,128)(2,1)} %band.1), calls=%async_computation.1 | async-start | bytes 1572864 | tf_op jit(solution)/shard_map/all_to_all | solution.py:369
  8.5 13.9 %collective-permute-start = (f32[2,8,2048]{2,1,0:T(8,128)S(1)}, f32[2,8,2048]{2,1,0:T(8,128)S(1)}, u32[]{:S(2)}, u32[]{:S(2)}) collective-permute-start(f32[2,8,2048]{2,1,0:T(8,128)S(1)} %pad_maximum_fusion), channel_id=1, source_target_pairs={{0,0},{1,1},{2,2},{3,3},{4,4},{5,5},{6,6},{7,7},{8,8},{9,9},{10,10... | collective-permute-start | bytes 393224 | tf_op jit(solution)/shard_map/ppermute | solution.py:347
  23.5 18.7 %all-to-all-start = ((f32[8,2,8,2048]{3,2,1,0:T(8,128)}), f32[8,2,8,2048]{3,2,1,0:T(8,128)S(1)}, u32[]{:S(2)}, u32[]{:S(2)}) async-start(f32[8,2,8,2048]{3,2,1,0:T(8,128)} %copies.1), calls=%async_computation | async-start | bytes 2097152 | tf_op jit(solution)/shard_map/all_to_all | solution.py:369
  29.3 22.6 %collective-permute-start.1 = (bf16[8,192,256]{2,1,0:T(8,128)(2,1)S(1)}, bf16[8,192,256]{2,1,0:T(8,128)(2,1)S(1)}, u32[]{:S(2)}, u32[]{:S(2)}) collective-permute-start(bf16[8,192,256]{2,1,0:T(8,128)(2,1)S(1)} %all-to-all-done.1.own_ref), channel_id=1, source_target_pairs={{0,1},{1,0},{2,3},{3,2},{4,5},{5,4},{6,7},{7,6},{8,9},{9,8},{10,11... | collective-permute-start | bytes 2359304 | tf_op jit(solution)/shard_map/ppermute | solution.py:400
  32.2 9.5 %collective-permute-start.2 = (bf16[32,2048]{1,0:T(8,128)(2,1)S(1)}, bf16[32,2048]{1,0:T(8,128)(2,1)S(1)}, u32[]{:S(2)}, u32[]{:S(2)}) collective-permute-start(bf16[32,2048]{1,0:T(8,128)(2,1)S(1)} %maximum_bitcast_fusion), channel_id=1, source_target_pairs={{0,0},{1,1},{2,2},{3,3},{4,4},{5,5},{6,6},{7,7},{8,8},{9,9},{10,10... | collective-permute-start | bytes 393224 | tf_op jit(solution)/shard_map/ppermute | solution.py:347
  42.9 10.2 %collective-permute-start.3 = (bf16[32,2048]{1,0:T(8,128)(2,1)S(1)}, bf16[32,2048]{1,0:T(8,128)(2,1)S(1)}, u32[]{:S(2)}, u32[]{:S(2)}) collective-permute-start(bf16[32,2048]{1,0:T(8,128)(2,1)S(1)} %get-tuple-element.75.rows_ref), channel_id=1, source_target_pairs={{1,2},{2,1},{3,4},{4,3},{5,6},{6,5},{7,8},{8,7},{9,10},{10,9},{11,... | collective-permute-start | bytes 393224 | tf_op jit(solution)/shard_map/ppermute | solution.py:364
  53.4 7.5 %collective-permute-start.5 = (bf16[32,2048]{1,0:T(8,128)(2,1)S(1)}, bf16[32,2048]{1,0:T(8,128)(2,1)S(1)}, u32[]{:S(2)}, u32[]{:S(2)}) collective-permute-start(bf16[32,2048]{1,0:T(8,128)(2,1)S(1)} %get-tuple-element.79.rows_ref), channel_id=1, source_target_pairs={{1,2},{2,1},{3,4},{4,3},{5,6},{6,5},{7,8},{8,7},{9,10},{10,9},{11,... | collective-permute-start | bytes 393224 | tf_op jit(solution)/shard_map/ppermute | solution.py:364
  61.5 7.5 %collective-permute-start.7 = (bf16[32,2048]{1,0:T(8,128)(2,1)S(1)}, bf16[32,2048]{1,0:T(8,128)(2,1)S(1)}, u32[]{:S(2)}, u32[]{:S(2)}) collective-permute-start(bf16[32,2048]{1,0:T(8,128)(2,1)S(1)} %get-tuple-element.84.rows_ref), channel_id=1, source_target_pairs={{1,2},{2,1},{3,4},{4,3},{5,6},{6,5},{7,8},{8,7},{9,10},{10,9},{11,... | collective-permute-start | bytes 393224 | tf_op jit(solution)/shard_map/ppermute | solution.py:364
  69.3 7.0 %collective-permute-start.10 = (bf16[32,2048]{1,0:T(8,128)(2,1)S(1)}, bf16[32,2048]{1,0:T(8,128)(2,1)S(1)}, u32[]{:S(2)}, u32[]{:S(2)}) collective-permute-start(bf16[32,2048]{1,0:T(8,128)(2,1)S(1)} %get-tuple-element.89.rows_ref), channel_id=1, source_target_pairs={{0,1},{1,0},{2,3},{3,2},{4,5},{5,4},{6,7},{7,6},{8,9},{9,8},{10,11... | collective-permute-start | bytes 393224 | tf_op jit(solution)/shard_map/ppermute | solution.py:364
  71.4 7.5 %collective-permute-start.9 = (bf16[32,2048]{1,0:T(8,128)(2,1)S(1)}, bf16[32,2048]{1,0:T(8,128)(2,1)S(1)}, u32[]{:S(2)}, u32[]{:S(2)}) collective-permute-start(bf16[32,2048]{1,0:T(8,128)(2,1)S(1)} %get-tuple-element.89.rows_ref), channel_id=1, source_target_pairs={{1,2},{2,1},{3,4},{4,3},{5,6},{6,5},{7,8},{8,7},{9,10},{10,9},{11,... | collective-permute-start | bytes 393224 | tf_op jit(solution)/shard_map/ppermute | solution.py:364
  79.1 7.5 %collective-permute-start.11 = (bf16[32,2048]{1,0:T(8,128)(2,1)S(1)}, bf16[32,2048]{1,0:T(8,128)(2,1)S(1)}, u32[]{:S(2)}, u32[]{:S(2)}) collective-permute-start(bf16[32,2048]{1,0:T(8,128)(2,1)S(1)} %get-tuple-element.94.rows_ref), channel_id=1, source_target_pairs={{1,2},{2,1},{3,4},{4,3},{5,6},{6,5},{7,8},{8,7},{9,10},{10,9},{11,... | collective-permute-start | bytes 393224 | tf_op jit(solution)/shard_map/ppermute | solution.py:364
  87.1 7.5 %collective-permute-start.13 = (bf16[32,2048]{1,0:T(8,128)(2,1)S(1)}, bf16[32,2048]{1,0:T(8,128)(2,1)S(1)}, u32[]{:S(2)}, u32[]{:S(2)}) collective-permute-start(bf16[32,2048]{1,0:T(8,128)(2,1)S(1)} %get-tuple-element.99.rows_ref), channel_id=1, source_target_pairs={{1,2},{2,1},{3,4},{4,3},{5,6},{6,5},{7,8},{8,7},{9,10},{10,9},{11,... | collective-permute-start | bytes 393224 | tf_op jit(solution)/shard_map/ppermute | solution.py:364
  94.9 7.5 %collective-permute-start.15 = (bf16[32,2048]{1,0:T(8,128)(2,1)S(1)}, bf16[32,2048]{1,0:T(8,128)(2,1)S(1)}, u32[]{:S(2)}, u32[]{:S(2)}) collective-permute-start(bf16[32,2048]{1,0:T(8,128)(2,1)S(1)} %get-tuple-element.104.rows_ref), channel_id=1, source_target_pairs={{1,2},{2,1},{3,4},{4,3},{5,6},{6,5},{7,8},{8,7},{9,10},{10,9},{11,... | collective-permute-start | bytes 393224 | tf_op jit(solution)/shard_map/ppermute | solution.py:364
  102.6 7.5 %collective-permute-start.17 = (bf16[32,2048]{1,0:T(8,128)(2,1)S(1)}, bf16[32,2048]{1,0:T(8,128)(2,1)S(1)}, u32[]{:S(2)}, u32[]{:S(2)}) collective-permute-start(bf16[32,2048]{1,0:T(8,128)(2,1)S(1)} %get-tuple-element.109.rows_ref), channel_id=1, source_target_pairs={{1,2},{2,1},{3,4},{4,3},{5,6},{6,5},{7,8},{8,7},{9,10},{10,9},{11,... | collective-permute-start | bytes 393224 | tf_op jit(solution)/shard_map/ppermute | solution.py:364
  130.5 6.8 %collective-permute-start.20 = (bf16[16,2048]{1,0:T(8,128)(2,1)S(1)}, bf16[16,2048]{1,0:T(8,128)(2,1)S(1)}, u32[]{:S(2)}, u32[]{:S(2)}) collective-permute-start(bf16[16,2048]{1,0:T(8,128)(2,1)S(1)} %get-tuple-element.116.rows_ref), channel_id=1, source_target_pairs={{1,2},{2,1},{3,4},{4,3},{5,6},{6,5},{7,8},{8,7},{9,10},{10,9},{11,... | collective-permute-start | bytes 196616 | tf_op jit(solution)/shard_map/ppermute | solution.py:364
  137.5 6.8 %collective-permute-start.22 = (bf16[16,2048]{1,0:T(8,128)(2,1)S(1)}, bf16[16,2048]{1,0:T(8,128)(2,1)S(1)}, u32[]{:S(2)}, u32[]{:S(2)}) collective-permute-start(bf16[16,2048]{1,0:T(8,128)(2,1)S(1)} %get-tuple-element.119.rows_ref), channel_id=1, source_target_pairs={{1,2},{2,1},{3,4},{4,3},{5,6},{6,5},{7,8},{8,7},{9,10},{10,9},{11,... | collective-permute-start | bytes 196616 | tf_op jit(solution)/shard_map/ppermute | solution.py:364
  144.5 6.8 %collective-permute-start.24 = (bf16[16,2048]{1,0:T(8,128)(2,1)S(1)}, bf16[16,2048]{1,0:T(8,128)(2,1)S(1)}, u32[]{:S(2)}, u32[]{:S(2)}) collective-permute-start(bf16[16,2048]{1,0:T(8,128)(2,1)S(1)} %get-tuple-element.122.rows_ref), channel_id=1, source_target_pairs={{1,2},{2,1},{3,4},{4,3},{5,6},{6,5},{7,8},{8,7},{9,10},{10,9},{11,... | collective-permute-start | bytes 196616 | tf_op jit(solution)/shard_map/ppermute | solution.py:364
  151.7 6.8 %collective-permute-start.26 = (bf16[16,2048]{1,0:T(8,128)(2,1)S(1)}, bf16[16,2048]{1,0:T(8,128)(2,1)S(1)}, u32[]{:S(2)}, u32[]{:S(2)}) collective-permute-start(bf16[16,2048]{1,0:T(8,128)(2,1)S(1)} %get-tuple-element.125.rows_ref), channel_id=1, source_target_pairs={{1,2},{2,1},{3,4},{4,3},{5,6},{6,5},{7,8},{8,7},{9,10},{10,9},{11,... | collective-permute-start | bytes 196616 | tf_op jit(solution)/shard_map/ppermute | solution.py:364
  159.0 6.8 %collective-permute-start.28 = (bf16[16,2048]{1,0:T(8,128)(2,1)S(1)}, bf16[16,2048]{1,0:T(8,128)(2,1)S(1)}, u32[]{:S(2)}, u32[]{:S(2)}) collective-permute-start(bf16[16,2048]{1,0:T(8,128)(2,1)S(1)} %get-tuple-element.128.rows_ref), channel_id=1, source_target_pairs={{1,2},{2,1},{3,4},{4,3},{5,6},{6,5},{7,8},{8,7},{9,10},{10,9},{11,... | collective-permute-start | bytes 196616 | tf_op jit(solution)/shard_map/ppermute | solution.py:364
  166.2 6.8 %collective-permute-start.30 = (bf16[16,2048]{1,0:T(8,128)(2,1)S(1)}, bf16[16,2048]{1,0:T(8,128)(2,1)S(1)}, u32[]{:S(2)}, u32[]{:S(2)}) collective-permute-start(bf16[16,2048]{1,0:T(8,128)(2,1)S(1)} %get-tuple-element.131.rows_ref), channel_id=1, source_target_pairs={{1,2},{2,1},{3,4},{4,3},{5,6},{6,5},{7,8},{8,7},{9,10},{10,9},{11,... | collective-permute-start | bytes 196616 | tf_op jit(solution)/shard_map/ppermute | solution.py:364
  173.2 6.8 %collective-permute-start.32 = (bf16[16,2048]{1,0:T(8,128)(2,1)S(1)}, bf16[16,2048]{1,0:T(8,128)(2,1)S(1)}, u32[]{:S(2)}, u32[]{:S(2)}) collective-permute-start(bf16[16,2048]{1,0:T(8,128)(2,1)S(1)} %get-tuple-element.134.rows_ref), channel_id=1, source_target_pairs={{1,2},{2,1},{3,4},{4,3},{5,6},{6,5},{7,8},{8,7},{9,10},{10,9},{11,... | collective-permute-start | bytes 196616 | tf_op jit(solution)/shard_map/ppermute | solution.py:364
  187.9 10.3 %all-to-all-start.4 = ((bf16[8,16,1024]{2,1,0:T(8,128)(2,1)}), bf16[8,16,1024]{2,1,0:T(8,128)(2,1)S(1)}, u32[]{:S(2)}, u32[]{:S(2)}) async-start(bf16[8,16,1024]{2,1,0:T(8,128)(2,1)} %back.15), calls=%async_computation.4 | async-start | bytes 524288 | tf_op jit(solution)/shard_map/all_to_all | solution.py:369
  192.1 8.2 %collective-permute-start.19 = (f32[8,2048]{1,0:T(8,128)S(1)}, f32[8,2048]{1,0:T(8,128)S(1)}, u32[]{:S(2)}, u32[]{:S(2)}) collective-permute-start(f32[8,2048]{1,0:T(8,128)S(1)} %get-tuple-element.113), channel_id=1, source_target_pairs={{0,0},{1,1},{2,2},{3,3},{4,4},{5,5},{6,6},{7,7},{8,8},{9,9},{10,10... | collective-permute-start | bytes 196616 | tf_op jit(solution)/shard_map/ppermute | solution.py:347
  198.3 7.4 %collective-permute-start.36 = (f32[8,2048]{1,0:T(8,128)S(1)}, f32[8,2048]{1,0:T(8,128)S(1)}, u32[]{:S(2)}, u32[]{:S(2)}) collective-permute-start(f32[8,2048]{1,0:T(8,128)S(1)} %gradient.1), channel_id=1, source_target_pairs={{0,0},{1,1},{2,2},{3,3},{4,4},{5,5},{6,6},{7,7},{8,8},{9,9},{10,10... | collective-permute-start | bytes 196616 | tf_op jit(solution)/shard_map/ppermute | solution.py:347
  (27 other events, 224.4 us)

commit v5 on v4

--- a/solution.py
+++ b/solution.py
@@ -10,7 +10,6 @@
 HALO = 8
 BLOCK = 128
 PAIR = 2 * BLOCK
-PIECE = BLOCK + BLOCK // 2
 VMEM = pl.BlockSpec(memory_space=pltpu.VMEM)
 SMEM = pl.BlockSpec(memory_space=pltpu.SMEM)
 F32, BF16 = jnp.float32, jnp.bfloat16
@@ -36,15 +35,11 @@
     return np.concatenate([high, low], axis=0)
 
 
-def own_weights(combos):
-    return split_weights(stencil_matrix(combos, 0))
-
-
-def side_weights(combos):
-    after, before = (stencil_matrix(combos, HALO), stencil_matrix(combos, -HALO))
-    even = split_weights(np.concatenate([before, after], axis=1))
-    odd = split_weights(np.concatenate([after, before], axis=1))
-    return np.stack([even, odd])
+def weights_of(combos):
+    own, after, before = [stencil_matrix(combos, shift) for shift in (0, HALO, -HALO)]
+    even = np.concatenate([before, after, own], axis=1)
+    odd = np.concatenate([after, before, own], axis=1)
+    return [split_weights(matrix) for matrix in (even, odd)]
 
 
 def cos_sin(theta):
@@ -84,23 +79,22 @@
     return slice(chunk * PAIR, (chunk + 1) * PAIR)
 
 
+def block_of(band_ref, index, offset):
+    pair, place = (index // 2, index % 2)
+    return jnp.concatenate([band_ref[half, pair, place, offset] for half in (0, 1)], axis=0)
+
+
 def centre_of(band_ref, pair):
-    return jnp.concatenate([band_ref[half, pair, 0:BLOCK, :] for half in (0, 1)], axis=0)
+    first, second = (2 * pair, 2 * pair + 1)
+    upper = [block_of(band_ref, first, 1), block_of(band_ref, second, 0)]
+    lower = [block_of(band_ref, first, 2), block_of(band_ref, second, 1)]
+    return jnp.concatenate(
+        [jnp.concatenate(upper, axis=1), jnp.concatenate(lower, axis=1)], axis=0
+    )
 
 
 def edge_of(band_ref, pair, side):
-    cols = slice(side * BLOCK, (side + 1) * BLOCK)
-    return jnp.concatenate([band_ref[half, pair, BLOCK:PIECE, cols] for half in (0, 1)], axis=0)
-
-
-def band_kernel(half_ref, band_ref, out_ref):
-    half = half_ref[0]
-    rows = pl.ds(pl.multiple_of(half * (BLOCK // 2), BLOCK // 2), BLOCK // 2)
-    centre = jnp.concatenate([band_ref[0, 1 + half], band_ref[1, half]], axis=1)
-    edge = jnp.concatenate([band_ref[0, 0, rows, :], band_ref[1, 2, rows, :]], axis=1)
-    for copy in range(out_ref.shape[0]):
-        out_ref[copy, 0:BLOCK, :] = centre
-        out_ref[copy, BLOCK:PIECE, :] = edge
+    return block_of(band_ref, 2 * pair + side, 2 * side)
 
 
 def merge_kernel(half_ref, own_ref, other_ref, out_ref):
@@ -132,14 +126,15 @@
     return jnp.concatenate(parts, axis=0)
 
 
-def first_kernel(omega_ref, params_ref, fields_ref, rows_ref, phased_ref, angle_ref):
+def first_kernel(omega_ref, params_ref, source_ref, receiver_ref, rows_ref, phased_ref, angle_ref):
     omega = omega_ref[0]
     for chunk in range(params_ref.shape[3] // PAIR):
         cols = columns(chunk)
         cosine, sine = cos_sin(omega * params_ref[0, 0, :, cols])
         angle_ref[0:HALO, cols] = cosine
         angle_ref[HALO : 2 * HALO, cols] = sine
-        phased = phase(fields_ref[:, cols].astype(F32), cosine, sine)
+        fields = jnp.concatenate([source_ref[:, cols], receiver_ref[:, cols]], axis=0)
+        phased = phase(fields.astype(F32), cosine, sine)
         phased_ref[:, cols] = phased
         rows_ref[:, cols] = phased.astype(BF16)
 
@@ -152,7 +147,7 @@
         cols = columns(pair)
         rows = rows_ref[:, cols]
         total = dot(rows, centre_of(band_ref, pair))
-        spread = dot(weights_ref[...], rows)
+        spread = dot(weights_ref[:, 2 * height : 3 * height], rows)
         total = total + (spread[:height] + spread[height:])
         zero = jnp.zeros((height, BLOCK), F32)
         left, right = (zero, zero)
@@ -171,8 +166,8 @@
 
 def sides(weights_ref, first_ref, second_ref, cols):
     both = jnp.concatenate([first_ref[:, cols], second_ref[:, cols]], axis=0)
-    spread = dot(weights_ref[...], both)
     height = first_ref.shape[0]
+    spread = dot(weights_ref[:, 0 : 2 * height], both)
     return spread[:height] + spread[height:]
 
 
@@ -183,9 +178,8 @@
     else:
         angle = refs[6]
         state, products, rows_next, phased_next = refs[-4:]
-    halves = products.shape[2] // PAIR
+    halves = params.shape[3] // PAIR // 2
     for index in range(halves):
-        pieces = []
         for chunk in (index, index + halves):
             cols = columns(chunk)
             total = lateral[:, cols] + sides(weights, first, second, cols)
@@ -198,7 +192,7 @@
             receiver_im = value[part[3]] + coef * total[part[2]]
             state[0:HALO, cols] = source_re
             state[HALO : 2 * HALO, cols] = source_im
-            pieces.append(source_re * receiver_re + source_im * receiver_im)
+            product = source_re * receiver_re + source_im * receiver_im
             if not last:
                 stepped = jnp.concatenate(
                     [source_re, source_im, receiver_re, receiver_im], axis=0
@@ -208,7 +202,7 @@
                 following = phase(entering, cosine, sine)
                 phased_next[:, cols] = following
                 rows_next[:, cols] = following.astype(BF16)
-        products[level, :, columns(index)] = jnp.concatenate(pieces, axis=0).astype(BF16)
+            products[level, :, cols] = product
 
 
 def mean_of(parts_ref, cols):
@@ -220,14 +214,12 @@
 
 
 def image_kernel(parts_ref, image_ref, copies_ref):
-    halves = parts_ref.shape[2] // PAIR
-    for index in range(halves):
-        cols = columns(index)
+    for chunk in range(parts_ref.shape[2] // PAIR):
+        cols = columns(chunk)
         image = mean_of(parts_ref, cols)
-        image_ref[:, cols] = image[:HALO]
-        image_ref[:, columns(index + halves)] = image[HALO:]
+        image_ref[:, cols] = image
         for copy in range(copies_ref.shape[0]):
-            copies_ref[copy, :, cols] = image.astype(BF16)
+            copies_ref[copy, :, cols] = image
 
 
 def gradient_kernel(parts_ref, gradient_ref):
@@ -247,14 +239,12 @@
 
 
 def adjoint_kernel(level, params, images, state, adjoint, scaled):
-    halves = images.shape[2] // PAIR
-    for index in range(halves):
-        image = images[level, :, columns(index)].astype(F32)
-        for chunk, part in ((index, image[:HALO]), (index + halves, image[HALO:])):
-            cols = columns(chunk)
-            value = weighted(visible(params, level, cols, part), state[:, cols])
-            adjoint[:, cols] = value
-            scaled[:, cols] = scaled_rows(value, coef_of(params, level, cols))
+    for chunk in range(images.shape[2] // PAIR):
+        cols = columns(chunk)
+        masked = visible(params, level, cols, images[level, :, cols])
+        value = weighted(masked, state[:, cols])
+        adjoint[:, cols] = value
+        scaled[:, cols] = scaled_rows(value, coef_of(params, level, cols))
 
 
 def middle_back_kernel(band_ref, weights_ref, rows_ref, lateral_ref):
@@ -264,7 +254,7 @@
         cols = columns(pair)
         rows = rows_ref[:, cols]
         total = dot_t(rows, centre_of(band_ref, pair))
-        spread = dot(weights_ref[...], rows)
+        spread = dot(weights_ref[:, 2 * height : 3 * height], rows)
         total = total + (spread[:height] + spread[height:])
         zero = jnp.zeros((height, BLOCK), F32)
         left, right = (zero, zero)
@@ -288,9 +278,7 @@
     halves = term.shape[1] // PAIR
     for index in range(halves):
         pieces = []
-        if not last:
-            image = images[level - 1, :, columns(index)].astype(F32)
-        for place, chunk in enumerate((index, index + halves)):
+        for chunk in (index, index + halves):
             cols = columns(chunk)
             total = lateral[:, cols] + sides(weights, first, second, cols)
             value = adjoint[:, cols]
@@ -306,8 +294,7 @@
                     axis=0,
                 )
                 upward = upward.astype(BF16).astype(F32)
-                part = image[place * HALO : (place + 1) * HALO]
-                masked = visible(params, level - 1, cols, part)
+                masked = visible(params, level - 1, cols, images[level - 1, :, cols])
                 following = weighted(masked, state[:, cols]) + upward
                 adjoint_next[:, cols] = following
                 scaled_next[:, cols] = scaled_rows(following, coef_of(params, level - 1, cols))
@@ -331,6 +318,21 @@
     )(*placed)
 
 
+def deliver_kernel(value_ref, out_ref):
+    out_ref[0] = value_ref[...]
+
+
+def delivered(value):
+    return pl.pallas_call(
+        deliver_kernel,
+        name="deliver",
+        out_shape=jax.ShapeDtypeStruct((1,) + value.shape, value.dtype),
+        in_specs=[VMEM],
+        out_specs=VMEM,
+        compiler_params=pltpu.CompilerParams(vmem_limit_bytes=8 << 20),
+    )(pltpu.with_memory_space_constraint(value, pltpu.VMEM))
+
+
 def frequency_of(depth, lat, sections, size):
     upper = lat >= size // 2
     return (depth + upper * (sections // 2)) % sections
@@ -338,7 +340,7 @@
 
 def home_of(row, size):
     half = size // 2
-    return row if row < half else half + (row - half - 2) % half
+    return (row + 2) % half if row < half else row
 
 
 def moved(value, inward=True):
@@ -377,22 +379,21 @@
     levels = sections
     omega = 0.1 * (lax.dynamic_slice_in_dim(freq_index, member, 1).astype(F32) + 1.0)
     odd = lax.rem(lat, 2)
-    side_fore = jnp.where(odd == 1, *side_weights(4)[::-1])
-    side_back = jnp.where(odd == 1, *side_weights(2)[::-1])
-    own_fore, own_back = (jnp.asarray(own_weights(4)), jnp.asarray(own_weights(2)))
-    source = lax.dynamic_index_in_dim(source_field, member, 0, keepdims=False)
-    receiver = lax.dynamic_index_in_dim(receiver_field, member, 0, keepdims=False)
-    fields = jnp.concatenate([source, receiver]).reshape(4 * height, width)
+    weights_fore = jnp.where(odd == 1, *weights_of(4)[::-1])
+    weights_back = jnp.where(odd == 1, *weights_of(2)[::-1])
+    fields = []
+    for field in (source_field, receiver_field):
+        own = lax.dynamic_index_in_dim(field, member, 0, keepdims=False)
+        fields.append(own.reshape(2 * height, width))
 
     wide, half, single = ((4 * height, width), (2 * height, width), (height, width))
     signed = jnp.where(image_mask[0] > 0, ffd_coef[0], -ffd_coef[0])
     own = moved(jnp.stack([slowness[0], signed]))
-    fields = moved(fields)
+    fields = [moved(field) for field in fields]
     half_index = odd.astype(jnp.int32).reshape(1)
-    (pieces,) = call(
-        band_kernel, "band", [((sections, PIECE, PAIR), BF16)], 1000, half_index, band
-    )
-    pieces = exchanged(pieces)
+    share = BLOCK // 2
+    pieces = lax.dynamic_slice_in_dim(band, odd * share, share, 2)
+    pieces = exchanged(jnp.broadcast_to(pieces[None], (sections,) + pieces.shape))
     (params,) = call(copies_kernel, "copies", [((sections, 2) + single, F32)], 1000, own)
     pieces, _ = lax.optimization_barrier((pieces, params))
     params = exchanged(params)
@@ -402,8 +403,9 @@
         merge_kernel, "merge", [((2,) + pieces.shape, BF16)], 1000, half_index, pieces, other
     )
     rows, phased, angle = call(
-        first_kernel, "first", [(wide, BF16), (wide, F32), (half, F32)], 1000, omega, params, fields
-    )
+        first_kernel, "first", [(wide, BF16), (wide, F32), (half, F32)], 1000, omega, params, *fields
+    )
+    stack = (sections, height, width)
     folded = (sections, 2 * height, width // 2)
     states, phases, angles = ([], [phased], [angle])
     products = []
@@ -419,13 +421,13 @@
             omega,
             params,
             band,
-            own_fore,
+            weights_fore,
             rows,
         )
         angles += more
-        outs = [(half, F32), (folded, BF16)]
+        outs = [(half, F32), (stack, F32)]
         outs += [] if last else [(wide, BF16), (wide, F32)]
-        args = [params, side_fore, lateral, first, second, phased] + more + products
+        args = [params, weights_fore, lateral, first, second, phased] + more + products
         state, products, *more = call(
             functools.partial(step_kernel, level, last),
             "step",
@@ -441,7 +443,7 @@
             phases.append(phased)
 
     image, images = call(
-        image_kernel, "image", [(single, F32), (folded, BF16)], 1000, exchanged(products[0])
+        image_kernel, "image", [(single, F32), (stack, F32)], 1000, exchanged(products[0])
     )
     images = exchanged(images)
     image = moved(image, False)
@@ -461,9 +463,9 @@
         last = level == 0
         first, second = swapped(scaled)
         (lateral,) = call(
-            middle_back_kernel, "middle_back", [(half, F32)], 1 << 28, band, own_back, scaled
+            middle_back_kernel, "middle_back", [(half, F32)], 1 << 28, band, weights_back, scaled
         )
-        args = [omega, params, side_back, lateral, first, second, adjoint, phases[level]]
+        args = [omega, params, weights_back, lateral, first, second, adjoint, phases[level]]
         if last:
             args += terms
             outs = [(folded, BF16)]
@@ -483,7 +485,8 @@
     (gradient,) = call(
         gradient_kernel, "gradient", [(single, F32)], 1000, exchanged(terms[0])
     )
-    return (image[None], moved(gradient, False)[None])
+    gradient = moved(gradient, False)
+    return (delivered(image), delivered(gradient))
 
 
 def solution(mesh):

time: 209 us -> 210 us (level)
  the two profiles are of different devices: /device:TPU:6 before, /device:TPU:2 now
where the time goes in v5:
time: 210 us; the launch traced here: 208 us
  starting transfers between devices  125 us (60%)
  waiting for transfers between devices  34.8 us (17%)
  blocking collectives  25.4 us (12%)
  Pallas kernels  17 us (8%)
  local copies, waits for them, and re-layouts  3.54 us (2%)
    ppermute x32, starting transfers between devices, swapped(): received.append(lax.ppermute(rows, ('depth', 'lat'), route))  91.1 us
    all_to_all x2, blocking collectives, exchanged(): return lax.all_to_all(parts, 'depth', 0, 0)  25.4 us
    all_to_all x3, starting transfers between devices, exchanged(): return lax.all_to_all(parts, 'depth', 0, 0)  19.9 us
    ppermute x5, waiting for transfers between devices, moved(): lax.ppermute(value, 'lat', route if inward else [(b, a) for a, b in route])  16.3 us
    pallas_call x38, Pallas kernels, call(): pl.pallas_call(kernel, name=name, out_shape=[pltpu.VMEM(shape, kind) for...  15.7 us
    ppermute x32, waiting for transfers between devices, swapped(): received.append(lax.ppermute(rows, ('depth', 'lat'), route))  15.3 us
    ppermute x5, starting transfers between devices, moved(): lax.ppermute(value, 'lat', route if inward else [(b, a) for a, b in route])  12.3 us
  transfers between devices with their start and end apart: 41, of which 21 were waited for; matrix products, arithmetic and copies ran while one was open for 1% of the time, Pallas kernels for 6%

profile of v5, /device:TPU:2, one launch (start us, length us, event | category | flops | bytes accessed | tf_op | source)
XLA Modules:
  0.0 208.0 jit_solution(14798987693297832067)
XLA Ops:
  2.7 9.4 %all-to-all-start.1 = ((bf16[8,2,3,64,128]{4,3,2,1,0:T(8,128)(2,1)}), bf16[8,2,3,64,128]{4,3,2,1,0:T(8,128)(2,1)S(1)}, u32[]{:S(2)}, u32[]{:S(2)}) async-start(bf16[8,2,3,64,128]{4,3,2,1,0:T(8,128)(2,1)} %broadcast_in_dim.2), calls=%async_computation.1 | async-start | bytes 1572864 | tf_op jit(solution)/shard_map/all_to_all | solution.py:371
  14.1 9.0 %collective-permute-done.value_ref = f32[2,8,2048]{2,1,0:T(8,128)S(1)} collective-permute-done((f32[2,8,2048]{2,1,0:T(8,128)S(1)}, f32[2,8,2048]{2,1,0:T(8,128)S(1)}, u32[]{:S(2)}, u32[]{:S(2)}) %collective-permute-start) | collective-permute-done | bytes 131104 | tf_op jit(solution)/shard_map/ppermute | solution.py:349
  24.2 5.8 %all-to-all-start = ((f32[8,2,8,2048]{3,2,1,0:T(8,128)}), f32[8,2,8,2048]{3,2,1,0:T(8,128)S(1)}, u32[]{:S(2)}, u32[]{:S(2)}) async-start(f32[8,2,8,2048]{3,2,1,0:T(8,128)} %copies.1), calls=%async_computation | async-start | bytes 2097152 | tf_op jit(solution)/shard_map/all_to_all | solution.py:371
  43.9 6.2 %collective-permute-start.4 = (bf16[32,2048]{1,0:T(8,128)(2,1)S(1)}, bf16[32,2048]{1,0:T(8,128)(2,1)S(1)}, u32[]{:S(2)}, u32[]{:S(2)}) collective-permute-start(bf16[32,2048]{1,0:T(8,128)(2,1)S(1)} %get-tuple-element.75.rows_ref), channel_id=1, source_target_pairs={{3,4},{4,3},{5,6},{6,5},{7,8},{8,7},{9,10},{10,9},{11,12},{12,11},... | collective-permute-start | bytes 393224 | tf_op jit(solution)/shard_map/ppermute | solution.py:366
  53.6 4.3 %collective-permute-start.6 = (bf16[32,2048]{1,0:T(8,128)(2,1)S(1)}, bf16[32,2048]{1,0:T(8,128)(2,1)S(1)}, u32[]{:S(2)}, u32[]{:S(2)}) collective-permute-start(bf16[32,2048]{1,0:T(8,128)(2,1)S(1)} %get-tuple-element.79.rows_ref), channel_id=1, source_target_pairs={{3,4},{4,3},{5,6},{6,5},{7,8},{8,7},{9,10},{10,9},{11,12},{12,11},... | collective-permute-start | bytes 393224 | tf_op jit(solution)/shard_map/ppermute | solution.py:366
  61.4 4.3 %collective-permute-start.8 = (bf16[32,2048]{1,0:T(8,128)(2,1)S(1)}, bf16[32,2048]{1,0:T(8,128)(2,1)S(1)}, u32[]{:S(2)}, u32[]{:S(2)}) collective-permute-start(bf16[32,2048]{1,0:T(8,128)(2,1)S(1)} %get-tuple-element.84.rows_ref), channel_id=1, source_target_pairs={{3,4},{4,3},{5,6},{6,5},{7,8},{8,7},{9,10},{10,9},{11,12},{12,11},... | collective-permute-start | bytes 393224 | tf_op jit(solution)/shard_map/ppermute | solution.py:366
  69.1 4.2 %collective-permute-start.10 = (bf16[32,2048]{1,0:T(8,128)(2,1)S(1)}, bf16[32,2048]{1,0:T(8,128)(2,1)S(1)}, u32[]{:S(2)}, u32[]{:S(2)}) collective-permute-start(bf16[32,2048]{1,0:T(8,128)(2,1)S(1)} %get-tuple-element.89.rows_ref), channel_id=1, source_target_pairs={{3,4},{4,3},{5,6},{6,5},{7,8},{8,7},{9,10},{10,9},{11,12},{12,11},... | collective-permute-start | bytes 393224 | tf_op jit(solution)/shard_map/ppermute | solution.py:366
  76.9 4.2 %collective-permute-start.12 = (bf16[32,2048]{1,0:T(8,128)(2,1)S(1)}, bf16[32,2048]{1,0:T(8,128)(2,1)S(1)}, u32[]{:S(2)}, u32[]{:S(2)}) collective-permute-start(bf16[32,2048]{1,0:T(8,128)(2,1)S(1)} %get-tuple-element.94.rows_ref), channel_id=1, source_target_pairs={{3,4},{4,3},{5,6},{6,5},{7,8},{8,7},{9,10},{10,9},{11,12},{12,11},... | collective-permute-start | bytes 393224 | tf_op jit(solution)/shard_map/ppermute | solution.py:366
  84.6 4.3 %collective-permute-start.14 = (bf16[32,2048]{1,0:T(8,128)(2,1)S(1)}, bf16[32,2048]{1,0:T(8,128)(2,1)S(1)}, u32[]{:S(2)}, u32[]{:S(2)}) collective-permute-start(bf16[32,2048]{1,0:T(8,128)(2,1)S(1)} %get-tuple-element.99.rows_ref), channel_id=1, source_target_pairs={{3,4},{4,3},{5,6},{6,5},{7,8},{8,7},{9,10},{10,9},{11,12},{12,11},... | collective-permute-start | bytes 393224 | tf_op jit(solution)/shard_map/ppermute | solution.py:366
  92.4 4.3 %collective-permute-start.16 = (bf16[32,2048]{1,0:T(8,128)(2,1)S(1)}, bf16[32,2048]{1,0:T(8,128)(2,1)S(1)}, u32[]{:S(2)}, u32[]{:S(2)}) collective-permute-start(bf16[32,2048]{1,0:T(8,128)(2,1)S(1)} %get-tuple-element.104.rows_ref), channel_id=1, source_target_pairs={{3,4},{4,3},{5,6},{6,5},{7,8},{8,7},{9,10},{10,9},{11,12},{12,11},... | collective-permute-start | bytes 393224 | tf_op jit(solution)/shard_map/ppermute | solution.py:366
  100.1 4.3 %collective-permute-start.18 = (bf16[32,2048]{1,0:T(8,128)(2,1)S(1)}, bf16[32,2048]{1,0:T(8,128)(2,1)S(1)}, u32[]{:S(2)}, u32[]{:S(2)}) collective-permute-start(bf16[32,2048]{1,0:T(8,128)(2,1)S(1)} %get-tuple-element.109.rows_ref), channel_id=1, source_target_pairs={{3,4},{4,3},{5,6},{6,5},{7,8},{8,7},{9,10},{10,9},{11,12},{12,11},... | collective-permute-start | bytes 393224 | tf_op jit(solution)/shard_map/ppermute | solution.py:366
  107.8 13.3 %all_to_all.25.parts_ref = f32[8,8,2048]{2,1,0:T(8,128)S(1)} all-to-all(f32[8,8,2048]{2,1,0:T(8,128)S(1)} %get-tuple-element.112), channel_id=1, replica_groups=mesh['depth'=8,'lat'=64] {'depth'}, dimensions={0} | all-to-all | bytes 1048576 | tf_op jit(solution)/shard_map/all_to_all | solution.py:371
  121.1 12.2 %all_to_all.26.images.refs_9_ = f32[8,8,2048]{2,1,0:T(8,128)S(1)} all-to-all(f32[8,8,2048]{2,1,0:T(8,128)S(1)} %get-tuple-element.114), channel_id=1, replica_groups=mesh['depth'=8,'lat'=64] {'depth'}, dimensions={0} | all-to-all | bytes 1048576 | tf_op jit(solution)/shard_map/all_to_all | solution.py:371
  140.4 3.1 %collective-permute-start.23 = (bf16[16,2048]{1,0:T(8,128)(2,1)S(1)}, bf16[16,2048]{1,0:T(8,128)(2,1)S(1)}, u32[]{:S(2)}, u32[]{:S(2)}) collective-permute-start(bf16[16,2048]{1,0:T(8,128)(2,1)S(1)} %get-tuple-element.119.rows_ref), channel_id=1, source_target_pairs={{3,4},{4,3},{5,6},{6,5},{7,8},{8,7},{9,10},{10,9},{11,12},{12,11},... | collective-permute-start | bytes 196616 | tf_op jit(solution)/shard_map/ppermute | solution.py:366
  147.4 3.1 %collective-permute-start.25 = (bf16[16,2048]{1,0:T(8,128)(2,1)S(1)}, bf16[16,2048]{1,0:T(8,128)(2,1)S(1)}, u32[]{:S(2)}, u32[]{:S(2)}) collective-permute-start(bf16[16,2048]{1,0:T(8,128)(2,1)S(1)} %get-tuple-element.122.rows_ref), channel_id=1, source_target_pairs={{3,4},{4,3},{5,6},{6,5},{7,8},{8,7},{9,10},{10,9},{11,12},{12,11},... | collective-permute-start | bytes 196616 | tf_op jit(solution)/shard_map/ppermute | solution.py:366
  154.4 3.1 %collective-permute-start.27 = (bf16[16,2048]{1,0:T(8,128)(2,1)S(1)}, bf16[16,2048]{1,0:T(8,128)(2,1)S(1)}, u32[]{:S(2)}, u32[]{:S(2)}) collective-permute-start(bf16[16,2048]{1,0:T(8,128)(2,1)S(1)} %get-tuple-element.125.rows_ref), channel_id=1, source_target_pairs={{3,4},{4,3},{5,6},{6,5},{7,8},{8,7},{9,10},{10,9},{11,12},{12,11},... | collective-permute-start | bytes 196616 | tf_op jit(solution)/shard_map/ppermute | solution.py:366
  161.4 3.1 %collective-permute-start.29 = (bf16[16,2048]{1,0:T(8,128)(2,1)S(1)}, bf16[16,2048]{1,0:T(8,128)(2,1)S(1)}, u32[]{:S(2)}, u32[]{:S(2)}) collective-permute-start(bf16[16,2048]{1,0:T(8,128)(2,1)S(1)} %get-tuple-element.128.rows_ref), channel_id=1, source_target_pairs={{3,4},{4,3},{5,6},{6,5},{7,8},{8,7},{9,10},{10,9},{11,12},{12,11},... | collective-permute-start | bytes 196616 | tf_op jit(solution)/shard_map/ppermute | solution.py:366
  168.4 3.1 %collective-permute-start.31 = (bf16[16,2048]{1,0:T(8,128)(2,1)S(1)}, bf16[16,2048]{1,0:T(8,128)(2,1)S(1)}, u32[]{:S(2)}, u32[]{:S(2)}) collective-permute-start(bf16[16,2048]{1,0:T(8,128)(2,1)S(1)} %get-tuple-element.131.rows_ref), channel_id=1, source_target_pairs={{3,4},{4,3},{5,6},{6,5},{7,8},{8,7},{9,10},{10,9},{11,12},{12,11},... | collective-permute-start | bytes 196616 | tf_op jit(solution)/shard_map/ppermute | solution.py:366
  175.4 3.1 %collective-permute-start.33 = (bf16[16,2048]{1,0:T(8,128)(2,1)S(1)}, bf16[16,2048]{1,0:T(8,128)(2,1)S(1)}, u32[]{:S(2)}, u32[]{:S(2)}) collective-permute-start(bf16[16,2048]{1,0:T(8,128)(2,1)S(1)} %get-tuple-element.134.rows_ref), channel_id=1, source_target_pairs={{3,4},{4,3},{5,6},{6,5},{7,8},{8,7},{9,10},{10,9},{11,12},{12,11},... | collective-permute-start | bytes 196616 | tf_op jit(solution)/shard_map/ppermute | solution.py:366
  182.4 3.1 %collective-permute-start.35 = (bf16[16,2048]{1,0:T(8,128)(2,1)S(1)}, bf16[16,2048]{1,0:T(8,128)(2,1)S(1)}, u32[]{:S(2)}, u32[]{:S(2)}) collective-permute-start(bf16[16,2048]{1,0:T(8,128)(2,1)S(1)} %get-tuple-element.137.rows_ref), channel_id=1, source_target_pairs={{3,4},{4,3},{5,6},{6,5},{7,8},{8,7},{9,10},{10,9},{11,12},{12,11},... | collective-permute-start | bytes 196616 | tf_op jit(solution)/shard_map/ppermute | solution.py:366
  190.1 4.7 %all-to-all-start.4 = ((bf16[8,16,1024]{2,1,0:T(8,128)(2,1)}), bf16[8,16,1024]{2,1,0:T(8,128)(2,1)S(1)}, u32[]{:S(2)}, u32[]{:S(2)}) async-start(bf16[8,16,1024]{2,1,0:T(8,128)(2,1)} %back.15), calls=%async_computation.4 | async-start | bytes 524288 | tf_op jit(solution)/shard_map/all_to_all | solution.py:371
  194.8 3.2 %collective-permute-start.20 = (f32[8,2048]{1,0:T(8,128)S(1)}, f32[8,2048]{1,0:T(8,128)S(1)}, u32[]{:S(2)}, u32[]{:S(2)}) collective-permute-start(f32[8,2048]{1,0:T(8,128)S(1)} %get-tuple-element.113), channel_id=1, source_target_pairs={{2,0},{3,1},{4,2},{5,3},{6,4},{7,5},{8,6},{9,7},{10,8},{11,9},{12,... | collective-permute-start | bytes 196616 | tf_op jit(solution)/shard_map/ppermute | solution.py:349
  198.0 3.2 %all-to-all-done.4.parts_ref = bf16[8,16,1024]{2,1,0:T(8,128)(2,1)S(1)} async-done(((bf16[8,16,1024]{2,1,0:T(8,128)(2,1)}), bf16[8,16,1024]{2,1,0:T(8,128)(2,1)S(1)}, u32[]{:S(2)}, u32[]{:S(2)}) %all-to-all-start.4) | async-done | bytes 262176 | tf_op jit(solution)/shard_map/all_to_all | solution.py:371
  201.2 3.4 %collective-permute-start.37 = (f32[8,2048]{1,0:T(8,128)S(1)}, f32[8,2048]{1,0:T(8,128)S(1)}, u32[]{:S(2)}, u32[]{:S(2)}) collective-permute-start(f32[8,2048]{1,0:T(8,128)S(1)} %gradient.1), channel_id=1, source_target_pairs={{2,0},{3,1},{4,2},{5,3},{6,4},{7,5},{8,6},{9,7},{10,8},{11,9},{12,... | collective-permute-start | bytes 196616 | tf_op jit(solution)/shard_map/ppermute | solution.py:349
  (127 shorter events, 84.1 us)
Async XLA Ops:
  2.7 21.4 %all-to-all-start.1 = ((bf16[8,2,3,64,128]{4,3,2,1,0:T(8,128)(2,1)}), bf16[8,2,3,64,128]{4,3,2,1,0:T(8,128)(2,1)S(1)}, u32[]{:S(2)}, u32[]{:S(2)}) async-start(bf16[8,2,3,64,128]{4,3,2,1,0:T(8,128)(2,1)} %broadcast_in_dim.2), calls=%async_computation.1 | async-start | bytes 1572864 | tf_op jit(solution)/shard_map/all_to_all | solution.py:371
  12.2 10.9 %collective-permute-start = (f32[2,8,2048]{2,1,0:T(8,128)S(1)}, f32[2,8,2048]{2,1,0:T(8,128)S(1)}, u32[]{:S(2)}, u32[]{:S(2)}) collective-permute-start(f32[2,8,2048]{2,1,0:T(8,128)S(1)} %pad_maximum_fusion), channel_id=1, source_target_pairs={{0,2},{1,3},{2,4},{3,5},{4,6},{5,7},{6,8},{7,9},{8,10},{9,11},{10,... | collective-permute-start | bytes 393224 | tf_op jit(solution)/shard_map/ppermute | solution.py:349
  24.2 19.0 %all-to-all-start = ((f32[8,2,8,2048]{3,2,1,0:T(8,128)}), f32[8,2,8,2048]{3,2,1,0:T(8,128)S(1)}, u32[]{:S(2)}, u32[]{:S(2)}) async-start(f32[8,2,8,2048]{3,2,1,0:T(8,128)} %copies.1), calls=%async_computation | async-start | bytes 2097152 | tf_op jit(solution)/shard_map/all_to_all | solution.py:371
  30.0 22.1 %collective-permute-start.1 = (bf16[8,2,3,64,128]{4,3,2,1,0:T(8,128)(2,1)S(1)}, bf16[8,2,3,64,128]{4,3,2,1,0:T(8,128)(2,1)S(1)}, u32[]{:S(2)}, u32[]{:S(2)}) collective-permute-start(bf16[8,2,3,64,128]{4,3,2,1,0:T(8,128)(2,1)S(1)} %all-to-all-done.1.own_ref), channel_id=1, source_target_pairs={{0,1},{1,0},{2,3},{3,2},{4,5},{5,4},{6,7},{7,6},{8,9},{9,8},{10,11... | collective-permute-start | bytes 2359304 | tf_op jit(solution)/shard_map/ppermute | solution.py:401
  32.0 8.5 %collective-permute-start.2 = (bf16[16,2048]{1,0:T(8,128)(2,1)S(1)}, bf16[16,2048]{1,0:T(8,128)(2,1)S(1)}, u32[]{:S(2)}, u32[]{:S(2)}) collective-permute-start(bf16[16,2048]{1,0:T(8,128)(2,1)S(1)} %dynamic-slice_bitcast_fusion.1), channel_id=1, source_target_pairs={{0,2},{1,3},{2,4},{3,5},{4,6},{5,7},{6,8},{7,9},{8,10},{9,11},{10,... | collective-permute-start | bytes 196616 | tf_op jit(solution)/shard_map/ppermute | solution.py:349
  34.7 8.4 %collective-permute-start.3 = (bf16[16,2048]{1,0:T(8,128)(2,1)S(1)}, bf16[16,2048]{1,0:T(8,128)(2,1)S(1)}, u32[]{:S(2)}, u32[]{:S(2)}) collective-permute-start(bf16[16,2048]{1,0:T(8,128)(2,1)S(1)} %dynamic-slice_bitcast_fusion), channel_id=1, source_target_pairs={{0,2},{1,3},{2,4},{3,5},{4,6},{5,7},{6,8},{7,9},{8,10},{9,11},{10,... | collective-permute-start | bytes 196616 | tf_op jit(solution)/shard_map/ppermute | solution.py:349
  43.9 8.9 %collective-permute-start.4 = (bf16[32,2048]{1,0:T(8,128)(2,1)S(1)}, bf16[32,2048]{1,0:T(8,128)(2,1)S(1)}, u32[]{:S(2)}, u32[]{:S(2)}) collective-permute-start(bf16[32,2048]{1,0:T(8,128)(2,1)S(1)} %get-tuple-element.75.rows_ref), channel_id=1, source_target_pairs={{3,4},{4,3},{5,6},{6,5},{7,8},{8,7},{9,10},{10,9},{11,12},{12,11},... | collective-permute-start | bytes 393224 | tf_op jit(solution)/shard_map/ppermute | solution.py:366
  53.6 7.5 %collective-permute-start.6 = (bf16[32,2048]{1,0:T(8,128)(2,1)S(1)}, bf16[32,2048]{1,0:T(8,128)(2,1)S(1)}, u32[]{:S(2)}, u32[]{:S(2)}) collective-permute-start(bf16[32,2048]{1,0:T(8,128)(2,1)S(1)} %get-tuple-element.79.rows_ref), channel_id=1, source_target_pairs={{3,4},{4,3},{5,6},{6,5},{7,8},{8,7},{9,10},{10,9},{11,12},{12,11},... | collective-permute-start | bytes 393224 | tf_op jit(solution)/shard_map/ppermute | solution.py:366
  61.4 7.5 %collective-permute-start.8 = (bf16[32,2048]{1,0:T(8,128)(2,1)S(1)}, bf16[32,2048]{1,0:T(8,128)(2,1)S(1)}, u32[]{:S(2)}, u32[]{:S(2)}) collective-permute-start(bf16[32,2048]{1,0:T(8,128)(2,1)S(1)} %get-tuple-element.84.rows_ref), channel_id=1, source_target_pairs={{3,4},{4,3},{5,6},{6,5},{7,8},{8,7},{9,10},{10,9},{11,12},{12,11},... | collective-permute-start | bytes 393224 | tf_op jit(solution)/shard_map/ppermute | solution.py:366
  69.1 7.5 %collective-permute-start.10 = (bf16[32,2048]{1,0:T(8,128)(2,1)S(1)}, bf16[32,2048]{1,0:T(8,128)(2,1)S(1)}, u32[]{:S(2)}, u32[]{:S(2)}) collective-permute-start(bf16[32,2048]{1,0:T(8,128)(2,1)S(1)} %get-tuple-element.89.rows_ref), channel_id=1, source_target_pairs={{3,4},{4,3},{5,6},{6,5},{7,8},{8,7},{9,10},{10,9},{11,12},{12,11},... | collective-permute-start | bytes 393224 | tf_op jit(solution)/shard_map/ppermute | solution.py:366
  76.9 7.5 %collective-permute-start.12 = (bf16[32,2048]{1,0:T(8,128)(2,1)S(1)}, bf16[32,2048]{1,0:T(8,128)(2,1)S(1)}, u32[]{:S(2)}, u32[]{:S(2)}) collective-permute-start(bf16[32,2048]{1,0:T(8,128)(2,1)S(1)} %get-tuple-element.94.rows_ref), channel_id=1, source_target_pairs={{3,4},{4,3},{5,6},{6,5},{7,8},{8,7},{9,10},{10,9},{11,12},{12,11},... | collective-permute-start | bytes 393224 | tf_op jit(solution)/shard_map/ppermute | solution.py:366
  84.6 7.5 %collective-permute-start.14 = (bf16[32,2048]{1,0:T(8,128)(2,1)S(1)}, bf16[32,2048]{1,0:T(8,128)(2,1)S(1)}, u32[]{:S(2)}, u32[]{:S(2)}) collective-permute-start(bf16[32,2048]{1,0:T(8,128)(2,1)S(1)} %get-tuple-element.99.rows_ref), channel_id=1, source_target_pairs={{3,4},{4,3},{5,6},{6,5},{7,8},{8,7},{9,10},{10,9},{11,12},{12,11},... | collective-permute-start | bytes 393224 | tf_op jit(solution)/shard_map/ppermute | solution.py:366
  92.4 7.5 %collective-permute-start.16 = (bf16[32,2048]{1,0:T(8,128)(2,1)S(1)}, bf16[32,2048]{1,0:T(8,128)(2,1)S(1)}, u32[]{:S(2)}, u32[]{:S(2)}) collective-permute-start(bf16[32,2048]{1,0:T(8,128)(2,1)S(1)} %get-tuple-element.104.rows_ref), channel_id=1, source_target_pairs={{3,4},{4,3},{5,6},{6,5},{7,8},{8,7},{9,10},{10,9},{11,12},{12,11},... | collective-permute-start | bytes 393224 | tf_op jit(solution)/shard_map/ppermute | solution.py:366
  100.1 7.5 %collective-permute-start.18 = (bf16[32,2048]{1,0:T(8,128)(2,1)S(1)}, bf16[32,2048]{1,0:T(8,128)(2,1)S(1)}, u32[]{:S(2)}, u32[]{:S(2)}) collective-permute-start(bf16[32,2048]{1,0:T(8,128)(2,1)S(1)} %get-tuple-element.109.rows_ref), channel_id=1, source_target_pairs={{3,4},{4,3},{5,6},{6,5},{7,8},{8,7},{9,10},{10,9},{11,12},{12,11},... | collective-permute-start | bytes 393224 | tf_op jit(solution)/shard_map/ppermute | solution.py:366
  133.4 6.8 %collective-permute-start.21 = (bf16[16,2048]{1,0:T(8,128)(2,1)S(1)}, bf16[16,2048]{1,0:T(8,128)(2,1)S(1)}, u32[]{:S(2)}, u32[]{:S(2)}) collective-permute-start(bf16[16,2048]{1,0:T(8,128)(2,1)S(1)} %get-tuple-element.116.rows_ref), channel_id=1, source_target_pairs={{3,4},{4,3},{5,6},{6,5},{7,8},{8,7},{9,10},{10,9},{11,12},{12,11},... | collective-permute-start | bytes 196616 | tf_op jit(solution)/shard_map/ppermute | solution.py:366
  140.4 6.8 %collective-permute-start.23 = (bf16[16,2048]{1,0:T(8,128)(2,1)S(1)}, bf16[16,2048]{1,0:T(8,128)(2,1)S(1)}, u32[]{:S(2)}, u32[]{:S(2)}) collective-permute-start(bf16[16,2048]{1,0:T(8,128)(2,1)S(1)} %get-tuple-element.119.rows_ref), channel_id=1, source_target_pairs={{3,4},{4,3},{5,6},{6,5},{7,8},{8,7},{9,10},{10,9},{11,12},{12,11},... | collective-permute-start | bytes 196616 | tf_op jit(solution)/shard_map/ppermute | solution.py:366
  147.4 6.8 %collective-permute-start.25 = (bf16[16,2048]{1,0:T(8,128)(2,1)S(1)}, bf16[16,2048]{1,0:T(8,128)(2,1)S(1)}, u32[]{:S(2)}, u32[]{:S(2)}) collective-permute-start(bf16[16,2048]{1,0:T(8,128)(2,1)S(1)} %get-tuple-element.122.rows_ref), channel_id=1, source_target_pairs={{3,4},{4,3},{5,6},{6,5},{7,8},{8,7},{9,10},{10,9},{11,12},{12,11},... | collective-permute-start | bytes 196616 | tf_op jit(solution)/shard_map/ppermute | solution.py:366
  154.4 6.8 %collective-permute-start.27 = (bf16[16,2048]{1,0:T(8,128)(2,1)S(1)}, bf16[16,2048]{1,0:T(8,128)(2,1)S(1)}, u32[]{:S(2)}, u32[]{:S(2)}) collective-permute-start(bf16[16,2048]{1,0:T(8,128)(2,1)S(1)} %get-tuple-element.125.rows_ref), channel_id=1, source_target_pairs={{3,4},{4,3},{5,6},{6,5},{7,8},{8,7},{9,10},{10,9},{11,12},{12,11},... | collective-permute-start | bytes 196616 | tf_op jit(solution)/shard_map/ppermute | solution.py:366
  161.4 6.8 %collective-permute-start.29 = (bf16[16,2048]{1,0:T(8,128)(2,1)S(1)}, bf16[16,2048]{1,0:T(8,128)(2,1)S(1)}, u32[]{:S(2)}, u32[]{:S(2)}) collective-permute-start(bf16[16,2048]{1,0:T(8,128)(2,1)S(1)} %get-tuple-element.128.rows_ref), channel_id=1, source_target_pairs={{3,4},{4,3},{5,6},{6,5},{7,8},{8,7},{9,10},{10,9},{11,12},{12,11},... | collective-permute-start | bytes 196616 | tf_op jit(solution)/shard_map/ppermute | solution.py:366
  168.4 6.8 %collective-permute-start.31 = (bf16[16,2048]{1,0:T(8,128)(2,1)S(1)}, bf16[16,2048]{1,0:T(8,128)(2,1)S(1)}, u32[]{:S(2)}, u32[]{:S(2)}) collective-permute-start(bf16[16,2048]{1,0:T(8,128)(2,1)S(1)} %get-tuple-element.131.rows_ref), channel_id=1, source_target_pairs={{3,4},{4,3},{5,6},{6,5},{7,8},{8,7},{9,10},{10,9},{11,12},{12,11},... | collective-permute-start | bytes 196616 | tf_op jit(solution)/shard_map/ppermute | solution.py:366
  175.4 6.8 %collective-permute-start.33 = (bf16[16,2048]{1,0:T(8,128)(2,1)S(1)}, bf16[16,2048]{1,0:T(8,128)(2,1)S(1)}, u32[]{:S(2)}, u32[]{:S(2)}) collective-permute-start(bf16[16,2048]{1,0:T(8,128)(2,1)S(1)} %get-tuple-element.134.rows_ref), channel_id=1, source_target_pairs={{3,4},{4,3},{5,6},{6,5},{7,8},{8,7},{9,10},{10,9},{11,12},{12,11},... | collective-permute-start | bytes 196616 | tf_op jit(solution)/shard_map/ppermute | solution.py:366
  182.4 6.8 %collective-permute-start.35 = (bf16[16,2048]{1,0:T(8,128)(2,1)S(1)}, bf16[16,2048]{1,0:T(8,128)(2,1)S(1)}, u32[]{:S(2)}, u32[]{:S(2)}) collective-permute-start(bf16[16,2048]{1,0:T(8,128)(2,1)S(1)} %get-tuple-element.137.rows_ref), channel_id=1, source_target_pairs={{3,4},{4,3},{5,6},{6,5},{7,8},{8,7},{9,10},{10,9},{11,12},{12,11},... | collective-permute-start | bytes 196616 | tf_op jit(solution)/shard_map/ppermute | solution.py:366
  190.1 11.1 %all-to-all-start.4 = ((bf16[8,16,1024]{2,1,0:T(8,128)(2,1)}), bf16[8,16,1024]{2,1,0:T(8,128)(2,1)S(1)}, u32[]{:S(2)}, u32[]{:S(2)}) async-start(bf16[8,16,1024]{2,1,0:T(8,128)(2,1)} %back.15), calls=%async_computation.4 | async-start | bytes 524288 | tf_op jit(solution)/shard_map/all_to_all | solution.py:371
  194.8 9.9 %collective-permute-start.20 = (f32[8,2048]{1,0:T(8,128)S(1)}, f32[8,2048]{1,0:T(8,128)S(1)}, u32[]{:S(2)}, u32[]{:S(2)}) collective-permute-start(f32[8,2048]{1,0:T(8,128)S(1)} %get-tuple-element.113), channel_id=1, source_target_pairs={{2,0},{3,1},{4,2},{5,3},{6,4},{7,5},{8,6},{9,7},{10,8},{11,9},{12,... | collective-permute-start | bytes 196616 | tf_op jit(solution)/shard_map/ppermute | solution.py:349
  (26 other events, 241.5 us)

commit v6 on v5

--- a/solution.py
+++ b/solution.py
@@ -97,6 +97,18 @@
     return block_of(band_ref, 2 * pair + side, 2 * side)
 
 
+def share_kernel(half_ref, band_ref, out_ref, semaphores):
+    share = out_ref.shape[3]
+    rows = pl.ds(pl.multiple_of(half_ref[0] * share, share), share)
+    copies = []
+    for copy in range(out_ref.shape[0]):
+        source = band_ref.at[:, :, rows, :]
+        copies.append(pltpu.make_async_copy(source, out_ref.at[copy], semaphores.at[copy]))
+        copies[-1].start()
+    for copy in copies:
+        copy.wait()
+
+
 def merge_kernel(half_ref, own_ref, other_ref, out_ref):
     half = half_ref[0]
     out_ref[half] = own_ref[...]
@@ -126,13 +138,11 @@
     return jnp.concatenate(parts, axis=0)
 
 
-def first_kernel(omega_ref, params_ref, source_ref, receiver_ref, rows_ref, phased_ref, angle_ref):
+def first_kernel(omega_ref, params_ref, source_ref, receiver_ref, rows_ref, phased_ref):
     omega = omega_ref[0]
     for chunk in range(params_ref.shape[3] // PAIR):
         cols = columns(chunk)
         cosine, sine = cos_sin(omega * params_ref[0, 0, :, cols])
-        angle_ref[0:HALO, cols] = cosine
-        angle_ref[HALO : 2 * HALO, cols] = sine
         fields = jnp.concatenate([source_ref[:, cols], receiver_ref[:, cols]], axis=0)
         phased = phase(fields.astype(F32), cosine, sine)
         phased_ref[:, cols] = phased
@@ -392,8 +402,16 @@
     fields = [moved(field) for field in fields]
     half_index = odd.astype(jnp.int32).reshape(1)
     share = BLOCK // 2
-    pieces = lax.dynamic_slice_in_dim(band, odd * share, share, 2)
-    pieces = exchanged(jnp.broadcast_to(pieces[None], (sections,) + pieces.shape))
+    pieces = pl.pallas_call(
+        share_kernel,
+        name="share",
+        out_shape=jax.ShapeDtypeStruct((sections,) + band.shape[:2] + (share, BLOCK), BF16),
+        in_specs=[SMEM, pl.BlockSpec(memory_space=pl.ANY)],
+        out_specs=pl.BlockSpec(memory_space=pl.ANY),
+        scratch_shapes=[pltpu.SemaphoreType.DMA((sections,))],
+        compiler_params=pltpu.CompilerParams(vmem_limit_bytes=8 << 20),
+    )(half_index, pltpu.with_memory_space_constraint(band, pltpu.VMEM))
+    pieces = exchanged(pieces)
     (params,) = call(copies_kernel, "copies", [((sections, 2) + single, F32)], 1000, own)
     pieces, _ = lax.optimization_barrier((pieces, params))
     params = exchanged(params)
@@ -402,12 +420,12 @@
     (band,) = call(
         merge_kernel, "merge", [((2,) + pieces.shape, BF16)], 1000, half_index, pieces, other
     )
-    rows, phased, angle = call(
-        first_kernel, "first", [(wide, BF16), (wide, F32), (half, F32)], 1000, omega, params, *fields
+    rows, phased = call(
+        first_kernel, "first", [(wide, BF16), (wide, F32)], 1000, omega, params, *fields
     )
     stack = (sections, height, width)
     folded = (sections, 2 * height, width // 2)
-    states, phases, angles = ([], [phased], [angle])
+    states, phases, angles = ([], [phased], [None])
     products = []
     for level in range(levels):
         last = level == levels - 1

time: 210 us -> 209 us (level)
  transfers between devices with their start and end apart: 41 -> 41, of which waited for: 21 -> 22; matrix products, arithmetic and copies ran while one was open for 1% -> 1% of each run, Pallas kernels for 6% -> 6%
where the time goes in v6:
time: 209 us; the launch traced here: 207 us
  starting transfers between devices  125 us (60%)
  waiting for transfers between devices  34.8 us (17%)
  blocking collectives  25.4 us (12%)
  Pallas kernels  17.3 us (8%)
  local copies, waits for them, and re-layouts  2.47 us (1%)
    ppermute x32, starting transfers between devices, swapped(): received.append(lax.ppermute(rows, ('depth', 'lat'), route))  91.1 us
    all_to_all x2, blocking collectives, exchanged(): return lax.all_to_all(parts, 'depth', 0, 0)  25.4 us
    all_to_all x3, starting transfers between devices, exchanged(): return lax.all_to_all(parts, 'depth', 0, 0)  20 us
    ppermute x5, waiting for transfers between devices, moved(): lax.ppermute(value, 'lat', route if inward else [(b, a) for a, b in route])  16.3 us
    ppermute x32, waiting for transfers between devices, swapped(): received.append(lax.ppermute(rows, ('depth', 'lat'), route))  15.3 us
    pallas_call x38, Pallas kernels, call(): pl.pallas_call(kernel, name=name, out_shape=[pltpu.VMEM(shape, kind) for...  15.1 us
    ppermute x5, starting transfers between devices, moved(): lax.ppermute(value, 'lat', route if inward else [(b, a) for a, b in route])  12.3 us
  transfers between devices with their start and end apart: 41, of which 22 were waited for; matrix products, arithmetic and copies ran while one was open for 1% of the time, Pallas kernels for 6%

profile of v6, /device:TPU:2, one launch (start us, length us, event | category | flops | bytes accessed | tf_op | source)
XLA Modules:
  0.0 207.3 jit_solution(6784147169948306571)
XLA Ops:
  2.6 9.4 %all-to-all-start.1 = ((bf16[8,2,3,64,128]{4,3,2,1,0:T(8,128)(2,1)}), bf16[8,2,3,64,128]{4,3,2,1,0:T(8,128)(2,1)S(1)}, u32[]{:S(2)}, u32[]{:S(2)}) async-start(bf16[8,2,3,64,128]{4,3,2,1,0:T(8,128)(2,1)} %share.1), calls=%async_computation.1 | async-start | bytes 1572864 | tf_op jit(solution)/shard_map/all_to_all | solution.py:381
  14.0 9.0 %collective-permute-done.value_ref = f32[2,8,2048]{2,1,0:T(8,128)S(1)} collective-permute-done((f32[2,8,2048]{2,1,0:T(8,128)S(1)}, f32[2,8,2048]{2,1,0:T(8,128)S(1)}, u32[]{:S(2)}, u32[]{:S(2)}) %collective-permute-start) | collective-permute-done | bytes 131104 | tf_op jit(solution)/shard_map/ppermute | solution.py:359
  24.0 5.8 %all-to-all-start = ((f32[8,2,8,2048]{3,2,1,0:T(8,128)}), f32[8,2,8,2048]{3,2,1,0:T(8,128)S(1)}, u32[]{:S(2)}, u32[]{:S(2)}) async-start(f32[8,2,8,2048]{3,2,1,0:T(8,128)} %copies.1), calls=%async_computation | async-start | bytes 2097152 | tf_op jit(solution)/shard_map/all_to_all | solution.py:381
  43.2 6.2 %collective-permute-start.4 = (bf16[32,2048]{1,0:T(8,128)(2,1)S(1)}, bf16[32,2048]{1,0:T(8,128)(2,1)S(1)}, u32[]{:S(2)}, u32[]{:S(2)}) collective-permute-start(bf16[32,2048]{1,0:T(8,128)(2,1)S(1)} %get-tuple-element.75.rows_ref), channel_id=1, source_target_pairs={{3,4},{4,3},{5,6},{6,5},{7,8},{8,7},{9,10},{10,9},{11,12},{12,11},... | collective-permute-start | bytes 393224 | tf_op jit(solution)/shard_map/ppermute | solution.py:376
  52.9 4.3 %collective-permute-start.6 = (bf16[32,2048]{1,0:T(8,128)(2,1)S(1)}, bf16[32,2048]{1,0:T(8,128)(2,1)S(1)}, u32[]{:S(2)}, u32[]{:S(2)}) collective-permute-start(bf16[32,2048]{1,0:T(8,128)(2,1)S(1)} %get-tuple-element.79.rows_ref), channel_id=1, source_target_pairs={{3,4},{4,3},{5,6},{6,5},{7,8},{8,7},{9,10},{10,9},{11,12},{12,11},... | collective-permute-start | bytes 393224 | tf_op jit(solution)/shard_map/ppermute | solution.py:376
  60.7 4.3 %collective-permute-start.8 = (bf16[32,2048]{1,0:T(8,128)(2,1)S(1)}, bf16[32,2048]{1,0:T(8,128)(2,1)S(1)}, u32[]{:S(2)}, u32[]{:S(2)}) collective-permute-start(bf16[32,2048]{1,0:T(8,128)(2,1)S(1)} %get-tuple-element.84.rows_ref), channel_id=1, source_target_pairs={{3,4},{4,3},{5,6},{6,5},{7,8},{8,7},{9,10},{10,9},{11,12},{12,11},... | collective-permute-start | bytes 393224 | tf_op jit(solution)/shard_map/ppermute | solution.py:376
  68.4 4.3 %collective-permute-start.10 = (bf16[32,2048]{1,0:T(8,128)(2,1)S(1)}, bf16[32,2048]{1,0:T(8,128)(2,1)S(1)}, u32[]{:S(2)}, u32[]{:S(2)}) collective-permute-start(bf16[32,2048]{1,0:T(8,128)(2,1)S(1)} %get-tuple-element.89.rows_ref), channel_id=1, source_target_pairs={{3,4},{4,3},{5,6},{6,5},{7,8},{8,7},{9,10},{10,9},{11,12},{12,11},... | collective-permute-start | bytes 393224 | tf_op jit(solution)/shard_map/ppermute | solution.py:376
  76.2 4.3 %collective-permute-start.12 = (bf16[32,2048]{1,0:T(8,128)(2,1)S(1)}, bf16[32,2048]{1,0:T(8,128)(2,1)S(1)}, u32[]{:S(2)}, u32[]{:S(2)}) collective-permute-start(bf16[32,2048]{1,0:T(8,128)(2,1)S(1)} %get-tuple-element.94.rows_ref), channel_id=1, source_target_pairs={{3,4},{4,3},{5,6},{6,5},{7,8},{8,7},{9,10},{10,9},{11,12},{12,11},... | collective-permute-start | bytes 393224 | tf_op jit(solution)/shard_map/ppermute | solution.py:376
  83.9 4.3 %collective-permute-start.14 = (bf16[32,2048]{1,0:T(8,128)(2,1)S(1)}, bf16[32,2048]{1,0:T(8,128)(2,1)S(1)}, u32[]{:S(2)}, u32[]{:S(2)}) collective-permute-start(bf16[32,2048]{1,0:T(8,128)(2,1)S(1)} %get-tuple-element.99.rows_ref), channel_id=1, source_target_pairs={{3,4},{4,3},{5,6},{6,5},{7,8},{8,7},{9,10},{10,9},{11,12},{12,11},... | collective-permute-start | bytes 393224 | tf_op jit(solution)/shard_map/ppermute | solution.py:376
  91.7 4.3 %collective-permute-start.16 = (bf16[32,2048]{1,0:T(8,128)(2,1)S(1)}, bf16[32,2048]{1,0:T(8,128)(2,1)S(1)}, u32[]{:S(2)}, u32[]{:S(2)}) collective-permute-start(bf16[32,2048]{1,0:T(8,128)(2,1)S(1)} %get-tuple-element.104.rows_ref), channel_id=1, source_target_pairs={{3,4},{4,3},{5,6},{6,5},{7,8},{8,7},{9,10},{10,9},{11,12},{12,11},... | collective-permute-start | bytes 393224 | tf_op jit(solution)/shard_map/ppermute | solution.py:376
  99.4 4.3 %collective-permute-start.18 = (bf16[32,2048]{1,0:T(8,128)(2,1)S(1)}, bf16[32,2048]{1,0:T(8,128)(2,1)S(1)}, u32[]{:S(2)}, u32[]{:S(2)}) collective-permute-start(bf16[32,2048]{1,0:T(8,128)(2,1)S(1)} %get-tuple-element.109.rows_ref), channel_id=1, source_target_pairs={{3,4},{4,3},{5,6},{6,5},{7,8},{8,7},{9,10},{10,9},{11,12},{12,11},... | collective-permute-start | bytes 393224 | tf_op jit(solution)/shard_map/ppermute | solution.py:376
  107.1 13.3 %all_to_all.25.parts_ref = f32[8,8,2048]{2,1,0:T(8,128)S(1)} all-to-all(f32[8,8,2048]{2,1,0:T(8,128)S(1)} %get-tuple-element.112), channel_id=1, replica_groups=mesh['depth'=8,'lat'=64] {'depth'}, dimensions={0} | all-to-all | bytes 1048576 | tf_op jit(solution)/shard_map/all_to_all | solution.py:381
  120.4 12.2 %all_to_all.26.images.refs_9_ = f32[8,8,2048]{2,1,0:T(8,128)S(1)} all-to-all(f32[8,8,2048]{2,1,0:T(8,128)S(1)} %get-tuple-element.114), channel_id=1, replica_groups=mesh['depth'=8,'lat'=64] {'depth'}, dimensions={0} | all-to-all | bytes 1048576 | tf_op jit(solution)/shard_map/all_to_all | solution.py:381
  139.7 3.1 %collective-permute-start.23 = (bf16[16,2048]{1,0:T(8,128)(2,1)S(1)}, bf16[16,2048]{1,0:T(8,128)(2,1)S(1)}, u32[]{:S(2)}, u32[]{:S(2)}) collective-permute-start(bf16[16,2048]{1,0:T(8,128)(2,1)S(1)} %get-tuple-element.119.rows_ref), channel_id=1, source_target_pairs={{3,4},{4,3},{5,6},{6,5},{7,8},{8,7},{9,10},{10,9},{11,12},{12,11},... | collective-permute-start | bytes 196616 | tf_op jit(solution)/shard_map/ppermute | solution.py:376
  146.7 3.1 %collective-permute-start.25 = (bf16[16,2048]{1,0:T(8,128)(2,1)S(1)}, bf16[16,2048]{1,0:T(8,128)(2,1)S(1)}, u32[]{:S(2)}, u32[]{:S(2)}) collective-permute-start(bf16[16,2048]{1,0:T(8,128)(2,1)S(1)} %get-tuple-element.122.rows_ref), channel_id=1, source_target_pairs={{3,4},{4,3},{5,6},{6,5},{7,8},{8,7},{9,10},{10,9},{11,12},{12,11},... | collective-permute-start | bytes 196616 | tf_op jit(solution)/shard_map/ppermute | solution.py:376
  153.7 3.1 %collective-permute-start.27 = (bf16[16,2048]{1,0:T(8,128)(2,1)S(1)}, bf16[16,2048]{1,0:T(8,128)(2,1)S(1)}, u32[]{:S(2)}, u32[]{:S(2)}) collective-permute-start(bf16[16,2048]{1,0:T(8,128)(2,1)S(1)} %get-tuple-element.125.rows_ref), channel_id=1, source_target_pairs={{3,4},{4,3},{5,6},{6,5},{7,8},{8,7},{9,10},{10,9},{11,12},{12,11},... | collective-permute-start | bytes 196616 | tf_op jit(solution)/shard_map/ppermute | solution.py:376
  160.7 3.1 %collective-permute-start.29 = (bf16[16,2048]{1,0:T(8,128)(2,1)S(1)}, bf16[16,2048]{1,0:T(8,128)(2,1)S(1)}, u32[]{:S(2)}, u32[]{:S(2)}) collective-permute-start(bf16[16,2048]{1,0:T(8,128)(2,1)S(1)} %get-tuple-element.128.rows_ref), channel_id=1, source_target_pairs={{3,4},{4,3},{5,6},{6,5},{7,8},{8,7},{9,10},{10,9},{11,12},{12,11},... | collective-permute-start | bytes 196616 | tf_op jit(solution)/shard_map/ppermute | solution.py:376
  167.7 3.1 %collective-permute-start.31 = (bf16[16,2048]{1,0:T(8,128)(2,1)S(1)}, bf16[16,2048]{1,0:T(8,128)(2,1)S(1)}, u32[]{:S(2)}, u32[]{:S(2)}) collective-permute-start(bf16[16,2048]{1,0:T(8,128)(2,1)S(1)} %get-tuple-element.131.rows_ref), channel_id=1, source_target_pairs={{3,4},{4,3},{5,6},{6,5},{7,8},{8,7},{9,10},{10,9},{11,12},{12,11},... | collective-permute-start | bytes 196616 | tf_op jit(solution)/shard_map/ppermute | solution.py:376
  174.7 3.1 %collective-permute-start.33 = (bf16[16,2048]{1,0:T(8,128)(2,1)S(1)}, bf16[16,2048]{1,0:T(8,128)(2,1)S(1)}, u32[]{:S(2)}, u32[]{:S(2)}) collective-permute-start(bf16[16,2048]{1,0:T(8,128)(2,1)S(1)} %get-tuple-element.134.rows_ref), channel_id=1, source_target_pairs={{3,4},{4,3},{5,6},{6,5},{7,8},{8,7},{9,10},{10,9},{11,12},{12,11},... | collective-permute-start | bytes 196616 | tf_op jit(solution)/shard_map/ppermute | solution.py:376
  181.7 3.1 %collective-permute-start.35 = (bf16[16,2048]{1,0:T(8,128)(2,1)S(1)}, bf16[16,2048]{1,0:T(8,128)(2,1)S(1)}, u32[]{:S(2)}, u32[]{:S(2)}) collective-permute-start(bf16[16,2048]{1,0:T(8,128)(2,1)S(1)} %get-tuple-element.137.rows_ref), channel_id=1, source_target_pairs={{3,4},{4,3},{5,6},{6,5},{7,8},{8,7},{9,10},{10,9},{11,12},{12,11},... | collective-permute-start | bytes 196616 | tf_op jit(solution)/shard_map/ppermute | solution.py:376
  189.4 4.7 %all-to-all-start.4 = ((bf16[8,16,1024]{2,1,0:T(8,128)(2,1)}), bf16[8,16,1024]{2,1,0:T(8,128)(2,1)S(1)}, u32[]{:S(2)}, u32[]{:S(2)}) async-start(bf16[8,16,1024]{2,1,0:T(8,128)(2,1)} %back.15), calls=%async_computation.4 | async-start | bytes 524288 | tf_op jit(solution)/shard_map/all_to_all | solution.py:381
  194.1 3.2 %collective-permute-start.20 = (f32[8,2048]{1,0:T(8,128)S(1)}, f32[8,2048]{1,0:T(8,128)S(1)}, u32[]{:S(2)}, u32[]{:S(2)}) collective-permute-start(f32[8,2048]{1,0:T(8,128)S(1)} %get-tuple-element.113), channel_id=1, source_target_pairs={{2,0},{3,1},{4,2},{5,3},{6,4},{7,5},{8,6},{9,7},{10,8},{11,9},{12,... | collective-permute-start | bytes 196616 | tf_op jit(solution)/shard_map/ppermute | solution.py:359
  197.3 3.2 %all-to-all-done.4.parts_ref = bf16[8,16,1024]{2,1,0:T(8,128)(2,1)S(1)} async-done(((bf16[8,16,1024]{2,1,0:T(8,128)(2,1)}), bf16[8,16,1024]{2,1,0:T(8,128)(2,1)S(1)}, u32[]{:S(2)}, u32[]{:S(2)}) %all-to-all-start.4) | async-done | bytes 262176 | tf_op jit(solution)/shard_map/all_to_all | solution.py:381
  200.5 3.4 %collective-permute-start.37 = (f32[8,2048]{1,0:T(8,128)S(1)}, f32[8,2048]{1,0:T(8,128)S(1)}, u32[]{:S(2)}, u32[]{:S(2)}) collective-permute-start(f32[8,2048]{1,0:T(8,128)S(1)} %gradient.1), channel_id=1, source_target_pairs={{2,0},{3,1},{4,2},{5,3},{6,4},{7,5},{8,6},{9,7},{10,8},{11,9},{12,... | collective-permute-start | bytes 196616 | tf_op jit(solution)/shard_map/ppermute | solution.py:359
  (128 shorter events, 83.3 us)
Async XLA Ops:
  2.6 21.4 %all-to-all-start.1 = ((bf16[8,2,3,64,128]{4,3,2,1,0:T(8,128)(2,1)}), bf16[8,2,3,64,128]{4,3,2,1,0:T(8,128)(2,1)S(1)}, u32[]{:S(2)}, u32[]{:S(2)}) async-start(bf16[8,2,3,64,128]{4,3,2,1,0:T(8,128)(2,1)} %share.1), calls=%async_computation.1 | async-start | bytes 1572864 | tf_op jit(solution)/shard_map/all_to_all | solution.py:381
  12.1 10.9 %collective-permute-start = (f32[2,8,2048]{2,1,0:T(8,128)S(1)}, f32[2,8,2048]{2,1,0:T(8,128)S(1)}, u32[]{:S(2)}, u32[]{:S(2)}) collective-permute-start(f32[2,8,2048]{2,1,0:T(8,128)S(1)} %pad_maximum_fusion), channel_id=1, source_target_pairs={{0,2},{1,3},{2,4},{3,5},{4,6},{5,7},{6,8},{7,9},{8,10},{9,11},{10,... | collective-permute-start | bytes 393224 | tf_op jit(solution)/shard_map/ppermute | solution.py:359
  24.0 19.0 %all-to-all-start = ((f32[8,2,8,2048]{3,2,1,0:T(8,128)}), f32[8,2,8,2048]{3,2,1,0:T(8,128)S(1)}, u32[]{:S(2)}, u32[]{:S(2)}) async-start(f32[8,2,8,2048]{3,2,1,0:T(8,128)} %copies.1), calls=%async_computation | async-start | bytes 2097152 | tf_op jit(solution)/shard_map/all_to_all | solution.py:381
  29.9 21.5 %collective-permute-start.1 = (bf16[8,2,3,64,128]{4,3,2,1,0:T(8,128)(2,1)S(1)}, bf16[8,2,3,64,128]{4,3,2,1,0:T(8,128)(2,1)S(1)}, u32[]{:S(2)}, u32[]{:S(2)}) collective-permute-start(bf16[8,2,3,64,128]{4,3,2,1,0:T(8,128)(2,1)S(1)} %all-to-all-done.1.own_ref), channel_id=1, source_target_pairs={{0,1},{1,0},{2,3},{3,2},{4,5},{5,4},{6,7},{7,6},{8,9},{9,8},{10,11... | collective-permute-start | bytes 2359304 | tf_op jit(solution)/shard_map/ppermute | solution.py:419
  31.9 8.5 %collective-permute-start.2 = (bf16[16,2048]{1,0:T(8,128)(2,1)S(1)}, bf16[16,2048]{1,0:T(8,128)(2,1)S(1)}, u32[]{:S(2)}, u32[]{:S(2)}) collective-permute-start(bf16[16,2048]{1,0:T(8,128)(2,1)S(1)} %dynamic-slice_bitcast_fusion.1), channel_id=1, source_target_pairs={{0,2},{1,3},{2,4},{3,5},{4,6},{5,7},{6,8},{7,9},{8,10},{9,11},{10,... | collective-permute-start | bytes 196616 | tf_op jit(solution)/shard_map/ppermute | solution.py:359
  34.6 8.4 %collective-permute-start.3 = (bf16[16,2048]{1,0:T(8,128)(2,1)S(1)}, bf16[16,2048]{1,0:T(8,128)(2,1)S(1)}, u32[]{:S(2)}, u32[]{:S(2)}) collective-permute-start(bf16[16,2048]{1,0:T(8,128)(2,1)S(1)} %dynamic-slice_bitcast_fusion), channel_id=1, source_target_pairs={{0,2},{1,3},{2,4},{3,5},{4,6},{5,7},{6,8},{7,9},{8,10},{9,11},{10,... | collective-permute-start | bytes 196616 | tf_op jit(solution)/shard_map/ppermute | solution.py:359
  43.2 8.9 %collective-permute-start.4 = (bf16[32,2048]{1,0:T(8,128)(2,1)S(1)}, bf16[32,2048]{1,0:T(8,128)(2,1)S(1)}, u32[]{:S(2)}, u32[]{:S(2)}) collective-permute-start(bf16[32,2048]{1,0:T(8,128)(2,1)S(1)} %get-tuple-element.75.rows_ref), channel_id=1, source_target_pairs={{3,4},{4,3},{5,6},{6,5},{7,8},{8,7},{9,10},{10,9},{11,12},{12,11},... | collective-permute-start | bytes 393224 | tf_op jit(solution)/shard_map/ppermute | solution.py:376
  52.9 7.5 %collective-permute-start.6 = (bf16[32,2048]{1,0:T(8,128)(2,1)S(1)}, bf16[32,2048]{1,0:T(8,128)(2,1)S(1)}, u32[]{:S(2)}, u32[]{:S(2)}) collective-permute-start(bf16[32,2048]{1,0:T(8,128)(2,1)S(1)} %get-tuple-element.79.rows_ref), channel_id=1, source_target_pairs={{3,4},{4,3},{5,6},{6,5},{7,8},{8,7},{9,10},{10,9},{11,12},{12,11},... | collective-permute-start | bytes 393224 | tf_op jit(solution)/shard_map/ppermute | solution.py:376
  60.7 7.5 %collective-permute-start.8 = (bf16[32,2048]{1,0:T(8,128)(2,1)S(1)}, bf16[32,2048]{1,0:T(8,128)(2,1)S(1)}, u32[]{:S(2)}, u32[]{:S(2)}) collective-permute-start(bf16[32,2048]{1,0:T(8,128)(2,1)S(1)} %get-tuple-element.84.rows_ref), channel_id=1, source_target_pairs={{3,4},{4,3},{5,6},{6,5},{7,8},{8,7},{9,10},{10,9},{11,12},{12,11},... | collective-permute-start | bytes 393224 | tf_op jit(solution)/shard_map/ppermute | solution.py:376
  68.4 7.5 %collective-permute-start.10 = (bf16[32,2048]{1,0:T(8,128)(2,1)S(1)}, bf16[32,2048]{1,0:T(8,128)(2,1)S(1)}, u32[]{:S(2)}, u32[]{:S(2)}) collective-permute-start(bf16[32,2048]{1,0:T(8,128)(2,1)S(1)} %get-tuple-element.89.rows_ref), channel_id=1, source_target_pairs={{3,4},{4,3},{5,6},{6,5},{7,8},{8,7},{9,10},{10,9},{11,12},{12,11},... | collective-permute-start | bytes 393224 | tf_op jit(solution)/shard_map/ppermute | solution.py:376
  76.2 7.5 %collective-permute-start.12 = (bf16[32,2048]{1,0:T(8,128)(2,1)S(1)}, bf16[32,2048]{1,0:T(8,128)(2,1)S(1)}, u32[]{:S(2)}, u32[]{:S(2)}) collective-permute-start(bf16[32,2048]{1,0:T(8,128)(2,1)S(1)} %get-tuple-element.94.rows_ref), channel_id=1, source_target_pairs={{3,4},{4,3},{5,6},{6,5},{7,8},{8,7},{9,10},{10,9},{11,12},{12,11},... | collective-permute-start | bytes 393224 | tf_op jit(solution)/shard_map/ppermute | solution.py:376
  83.9 7.5 %collective-permute-start.14 = (bf16[32,2048]{1,0:T(8,128)(2,1)S(1)}, bf16[32,2048]{1,0:T(8,128)(2,1)S(1)}, u32[]{:S(2)}, u32[]{:S(2)}) collective-permute-start(bf16[32,2048]{1,0:T(8,128)(2,1)S(1)} %get-tuple-element.99.rows_ref), channel_id=1, source_target_pairs={{3,4},{4,3},{5,6},{6,5},{7,8},{8,7},{9,10},{10,9},{11,12},{12,11},... | collective-permute-start | bytes 393224 | tf_op jit(solution)/shard_map/ppermute | solution.py:376
  91.7 7.5 %collective-permute-start.16 = (bf16[32,2048]{1,0:T(8,128)(2,1)S(1)}, bf16[32,2048]{1,0:T(8,128)(2,1)S(1)}, u32[]{:S(2)}, u32[]{:S(2)}) collective-permute-start(bf16[32,2048]{1,0:T(8,128)(2,1)S(1)} %get-tuple-element.104.rows_ref), channel_id=1, source_target_pairs={{3,4},{4,3},{5,6},{6,5},{7,8},{8,7},{9,10},{10,9},{11,12},{12,11},... | collective-permute-start | bytes 393224 | tf_op jit(solution)/shard_map/ppermute | solution.py:376
  99.4 7.5 %collective-permute-start.18 = (bf16[32,2048]{1,0:T(8,128)(2,1)S(1)}, bf16[32,2048]{1,0:T(8,128)(2,1)S(1)}, u32[]{:S(2)}, u32[]{:S(2)}) collective-permute-start(bf16[32,2048]{1,0:T(8,128)(2,1)S(1)} %get-tuple-element.109.rows_ref), channel_id=1, source_target_pairs={{3,4},{4,3},{5,6},{6,5},{7,8},{8,7},{9,10},{10,9},{11,12},{12,11},... | collective-permute-start | bytes 393224 | tf_op jit(solution)/shard_map/ppermute | solution.py:376
  132.7 6.8 %collective-permute-start.21 = (bf16[16,2048]{1,0:T(8,128)(2,1)S(1)}, bf16[16,2048]{1,0:T(8,128)(2,1)S(1)}, u32[]{:S(2)}, u32[]{:S(2)}) collective-permute-start(bf16[16,2048]{1,0:T(8,128)(2,1)S(1)} %get-tuple-element.116.rows_ref), channel_id=1, source_target_pairs={{3,4},{4,3},{5,6},{6,5},{7,8},{8,7},{9,10},{10,9},{11,12},{12,11},... | collective-permute-start | bytes 196616 | tf_op jit(solution)/shard_map/ppermute | solution.py:376
  139.7 6.8 %collective-permute-start.23 = (bf16[16,2048]{1,0:T(8,128)(2,1)S(1)}, bf16[16,2048]{1,0:T(8,128)(2,1)S(1)}, u32[]{:S(2)}, u32[]{:S(2)}) collective-permute-start(bf16[16,2048]{1,0:T(8,128)(2,1)S(1)} %get-tuple-element.119.rows_ref), channel_id=1, source_target_pairs={{3,4},{4,3},{5,6},{6,5},{7,8},{8,7},{9,10},{10,9},{11,12},{12,11},... | collective-permute-start | bytes 196616 | tf_op jit(solution)/shard_map/ppermute | solution.py:376
  146.7 6.8 %collective-permute-start.25 = (bf16[16,2048]{1,0:T(8,128)(2,1)S(1)}, bf16[16,2048]{1,0:T(8,128)(2,1)S(1)}, u32[]{:S(2)}, u32[]{:S(2)}) collective-permute-start(bf16[16,2048]{1,0:T(8,128)(2,1)S(1)} %get-tuple-element.122.rows_ref), channel_id=1, source_target_pairs={{3,4},{4,3},{5,6},{6,5},{7,8},{8,7},{9,10},{10,9},{11,12},{12,11},... | collective-permute-start | bytes 196616 | tf_op jit(solution)/shard_map/ppermute | solution.py:376
  153.7 6.8 %collective-permute-start.27 = (bf16[16,2048]{1,0:T(8,128)(2,1)S(1)}, bf16[16,2048]{1,0:T(8,128)(2,1)S(1)}, u32[]{:S(2)}, u32[]{:S(2)}) collective-permute-start(bf16[16,2048]{1,0:T(8,128)(2,1)S(1)} %get-tuple-element.125.rows_ref), channel_id=1, source_target_pairs={{3,4},{4,3},{5,6},{6,5},{7,8},{8,7},{9,10},{10,9},{11,12},{12,11},... | collective-permute-start | bytes 196616 | tf_op jit(solution)/shard_map/ppermute | solution.py:376
  160.7 6.8 %collective-permute-start.29 = (bf16[16,2048]{1,0:T(8,128)(2,1)S(1)}, bf16[16,2048]{1,0:T(8,128)(2,1)S(1)}, u32[]{:S(2)}, u32[]{:S(2)}) collective-permute-start(bf16[16,2048]{1,0:T(8,128)(2,1)S(1)} %get-tuple-element.128.rows_ref), channel_id=1, source_target_pairs={{3,4},{4,3},{5,6},{6,5},{7,8},{8,7},{9,10},{10,9},{11,12},{12,11},... | collective-permute-start | bytes 196616 | tf_op jit(solution)/shard_map/ppermute | solution.py:376
  167.7 6.8 %collective-permute-start.31 = (bf16[16,2048]{1,0:T(8,128)(2,1)S(1)}, bf16[16,2048]{1,0:T(8,128)(2,1)S(1)}, u32[]{:S(2)}, u32[]{:S(2)}) collective-permute-start(bf16[16,2048]{1,0:T(8,128)(2,1)S(1)} %get-tuple-element.131.rows_ref), channel_id=1, source_target_pairs={{3,4},{4,3},{5,6},{6,5},{7,8},{8,7},{9,10},{10,9},{11,12},{12,11},... | collective-permute-start | bytes 196616 | tf_op jit(solution)/shard_map/ppermute | solution.py:376
  174.7 6.8 %collective-permute-start.33 = (bf16[16,2048]{1,0:T(8,128)(2,1)S(1)}, bf16[16,2048]{1,0:T(8,128)(2,1)S(1)}, u32[]{:S(2)}, u32[]{:S(2)}) collective-permute-start(bf16[16,2048]{1,0:T(8,128)(2,1)S(1)} %get-tuple-element.134.rows_ref), channel_id=1, source_target_pairs={{3,4},{4,3},{5,6},{6,5},{7,8},{8,7},{9,10},{10,9},{11,12},{12,11},... | collective-permute-start | bytes 196616 | tf_op jit(solution)/shard_map/ppermute | solution.py:376
  181.7 6.8 %collective-permute-start.35 = (bf16[16,2048]{1,0:T(8,128)(2,1)S(1)}, bf16[16,2048]{1,0:T(8,128)(2,1)S(1)}, u32[]{:S(2)}, u32[]{:S(2)}) collective-permute-start(bf16[16,2048]{1,0:T(8,128)(2,1)S(1)} %get-tuple-element.137.rows_ref), channel_id=1, source_target_pairs={{3,4},{4,3},{5,6},{6,5},{7,8},{8,7},{9,10},{10,9},{11,12},{12,11},... | collective-permute-start | bytes 196616 | tf_op jit(solution)/shard_map/ppermute | solution.py:376
  189.4 11.1 %all-to-all-start.4 = ((bf16[8,16,1024]{2,1,0:T(8,128)(2,1)}), bf16[8,16,1024]{2,1,0:T(8,128)(2,1)S(1)}, u32[]{:S(2)}, u32[]{:S(2)}) async-start(bf16[8,16,1024]{2,1,0:T(8,128)(2,1)} %back.15), calls=%async_computation.4 | async-start | bytes 524288 | tf_op jit(solution)/shard_map/all_to_all | solution.py:381
  194.1 9.9 %collective-permute-start.20 = (f32[8,2048]{1,0:T(8,128)S(1)}, f32[8,2048]{1,0:T(8,128)S(1)}, u32[]{:S(2)}, u32[]{:S(2)}) collective-permute-start(f32[8,2048]{1,0:T(8,128)S(1)} %get-tuple-element.113), channel_id=1, source_target_pairs={{2,0},{3,1},{4,2},{5,3},{6,4},{7,5},{8,6},{9,7},{10,8},{11,9},{12,... | collective-permute-start | bytes 196616 | tf_op jit(solution)/shard_map/ppermute | solution.py:359
  (27 other events, 237.9 us)

commit v7 on v6

--- a/solution.py
+++ b/solution.py
@@ -232,12 +232,13 @@
             copies_ref[copy, :, cols] = image
 
 
-def gradient_kernel(parts_ref, gradient_ref):
+def gradient_kernel(parts_ref, image_ref, both_ref):
+    both_ref[0] = image_ref[...]
     halves = parts_ref.shape[2] // PAIR
     for index in range(halves):
         gradient = mean_of(parts_ref, columns(index))
-        gradient_ref[:, columns(index)] = gradient[:HALO]
-        gradient_ref[:, columns(index + halves)] = gradient[HALO:]
+        both_ref[1, :, columns(index)] = gradient[:HALO]
+        both_ref[1, :, columns(index + halves)] = gradient[HALO:]
 
 
 def scaled_rows(adjoint, coef):
@@ -328,19 +329,21 @@
     )(*placed)
 
 
-def deliver_kernel(value_ref, out_ref):
-    out_ref[0] = value_ref[...]
-
-
-def delivered(value):
+def deliver_kernel(both_ref, image_ref, gradient_ref):
+    image_ref[0] = both_ref[0]
+    gradient_ref[0] = both_ref[1]
+
+
+def delivered(both):
+    out = jax.ShapeDtypeStruct((1,) + both.shape[1:], both.dtype)
     return pl.pallas_call(
         deliver_kernel,
         name="deliver",
-        out_shape=jax.ShapeDtypeStruct((1,) + value.shape, value.dtype),
+        out_shape=(out, out),
         in_specs=[VMEM],
-        out_specs=VMEM,
+        out_specs=(VMEM, VMEM),
         compiler_params=pltpu.CompilerParams(vmem_limit_bytes=8 << 20),
-    )(pltpu.with_memory_space_constraint(value, pltpu.VMEM))
+    )(pltpu.with_memory_space_constraint(both, pltpu.VMEM))
 
 
 def frequency_of(depth, lat, sections, size):
@@ -464,7 +467,6 @@
         image_kernel, "image", [(single, F32), (stack, F32)], 1000, exchanged(products[0])
     )
     images = exchanged(images)
-    image = moved(image, False)
 
     level = levels - 1
     adjoint, scaled = call(
@@ -500,11 +502,10 @@
         terms = [term] + terms
         if not last:
             adjoint, scaled = more
-    (gradient,) = call(
-        gradient_kernel, "gradient", [(single, F32)], 1000, exchanged(terms[0])
-    )
-    gradient = moved(gradient, False)
-    return (delivered(image), delivered(gradient))
+    (both,) = call(
+        gradient_kernel, "gradient", [((2,) + single, F32)], 1000, exchanged(terms[0]), image
+    )
+    return delivered(moved(both, False))
 
 
 def solution(mesh):

time: 209 us -> 208 us (level)
  blocking collectives: 25.4 us -> 35.6 us
  starting transfers between devices: 125 us -> 117 us
    all_to_all x2 -> x3, blocking collectives: 25.4 us -> 35.6 us  [exchanged(): return lax.all_to_all(parts, 'depth', 0, 0)]
    all_to_all x3 -> x2, starting transfers between devices: 20 us -> 15.2 us  [exchanged(): return lax.all_to_all(parts, 'depth', 0, 0)]
    all_to_all x3 -> x2, waiting for transfers between devices: 3.23 us -> 0.01 us  [exchanged(): return lax.all_to_all(parts, 'depth', 0, 0)]
    ppermute x5 -> x4, starting transfers between devices: 12.3 us -> 9.16 us  [moved(): lax.ppermute(value, 'lat', route if inward else [(b, a) for a, b in route])]
    ppermute x5 -> x4, waiting for transfers between devices: 16.3 us -> 17.7 us  [moved(): lax.ppermute(value, 'lat', route if inward else [(b, a) for a, b in route])]
  transfers between devices with their start and end apart: 41 -> 39, of which waited for: 22 -> 20; matrix products, arithmetic and copies ran while one was open for 1% -> 1% of each run, Pallas kernels for 6% -> 5%
where the time goes in v7:
time: 208 us; the launch traced here: 206 us
  starting transfers between devices  117 us (56%)
  blocking collectives  35.6 us (17%)
  waiting for transfers between devices  33 us (16%)
  Pallas kernels  16 us (8%)
  local copies, waits for them, and re-layouts  2.47 us (1%)
    ppermute x32, starting transfers between devices, swapped(): received.append(lax.ppermute(rows, ('depth', 'lat'), route))  91.1 us
    all_to_all x3, blocking collectives, exchanged(): return lax.all_to_all(parts, 'depth', 0, 0)  35.6 us
    ppermute x4, waiting for transfers between devices, moved(): lax.ppermute(value, 'lat', route if inward else [(b, a) for a, b in route])  17.7 us
    ppermute x32, waiting for transfers between devices, swapped(): received.append(lax.ppermute(rows, ('depth', 'lat'), route))  15.3 us
    all_to_all x2, starting transfers between devices, exchanged(): return lax.all_to_all(parts, 'depth', 0, 0)  15.2 us
    pallas_call x38, Pallas kernels, call(): pl.pallas_call(kernel, name=name, out_shape=[pltpu.VMEM(shape, kind) for...  14.4 us
    ppermute x4, starting transfers between devices, moved(): lax.ppermute(value, 'lat', route if inward else [(b, a) for a, b in route])  9.16 us
  transfers between devices with their start and end apart: 39, of which 20 were waited for; matrix products, arithmetic and copies ran while one was open for 1% of the time, Pallas kernels for 5%

profile of v7, /device:TPU:2, one launch (start us, length us, event | category | flops | bytes accessed | tf_op | source)
XLA Modules:
  0.0 206.4 jit_solution(8008361376206534894)
XLA Ops:
  2.6 9.4 %all-to-all-start.1 = ((bf16[8,2,3,64,128]{4,3,2,1,0:T(8,128)(2,1)}), bf16[8,2,3,64,128]{4,3,2,1,0:T(8,128)(2,1)S(1)}, u32[]{:S(2)}, u32[]{:S(2)}) async-start(bf16[8,2,3,64,128]{4,3,2,1,0:T(8,128)(2,1)} %share.1), calls=%async_computation.1 | async-start | bytes 1572864 | tf_op jit(solution)/shard_map/all_to_all | solution.py:384
  14.0 9.0 %collective-permute-done.value_ref = f32[2,8,2048]{2,1,0:T(8,128)S(1)} collective-permute-done((f32[2,8,2048]{2,1,0:T(8,128)S(1)}, f32[2,8,2048]{2,1,0:T(8,128)S(1)}, u32[]{:S(2)}, u32[]{:S(2)}) %collective-permute-start) | collective-permute-done | bytes 131104 | tf_op jit(solution)/shard_map/ppermute | solution.py:362
  24.0 5.8 %all-to-all-start = ((f32[8,2,8,2048]{3,2,1,0:T(8,128)}), f32[8,2,8,2048]{3,2,1,0:T(8,128)S(1)}, u32[]{:S(2)}, u32[]{:S(2)}) async-start(f32[8,2,8,2048]{3,2,1,0:T(8,128)} %copies.1), calls=%async_computation | async-start | bytes 2097152 | tf_op jit(solution)/shard_map/all_to_all | solution.py:384
  40.3 2.8 %collective-permute-done.3.receiver_ref = bf16[16,2048]{1,0:T(8,128)(2,1)S(1)} collective-permute-done((bf16[16,2048]{1,0:T(8,128)(2,1)S(1)}, bf16[16,2048]{1,0:T(8,128)(2,1)S(1)}, u32[]{:S(2)}, u32[]{:S(2)}) %collective-permute-start.3) | collective-permute-done | bytes 65568 | tf_op jit(solution)/shard_map/ppermute | solution.py:362
  43.2 6.2 %collective-permute-start.4 = (bf16[32,2048]{1,0:T(8,128)(2,1)S(1)}, bf16[32,2048]{1,0:T(8,128)(2,1)S(1)}, u32[]{:S(2)}, u32[]{:S(2)}) collective-permute-start(bf16[32,2048]{1,0:T(8,128)(2,1)S(1)} %get-tuple-element.75.rows_ref), channel_id=1, source_target_pairs={{3,4},{4,3},{5,6},{6,5},{7,8},{8,7},{9,10},{10,9},{11,12},{12,11},... | collective-permute-start | bytes 393224 | tf_op jit(solution)/shard_map/ppermute | solution.py:379
  52.9 4.3 %collective-permute-start.6 = (bf16[32,2048]{1,0:T(8,128)(2,1)S(1)}, bf16[32,2048]{1,0:T(8,128)(2,1)S(1)}, u32[]{:S(2)}, u32[]{:S(2)}) collective-permute-start(bf16[32,2048]{1,0:T(8,128)(2,1)S(1)} %get-tuple-element.79.rows_ref), channel_id=1, source_target_pairs={{3,4},{4,3},{5,6},{6,5},{7,8},{8,7},{9,10},{10,9},{11,12},{12,11},... | collective-permute-start | bytes 393224 | tf_op jit(solution)/shard_map/ppermute | solution.py:379
  60.7 4.3 %collective-permute-start.8 = (bf16[32,2048]{1,0:T(8,128)(2,1)S(1)}, bf16[32,2048]{1,0:T(8,128)(2,1)S(1)}, u32[]{:S(2)}, u32[]{:S(2)}) collective-permute-start(bf16[32,2048]{1,0:T(8,128)(2,1)S(1)} %get-tuple-element.84.rows_ref), channel_id=1, source_target_pairs={{3,4},{4,3},{5,6},{6,5},{7,8},{8,7},{9,10},{10,9},{11,12},{12,11},... | collective-permute-start | bytes 393224 | tf_op jit(solution)/shard_map/ppermute | solution.py:379
  68.4 4.3 %collective-permute-start.10 = (bf16[32,2048]{1,0:T(8,128)(2,1)S(1)}, bf16[32,2048]{1,0:T(8,128)(2,1)S(1)}, u32[]{:S(2)}, u32[]{:S(2)}) collective-permute-start(bf16[32,2048]{1,0:T(8,128)(2,1)S(1)} %get-tuple-element.89.rows_ref), channel_id=1, source_target_pairs={{3,4},{4,3},{5,6},{6,5},{7,8},{8,7},{9,10},{10,9},{11,12},{12,11},... | collective-permute-start | bytes 393224 | tf_op jit(solution)/shard_map/ppermute | solution.py:379
  76.2 4.3 %collective-permute-start.12 = (bf16[32,2048]{1,0:T(8,128)(2,1)S(1)}, bf16[32,2048]{1,0:T(8,128)(2,1)S(1)}, u32[]{:S(2)}, u32[]{:S(2)}) collective-permute-start(bf16[32,2048]{1,0:T(8,128)(2,1)S(1)} %get-tuple-element.94.rows_ref), channel_id=1, source_target_pairs={{3,4},{4,3},{5,6},{6,5},{7,8},{8,7},{9,10},{10,9},{11,12},{12,11},... | collective-permute-start | bytes 393224 | tf_op jit(solution)/shard_map/ppermute | solution.py:379
  83.9 4.3 %collective-permute-start.14 = (bf16[32,2048]{1,0:T(8,128)(2,1)S(1)}, bf16[32,2048]{1,0:T(8,128)(2,1)S(1)}, u32[]{:S(2)}, u32[]{:S(2)}) collective-permute-start(bf16[32,2048]{1,0:T(8,128)(2,1)S(1)} %get-tuple-element.99.rows_ref), channel_id=1, source_target_pairs={{3,4},{4,3},{5,6},{6,5},{7,8},{8,7},{9,10},{10,9},{11,12},{12,11},... | collective-permute-start | bytes 393224 | tf_op jit(solution)/shard_map/ppermute | solution.py:379
  91.7 4.3 %collective-permute-start.16 = (bf16[32,2048]{1,0:T(8,128)(2,1)S(1)}, bf16[32,2048]{1,0:T(8,128)(2,1)S(1)}, u32[]{:S(2)}, u32[]{:S(2)}) collective-permute-start(bf16[32,2048]{1,0:T(8,128)(2,1)S(1)} %get-tuple-element.104.rows_ref), channel_id=1, source_target_pairs={{3,4},{4,3},{5,6},{6,5},{7,8},{8,7},{9,10},{10,9},{11,12},{12,11},... | collective-permute-start | bytes 393224 | tf_op jit(solution)/shard_map/ppermute | solution.py:379
  99.4 4.3 %collective-permute-start.18 = (bf16[32,2048]{1,0:T(8,128)(2,1)S(1)}, bf16[32,2048]{1,0:T(8,128)(2,1)S(1)}, u32[]{:S(2)}, u32[]{:S(2)}) collective-permute-start(bf16[32,2048]{1,0:T(8,128)(2,1)S(1)} %get-tuple-element.109.rows_ref), channel_id=1, source_target_pairs={{3,4},{4,3},{5,6},{6,5},{7,8},{8,7},{9,10},{10,9},{11,12},{12,11},... | collective-permute-start | bytes 393224 | tf_op jit(solution)/shard_map/ppermute | solution.py:379
  107.1 13.3 %all_to_all.25.parts_ref = f32[8,8,2048]{2,1,0:T(8,128)S(1)} all-to-all(f32[8,8,2048]{2,1,0:T(8,128)S(1)} %get-tuple-element.112), channel_id=1, replica_groups=mesh['depth'=8,'lat'=64] {'depth'}, dimensions={0} | all-to-all | bytes 1048576 | tf_op jit(solution)/shard_map/all_to_all | solution.py:384
  120.4 12.2 %all_to_all.26.images.refs_9_ = f32[8,8,2048]{2,1,0:T(8,128)S(1)} all-to-all(f32[8,8,2048]{2,1,0:T(8,128)S(1)} %get-tuple-element.113), channel_id=1, replica_groups=mesh['depth'=8,'lat'=64] {'depth'}, dimensions={0} | all-to-all | bytes 1048576 | tf_op jit(solution)/shard_map/all_to_all | solution.py:384
  139.7 3.1 %collective-permute-start.22 = (bf16[16,2048]{1,0:T(8,128)(2,1)S(1)}, bf16[16,2048]{1,0:T(8,128)(2,1)S(1)}, u32[]{:S(2)}, u32[]{:S(2)}) collective-permute-start(bf16[16,2048]{1,0:T(8,128)(2,1)S(1)} %get-tuple-element.118.rows_ref), channel_id=1, source_target_pairs={{3,4},{4,3},{5,6},{6,5},{7,8},{8,7},{9,10},{10,9},{11,12},{12,11},... | collective-permute-start | bytes 196616 | tf_op jit(solution)/shard_map/ppermute | solution.py:379
  146.7 3.1 %collective-permute-start.24 = (bf16[16,2048]{1,0:T(8,128)(2,1)S(1)}, bf16[16,2048]{1,0:T(8,128)(2,1)S(1)}, u32[]{:S(2)}, u32[]{:S(2)}) collective-permute-start(bf16[16,2048]{1,0:T(8,128)(2,1)S(1)} %get-tuple-element.121.rows_ref), channel_id=1, source_target_pairs={{3,4},{4,3},{5,6},{6,5},{7,8},{8,7},{9,10},{10,9},{11,12},{12,11},... | collective-permute-start | bytes 196616 | tf_op jit(solution)/shard_map/ppermute | solution.py:379
  153.7 3.1 %collective-permute-start.26 = (bf16[16,2048]{1,0:T(8,128)(2,1)S(1)}, bf16[16,2048]{1,0:T(8,128)(2,1)S(1)}, u32[]{:S(2)}, u32[]{:S(2)}) collective-permute-start(bf16[16,2048]{1,0:T(8,128)(2,1)S(1)} %get-tuple-element.124.rows_ref), channel_id=1, source_target_pairs={{3,4},{4,3},{5,6},{6,5},{7,8},{8,7},{9,10},{10,9},{11,12},{12,11},... | collective-permute-start | bytes 196616 | tf_op jit(solution)/shard_map/ppermute | solution.py:379
  160.7 3.1 %collective-permute-start.28 = (bf16[16,2048]{1,0:T(8,128)(2,1)S(1)}, bf16[16,2048]{1,0:T(8,128)(2,1)S(1)}, u32[]{:S(2)}, u32[]{:S(2)}) collective-permute-start(bf16[16,2048]{1,0:T(8,128)(2,1)S(1)} %get-tuple-element.127.rows_ref), channel_id=1, source_target_pairs={{3,4},{4,3},{5,6},{6,5},{7,8},{8,7},{9,10},{10,9},{11,12},{12,11},... | collective-permute-start | bytes 196616 | tf_op jit(solution)/shard_map/ppermute | solution.py:379
  167.7 3.1 %collective-permute-start.30 = (bf16[16,2048]{1,0:T(8,128)(2,1)S(1)}, bf16[16,2048]{1,0:T(8,128)(2,1)S(1)}, u32[]{:S(2)}, u32[]{:S(2)}) collective-permute-start(bf16[16,2048]{1,0:T(8,128)(2,1)S(1)} %get-tuple-element.130.rows_ref), channel_id=1, source_target_pairs={{3,4},{4,3},{5,6},{6,5},{7,8},{8,7},{9,10},{10,9},{11,12},{12,11},... | collective-permute-start | bytes 196616 | tf_op jit(solution)/shard_map/ppermute | solution.py:379
  174.7 3.1 %collective-permute-start.32 = (bf16[16,2048]{1,0:T(8,128)(2,1)S(1)}, bf16[16,2048]{1,0:T(8,128)(2,1)S(1)}, u32[]{:S(2)}, u32[]{:S(2)}) collective-permute-start(bf16[16,2048]{1,0:T(8,128)(2,1)S(1)} %get-tuple-element.133.rows_ref), channel_id=1, source_target_pairs={{3,4},{4,3},{5,6},{6,5},{7,8},{8,7},{9,10},{10,9},{11,12},{12,11},... | collective-permute-start | bytes 196616 | tf_op jit(solution)/shard_map/ppermute | solution.py:379
  181.7 3.1 %collective-permute-start.34 = (bf16[16,2048]{1,0:T(8,128)(2,1)S(1)}, bf16[16,2048]{1,0:T(8,128)(2,1)S(1)}, u32[]{:S(2)}, u32[]{:S(2)}) collective-permute-start(bf16[16,2048]{1,0:T(8,128)(2,1)S(1)} %get-tuple-element.136.rows_ref), channel_id=1, source_target_pairs={{3,4},{4,3},{5,6},{6,5},{7,8},{8,7},{9,10},{10,9},{11,12},{12,11},... | collective-permute-start | bytes 196616 | tf_op jit(solution)/shard_map/ppermute | solution.py:379
  188.6 10.2 %all_to_all.27.parts_ref = bf16[8,16,1024]{2,1,0:T(8,128)(2,1)S(1)} all-to-all(bf16[8,16,1024]{2,1,0:T(8,128)(2,1)S(1)} %back.15), channel_id=1, replica_groups=mesh['depth'=8,'lat'=64] {'depth'}, dimensions={0} | all-to-all | bytes 524288 | tf_op jit(solution)/shard_map/all_to_all | solution.py:384
  198.9 3.4 %collective-permute-start.36 = (f32[2,8,2048]{2,1,0:T(8,128)S(1)}, f32[2,8,2048]{2,1,0:T(8,128)S(1)}, u32[]{:S(2)}, u32[]{:S(2)}) collective-permute-start(f32[2,8,2048]{2,1,0:T(8,128)S(1)} %gradient.1), channel_id=1, source_target_pairs={{2,0},{3,1},{4,2},{5,3},{6,4},{7,5},{8,6},{9,7},{10,8},{11,9},{12,... | collective-permute-start | bytes 393224 | tf_op jit(solution)/shard_map/ppermute | solution.py:362
  202.3 3.4 %collective-permute-done.36.both_ref = f32[2,8,2048]{2,1,0:T(8,128)S(1)} collective-permute-done((f32[2,8,2048]{2,1,0:T(8,128)S(1)}, f32[2,8,2048]{2,1,0:T(8,128)S(1)}, u32[]{:S(2)}, u32[]{:S(2)}) %collective-permute-start.36) | collective-permute-done | bytes 131104 | tf_op jit(solution)/shard_map/ppermute | solution.py:362
  (124 shorter events, 77.1 us)
Async XLA Ops:
  2.6 21.4 %all-to-all-start.1 = ((bf16[8,2,3,64,128]{4,3,2,1,0:T(8,128)(2,1)}), bf16[8,2,3,64,128]{4,3,2,1,0:T(8,128)(2,1)S(1)}, u32[]{:S(2)}, u32[]{:S(2)}) async-start(bf16[8,2,3,64,128]{4,3,2,1,0:T(8,128)(2,1)} %share.1), calls=%async_computation.1 | async-start | bytes 1572864 | tf_op jit(solution)/shard_map/all_to_all | solution.py:384
  12.1 10.9 %collective-permute-start = (f32[2,8,2048]{2,1,0:T(8,128)S(1)}, f32[2,8,2048]{2,1,0:T(8,128)S(1)}, u32[]{:S(2)}, u32[]{:S(2)}) collective-permute-start(f32[2,8,2048]{2,1,0:T(8,128)S(1)} %pad_maximum_fusion), channel_id=1, source_target_pairs={{0,2},{1,3},{2,4},{3,5},{4,6},{5,7},{6,8},{7,9},{8,10},{9,11},{10,... | collective-permute-start | bytes 393224 | tf_op jit(solution)/shard_map/ppermute | solution.py:362
  24.0 19.0 %all-to-all-start = ((f32[8,2,8,2048]{3,2,1,0:T(8,128)}), f32[8,2,8,2048]{3,2,1,0:T(8,128)S(1)}, u32[]{:S(2)}, u32[]{:S(2)}) async-start(f32[8,2,8,2048]{3,2,1,0:T(8,128)} %copies.1), calls=%async_computation | async-start | bytes 2097152 | tf_op jit(solution)/shard_map/all_to_all | solution.py:384
  29.9 21.5 %collective-permute-start.1 = (bf16[8,2,3,64,128]{4,3,2,1,0:T(8,128)(2,1)S(1)}, bf16[8,2,3,64,128]{4,3,2,1,0:T(8,128)(2,1)S(1)}, u32[]{:S(2)}, u32[]{:S(2)}) collective-permute-start(bf16[8,2,3,64,128]{4,3,2,1,0:T(8,128)(2,1)S(1)} %all-to-all-done.1.own_ref), channel_id=1, source_target_pairs={{0,1},{1,0},{2,3},{3,2},{4,5},{5,4},{6,7},{7,6},{8,9},{9,8},{10,11... | collective-permute-start | bytes 2359304 | tf_op jit(solution)/shard_map/ppermute | solution.py:422
  31.8 8.5 %collective-permute-start.2 = (bf16[16,2048]{1,0:T(8,128)(2,1)S(1)}, bf16[16,2048]{1,0:T(8,128)(2,1)S(1)}, u32[]{:S(2)}, u32[]{:S(2)}) collective-permute-start(bf16[16,2048]{1,0:T(8,128)(2,1)S(1)} %dynamic-slice_bitcast_fusion.1), channel_id=1, source_target_pairs={{0,2},{1,3},{2,4},{3,5},{4,6},{5,7},{6,8},{7,9},{8,10},{9,11},{10,... | collective-permute-start | bytes 196616 | tf_op jit(solution)/shard_map/ppermute | solution.py:362
  34.6 8.4 %collective-permute-start.3 = (bf16[16,2048]{1,0:T(8,128)(2,1)S(1)}, bf16[16,2048]{1,0:T(8,128)(2,1)S(1)}, u32[]{:S(2)}, u32[]{:S(2)}) collective-permute-start(bf16[16,2048]{1,0:T(8,128)(2,1)S(1)} %dynamic-slice_bitcast_fusion), channel_id=1, source_target_pairs={{0,2},{1,3},{2,4},{3,5},{4,6},{5,7},{6,8},{7,9},{8,10},{9,11},{10,... | collective-permute-start | bytes 196616 | tf_op jit(solution)/shard_map/ppermute | solution.py:362
  43.2 8.9 %collective-permute-start.4 = (bf16[32,2048]{1,0:T(8,128)(2,1)S(1)}, bf16[32,2048]{1,0:T(8,128)(2,1)S(1)}, u32[]{:S(2)}, u32[]{:S(2)}) collective-permute-start(bf16[32,2048]{1,0:T(8,128)(2,1)S(1)} %get-tuple-element.75.rows_ref), channel_id=1, source_target_pairs={{3,4},{4,3},{5,6},{6,5},{7,8},{8,7},{9,10},{10,9},{11,12},{12,11},... | collective-permute-start | bytes 393224 | tf_op jit(solution)/shard_map/ppermute | solution.py:379
  52.9 7.5 %collective-permute-start.6 = (bf16[32,2048]{1,0:T(8,128)(2,1)S(1)}, bf16[32,2048]{1,0:T(8,128)(2,1)S(1)}, u32[]{:S(2)}, u32[]{:S(2)}) collective-permute-start(bf16[32,2048]{1,0:T(8,128)(2,1)S(1)} %get-tuple-element.79.rows_ref), channel_id=1, source_target_pairs={{3,4},{4,3},{5,6},{6,5},{7,8},{8,7},{9,10},{10,9},{11,12},{12,11},... | collective-permute-start | bytes 393224 | tf_op jit(solution)/shard_map/ppermute | solution.py:379
  60.7 7.5 %collective-permute-start.8 = (bf16[32,2048]{1,0:T(8,128)(2,1)S(1)}, bf16[32,2048]{1,0:T(8,128)(2,1)S(1)}, u32[]{:S(2)}, u32[]{:S(2)}) collective-permute-start(bf16[32,2048]{1,0:T(8,128)(2,1)S(1)} %get-tuple-element.84.rows_ref), channel_id=1, source_target_pairs={{3,4},{4,3},{5,6},{6,5},{7,8},{8,7},{9,10},{10,9},{11,12},{12,11},... | collective-permute-start | bytes 393224 | tf_op jit(solution)/shard_map/ppermute | solution.py:379
  68.4 7.5 %collective-permute-start.10 = (bf16[32,2048]{1,0:T(8,128)(2,1)S(1)}, bf16[32,2048]{1,0:T(8,128)(2,1)S(1)}, u32[]{:S(2)}, u32[]{:S(2)}) collective-permute-start(bf16[32,2048]{1,0:T(8,128)(2,1)S(1)} %get-tuple-element.89.rows_ref), channel_id=1, source_target_pairs={{3,4},{4,3},{5,6},{6,5},{7,8},{8,7},{9,10},{10,9},{11,12},{12,11},... | collective-permute-start | bytes 393224 | tf_op jit(solution)/shard_map/ppermute | solution.py:379
  76.2 7.5 %collective-permute-start.12 = (bf16[32,2048]{1,0:T(8,128)(2,1)S(1)}, bf16[32,2048]{1,0:T(8,128)(2,1)S(1)}, u32[]{:S(2)}, u32[]{:S(2)}) collective-permute-start(bf16[32,2048]{1,0:T(8,128)(2,1)S(1)} %get-tuple-element.94.rows_ref), channel_id=1, source_target_pairs={{3,4},{4,3},{5,6},{6,5},{7,8},{8,7},{9,10},{10,9},{11,12},{12,11},... | collective-permute-start | bytes 393224 | tf_op jit(solution)/shard_map/ppermute | solution.py:379
  83.9 7.5 %collective-permute-start.14 = (bf16[32,2048]{1,0:T(8,128)(2,1)S(1)}, bf16[32,2048]{1,0:T(8,128)(2,1)S(1)}, u32[]{:S(2)}, u32[]{:S(2)}) collective-permute-start(bf16[32,2048]{1,0:T(8,128)(2,1)S(1)} %get-tuple-element.99.rows_ref), channel_id=1, source_target_pairs={{3,4},{4,3},{5,6},{6,5},{7,8},{8,7},{9,10},{10,9},{11,12},{12,11},... | collective-permute-start | bytes 393224 | tf_op jit(solution)/shard_map/ppermute | solution.py:379
  91.7 7.5 %collective-permute-start.16 = (bf16[32,2048]{1,0:T(8,128)(2,1)S(1)}, bf16[32,2048]{1,0:T(8,128)(2,1)S(1)}, u32[]{:S(2)}, u32[]{:S(2)}) collective-permute-start(bf16[32,2048]{1,0:T(8,128)(2,1)S(1)} %get-tuple-element.104.rows_ref), channel_id=1, source_target_pairs={{3,4},{4,3},{5,6},{6,5},{7,8},{8,7},{9,10},{10,9},{11,12},{12,11},... | collective-permute-start | bytes 393224 | tf_op jit(solution)/shard_map/ppermute | solution.py:379
  99.4 7.5 %collective-permute-start.18 = (bf16[32,2048]{1,0:T(8,128)(2,1)S(1)}, bf16[32,2048]{1,0:T(8,128)(2,1)S(1)}, u32[]{:S(2)}, u32[]{:S(2)}) collective-permute-start(bf16[32,2048]{1,0:T(8,128)(2,1)S(1)} %get-tuple-element.109.rows_ref), channel_id=1, source_target_pairs={{3,4},{4,3},{5,6},{6,5},{7,8},{8,7},{9,10},{10,9},{11,12},{12,11},... | collective-permute-start | bytes 393224 | tf_op jit(solution)/shard_map/ppermute | solution.py:379
  132.7 6.8 %collective-permute-start.20 = (bf16[16,2048]{1,0:T(8,128)(2,1)S(1)}, bf16[16,2048]{1,0:T(8,128)(2,1)S(1)}, u32[]{:S(2)}, u32[]{:S(2)}) collective-permute-start(bf16[16,2048]{1,0:T(8,128)(2,1)S(1)} %get-tuple-element.115.rows_ref), channel_id=1, source_target_pairs={{3,4},{4,3},{5,6},{6,5},{7,8},{8,7},{9,10},{10,9},{11,12},{12,11},... | collective-permute-start | bytes 196616 | tf_op jit(solution)/shard_map/ppermute | solution.py:379
  135.1 4.3 %collective-permute-start.21 = (bf16[16,2048]{1,0:T(8,128)(2,1)S(1)}, bf16[16,2048]{1,0:T(8,128)(2,1)S(1)}, u32[]{:S(2)}, u32[]{:S(2)}) collective-permute-start(bf16[16,2048]{1,0:T(8,128)(2,1)S(1)} %get-tuple-element.115.rows_ref), channel_id=1, source_target_pairs={{2,3},{3,2},{4,5},{5,4},{6,7},{7,6},{8,9},{9,8},{10,11},{11,10},{1... | collective-permute-start | bytes 196616 | tf_op jit(solution)/shard_map/ppermute | solution.py:379
  139.7 6.8 %collective-permute-start.22 = (bf16[16,2048]{1,0:T(8,128)(2,1)S(1)}, bf16[16,2048]{1,0:T(8,128)(2,1)S(1)}, u32[]{:S(2)}, u32[]{:S(2)}) collective-permute-start(bf16[16,2048]{1,0:T(8,128)(2,1)S(1)} %get-tuple-element.118.rows_ref), channel_id=1, source_target_pairs={{3,4},{4,3},{5,6},{6,5},{7,8},{8,7},{9,10},{10,9},{11,12},{12,11},... | collective-permute-start | bytes 196616 | tf_op jit(solution)/shard_map/ppermute | solution.py:379
  146.7 6.8 %collective-permute-start.24 = (bf16[16,2048]{1,0:T(8,128)(2,1)S(1)}, bf16[16,2048]{1,0:T(8,128)(2,1)S(1)}, u32[]{:S(2)}, u32[]{:S(2)}) collective-permute-start(bf16[16,2048]{1,0:T(8,128)(2,1)S(1)} %get-tuple-element.121.rows_ref), channel_id=1, source_target_pairs={{3,4},{4,3},{5,6},{6,5},{7,8},{8,7},{9,10},{10,9},{11,12},{12,11},... | collective-permute-start | bytes 196616 | tf_op jit(solution)/shard_map/ppermute | solution.py:379
  153.7 6.8 %collective-permute-start.26 = (bf16[16,2048]{1,0:T(8,128)(2,1)S(1)}, bf16[16,2048]{1,0:T(8,128)(2,1)S(1)}, u32[]{:S(2)}, u32[]{:S(2)}) collective-permute-start(bf16[16,2048]{1,0:T(8,128)(2,1)S(1)} %get-tuple-element.124.rows_ref), channel_id=1, source_target_pairs={{3,4},{4,3},{5,6},{6,5},{7,8},{8,7},{9,10},{10,9},{11,12},{12,11},... | collective-permute-start | bytes 196616 | tf_op jit(solution)/shard_map/ppermute | solution.py:379
  160.7 6.8 %collective-permute-start.28 = (bf16[16,2048]{1,0:T(8,128)(2,1)S(1)}, bf16[16,2048]{1,0:T(8,128)(2,1)S(1)}, u32[]{:S(2)}, u32[]{:S(2)}) collective-permute-start(bf16[16,2048]{1,0:T(8,128)(2,1)S(1)} %get-tuple-element.127.rows_ref), channel_id=1, source_target_pairs={{3,4},{4,3},{5,6},{6,5},{7,8},{8,7},{9,10},{10,9},{11,12},{12,11},... | collective-permute-start | bytes 196616 | tf_op jit(solution)/shard_map/ppermute | solution.py:379
  167.7 6.8 %collective-permute-start.30 = (bf16[16,2048]{1,0:T(8,128)(2,1)S(1)}, bf16[16,2048]{1,0:T(8,128)(2,1)S(1)}, u32[]{:S(2)}, u32[]{:S(2)}) collective-permute-start(bf16[16,2048]{1,0:T(8,128)(2,1)S(1)} %get-tuple-element.130.rows_ref), channel_id=1, source_target_pairs={{3,4},{4,3},{5,6},{6,5},{7,8},{8,7},{9,10},{10,9},{11,12},{12,11},... | collective-permute-start | bytes 196616 | tf_op jit(solution)/shard_map/ppermute | solution.py:379
  174.7 6.8 %collective-permute-start.32 = (bf16[16,2048]{1,0:T(8,128)(2,1)S(1)}, bf16[16,2048]{1,0:T(8,128)(2,1)S(1)}, u32[]{:S(2)}, u32[]{:S(2)}) collective-permute-start(bf16[16,2048]{1,0:T(8,128)(2,1)S(1)} %get-tuple-element.133.rows_ref), channel_id=1, source_target_pairs={{3,4},{4,3},{5,6},{6,5},{7,8},{8,7},{9,10},{10,9},{11,12},{12,11},... | collective-permute-start | bytes 196616 | tf_op jit(solution)/shard_map/ppermute | solution.py:379
  181.7 6.8 %collective-permute-start.34 = (bf16[16,2048]{1,0:T(8,128)(2,1)S(1)}, bf16[16,2048]{1,0:T(8,128)(2,1)S(1)}, u32[]{:S(2)}, u32[]{:S(2)}) collective-permute-start(bf16[16,2048]{1,0:T(8,128)(2,1)S(1)} %get-tuple-element.136.rows_ref), channel_id=1, source_target_pairs={{3,4},{4,3},{5,6},{6,5},{7,8},{8,7},{9,10},{10,9},{11,12},{12,11},... | collective-permute-start | bytes 196616 | tf_op jit(solution)/shard_map/ppermute | solution.py:379
  198.9 6.9 %collective-permute-start.36 = (f32[2,8,2048]{2,1,0:T(8,128)S(1)}, f32[2,8,2048]{2,1,0:T(8,128)S(1)}, u32[]{:S(2)}, u32[]{:S(2)}) collective-permute-start(f32[2,8,2048]{2,1,0:T(8,128)S(1)} %gradient.1), channel_id=1, source_target_pairs={{2,0},{3,1},{4,2},{5,3},{6,4},{7,5},{8,6},{9,7},{10,8},{11,9},{12,... | collective-permute-start | bytes 393224 | tf_op jit(solution)/shard_map/ppermute | solution.py:362
  (25 other events, 227.4 us)

commit v8 on v7

--- a/solution.py
+++ b/solution.py
@@ -115,9 +115,13 @@
     out_ref[1 - half] = other_ref[...]
 
 
-def copies_kernel(value_ref, out_ref):
+def copies_kernel(value_ref, out_ref, semaphores):
+    copies = []
     for copy in range(out_ref.shape[0]):
-        out_ref[copy] = value_ref[...]
+        copies.append(pltpu.make_async_copy(value_ref, out_ref.at[copy], semaphores.at[copy]))
+        copies[-1].start()
+    for copy in copies:
+        copy.wait()
 
 
 def coef_of(params, level, cols):
@@ -415,7 +419,15 @@
         compiler_params=pltpu.CompilerParams(vmem_limit_bytes=8 << 20),
     )(half_index, pltpu.with_memory_space_constraint(band, pltpu.VMEM))
     pieces = exchanged(pieces)
-    (params,) = call(copies_kernel, "copies", [((sections, 2) + single, F32)], 1000, own)
+    params = pl.pallas_call(
+        copies_kernel,
+        name="copies",
+        out_shape=jax.ShapeDtypeStruct((sections,) + own.shape, F32),
+        in_specs=[VMEM],
+        out_specs=pl.BlockSpec(memory_space=pl.ANY),
+        scratch_shapes=[pltpu.SemaphoreType.DMA((sections,))],
+        compiler_params=pltpu.CompilerParams(vmem_limit_bytes=8 << 20),
+    )(pltpu.with_memory_space_constraint(own, pltpu.VMEM))
     pieces, _ = lax.optimization_barrier((pieces, params))
     params = exchanged(params)
     route = [(lat, lat + 1 - lat % 2 * 2) for lat in range(size)]

time: 208 us -> 208 us (level)
    pallas_call x38 -> x37, Pallas kernels: 14.4 us -> 13.3 us  [call(): pl.pallas_call(kernel, name=name, out_shape=[pltpu.VMEM(shape, kind) for...]
where the time goes in v8:
time: 208 us; the launch traced here: 206 us
  starting transfers between devices  117 us (56%)
  blocking collectives  35.6 us (17%)
  waiting for transfers between devices  33 us (16%)
  Pallas kernels  16 us (8%)
  local copies, waits for them, and re-layouts  2.47 us (1%)
    ppermute x32, starting transfers between devices, swapped(): received.append(lax.ppermute(rows, ('depth', 'lat'), route))  91.1 us
    all_to_all x3, blocking collectives, exchanged(): return lax.all_to_all(parts, 'depth', 0, 0)  35.6 us
    ppermute x4, waiting for transfers between devices, moved(): lax.ppermute(value, 'lat', route if inward else [(b, a) for a, b in route])  17.8 us
    ppermute x32, waiting for transfers between devices, swapped(): received.append(lax.ppermute(rows, ('depth', 'lat'), route))  15.3 us
    all_to_all x2, starting transfers between devices, exchanged(): return lax.all_to_all(parts, 'depth', 0, 0)  15.1 us
    pallas_call x37, Pallas kernels, call(): pl.pallas_call(kernel, name=name, out_shape=[pltpu.VMEM(shape, kind) for...  13.3 us
    ppermute x4, starting transfers between devices, moved(): lax.ppermute(value, 'lat', route if inward else [(b, a) for a, b in route])  9.16 us
  transfers between devices with their start and end apart: 39, of which 20 were waited for; matrix products, arithmetic and copies ran while one was open for 1% of the time, Pallas kernels for 5%

profile of v8, /device:TPU:2, one launch (start us, length us, event | category | flops | bytes accessed | tf_op | source)
XLA Modules:
  0.0 206.4 jit_solution(13918311617105387205)
XLA Ops:
  2.6 9.4 %all-to-all-start.1 = ((bf16[8,2,3,64,128]{4,3,2,1,0:T(8,128)(2,1)}), bf16[8,2,3,64,128]{4,3,2,1,0:T(8,128)(2,1)S(1)}, u32[]{:S(2)}, u32[]{:S(2)}) async-start(bf16[8,2,3,64,128]{4,3,2,1,0:T(8,128)(2,1)} %share.1), calls=%async_computation.1 | async-start | bytes 1572864 | tf_op jit(solution)/shard_map/all_to_all | solution.py:388
  14.0 9.0 %collective-permute-done.value_ref = f32[2,8,2048]{2,1,0:T(8,128)S(1)} collective-permute-done((f32[2,8,2048]{2,1,0:T(8,128)S(1)}, f32[2,8,2048]{2,1,0:T(8,128)S(1)}, u32[]{:S(2)}, u32[]{:S(2)}) %collective-permute-start) | collective-permute-done | bytes 131104 | tf_op jit(solution)/shard_map/ppermute | solution.py:366
  24.1 5.7 %all-to-all-start = ((f32[8,2,8,2048]{3,2,1,0:T(8,128)}), f32[8,2,8,2048]{3,2,1,0:T(8,128)S(1)}, u32[]{:S(2)}, u32[]{:S(2)}) async-start(f32[8,2,8,2048]{3,2,1,0:T(8,128)} %copies.1), calls=%async_computation | async-start | bytes 2097152 | tf_op jit(solution)/shard_map/all_to_all | solution.py:388
  40.3 2.8 %collective-permute-done.3.receiver_ref = bf16[16,2048]{1,0:T(8,128)(2,1)S(1)} collective-permute-done((bf16[16,2048]{1,0:T(8,128)(2,1)S(1)}, bf16[16,2048]{1,0:T(8,128)(2,1)S(1)}, u32[]{:S(2)}, u32[]{:S(2)}) %collective-permute-start.3) | collective-permute-done | bytes 65568 | tf_op jit(solution)/shard_map/ppermute | solution.py:366
  43.2 6.2 %collective-permute-start.4 = (bf16[32,2048]{1,0:T(8,128)(2,1)S(1)}, bf16[32,2048]{1,0:T(8,128)(2,1)S(1)}, u32[]{:S(2)}, u32[]{:S(2)}) collective-permute-start(bf16[32,2048]{1,0:T(8,128)(2,1)S(1)} %get-tuple-element.75.rows_ref), channel_id=1, source_target_pairs={{3,4},{4,3},{5,6},{6,5},{7,8},{8,7},{9,10},{10,9},{11,12},{12,11},... | collective-permute-start | bytes 393224 | tf_op jit(solution)/shard_map/ppermute | solution.py:383
  52.9 4.3 %collective-permute-start.6 = (bf16[32,2048]{1,0:T(8,128)(2,1)S(1)}, bf16[32,2048]{1,0:T(8,128)(2,1)S(1)}, u32[]{:S(2)}, u32[]{:S(2)}) collective-permute-start(bf16[32,2048]{1,0:T(8,128)(2,1)S(1)} %get-tuple-element.79.rows_ref), channel_id=1, source_target_pairs={{3,4},{4,3},{5,6},{6,5},{7,8},{8,7},{9,10},{10,9},{11,12},{12,11},... | collective-permute-start | bytes 393224 | tf_op jit(solution)/shard_map/ppermute | solution.py:383
  60.7 4.3 %collective-permute-start.8 = (bf16[32,2048]{1,0:T(8,128)(2,1)S(1)}, bf16[32,2048]{1,0:T(8,128)(2,1)S(1)}, u32[]{:S(2)}, u32[]{:S(2)}) collective-permute-start(bf16[32,2048]{1,0:T(8,128)(2,1)S(1)} %get-tuple-element.84.rows_ref), channel_id=1, source_target_pairs={{3,4},{4,3},{5,6},{6,5},{7,8},{8,7},{9,10},{10,9},{11,12},{12,11},... | collective-permute-start | bytes 393224 | tf_op jit(solution)/shard_map/ppermute | solution.py:383
  68.4 4.3 %collective-permute-start.10 = (bf16[32,2048]{1,0:T(8,128)(2,1)S(1)}, bf16[32,2048]{1,0:T(8,128)(2,1)S(1)}, u32[]{:S(2)}, u32[]{:S(2)}) collective-permute-start(bf16[32,2048]{1,0:T(8,128)(2,1)S(1)} %get-tuple-element.89.rows_ref), channel_id=1, source_target_pairs={{3,4},{4,3},{5,6},{6,5},{7,8},{8,7},{9,10},{10,9},{11,12},{12,11},... | collective-permute-start | bytes 393224 | tf_op jit(solution)/shard_map/ppermute | solution.py:383
  76.2 4.3 %collective-permute-start.12 = (bf16[32,2048]{1,0:T(8,128)(2,1)S(1)}, bf16[32,2048]{1,0:T(8,128)(2,1)S(1)}, u32[]{:S(2)}, u32[]{:S(2)}) collective-permute-start(bf16[32,2048]{1,0:T(8,128)(2,1)S(1)} %get-tuple-element.94.rows_ref), channel_id=1, source_target_pairs={{3,4},{4,3},{5,6},{6,5},{7,8},{8,7},{9,10},{10,9},{11,12},{12,11},... | collective-permute-start | bytes 393224 | tf_op jit(solution)/shard_map/ppermute | solution.py:383
  83.9 4.3 %collective-permute-start.14 = (bf16[32,2048]{1,0:T(8,128)(2,1)S(1)}, bf16[32,2048]{1,0:T(8,128)(2,1)S(1)}, u32[]{:S(2)}, u32[]{:S(2)}) collective-permute-start(bf16[32,2048]{1,0:T(8,128)(2,1)S(1)} %get-tuple-element.99.rows_ref), channel_id=1, source_target_pairs={{3,4},{4,3},{5,6},{6,5},{7,8},{8,7},{9,10},{10,9},{11,12},{12,11},... | collective-permute-start | bytes 393224 | tf_op jit(solution)/shard_map/ppermute | solution.py:383
  91.7 4.3 %collective-permute-start.16 = (bf16[32,2048]{1,0:T(8,128)(2,1)S(1)}, bf16[32,2048]{1,0:T(8,128)(2,1)S(1)}, u32[]{:S(2)}, u32[]{:S(2)}) collective-permute-start(bf16[32,2048]{1,0:T(8,128)(2,1)S(1)} %get-tuple-element.104.rows_ref), channel_id=1, source_target_pairs={{3,4},{4,3},{5,6},{6,5},{7,8},{8,7},{9,10},{10,9},{11,12},{12,11},... | collective-permute-start | bytes 393224 | tf_op jit(solution)/shard_map/ppermute | solution.py:383
  99.4 4.3 %collective-permute-start.18 = (bf16[32,2048]{1,0:T(8,128)(2,1)S(1)}, bf16[32,2048]{1,0:T(8,128)(2,1)S(1)}, u32[]{:S(2)}, u32[]{:S(2)}) collective-permute-start(bf16[32,2048]{1,0:T(8,128)(2,1)S(1)} %get-tuple-element.109.rows_ref), channel_id=1, source_target_pairs={{3,4},{4,3},{5,6},{6,5},{7,8},{8,7},{9,10},{10,9},{11,12},{12,11},... | collective-permute-start | bytes 393224 | tf_op jit(solution)/shard_map/ppermute | solution.py:383
  107.1 13.3 %all_to_all.25.parts_ref = f32[8,8,2048]{2,1,0:T(8,128)S(1)} all-to-all(f32[8,8,2048]{2,1,0:T(8,128)S(1)} %get-tuple-element.112), channel_id=1, replica_groups=mesh['depth'=8,'lat'=64] {'depth'}, dimensions={0} | all-to-all | bytes 1048576 | tf_op jit(solution)/shard_map/all_to_all | solution.py:388
  120.4 12.2 %all_to_all.26.images.refs_9_ = f32[8,8,2048]{2,1,0:T(8,128)S(1)} all-to-all(f32[8,8,2048]{2,1,0:T(8,128)S(1)} %get-tuple-element.113), channel_id=1, replica_groups=mesh['depth'=8,'lat'=64] {'depth'}, dimensions={0} | all-to-all | bytes 1048576 | tf_op jit(solution)/shard_map/all_to_all | solution.py:388
  139.7 3.1 %collective-permute-start.22 = (bf16[16,2048]{1,0:T(8,128)(2,1)S(1)}, bf16[16,2048]{1,0:T(8,128)(2,1)S(1)}, u32[]{:S(2)}, u32[]{:S(2)}) collective-permute-start(bf16[16,2048]{1,0:T(8,128)(2,1)S(1)} %get-tuple-element.118.rows_ref), channel_id=1, source_target_pairs={{3,4},{4,3},{5,6},{6,5},{7,8},{8,7},{9,10},{10,9},{11,12},{12,11},... | collective-permute-start | bytes 196616 | tf_op jit(solution)/shard_map/ppermute | solution.py:383
  146.7 3.1 %collective-permute-start.24 = (bf16[16,2048]{1,0:T(8,128)(2,1)S(1)}, bf16[16,2048]{1,0:T(8,128)(2,1)S(1)}, u32[]{:S(2)}, u32[]{:S(2)}) collective-permute-start(bf16[16,2048]{1,0:T(8,128)(2,1)S(1)} %get-tuple-element.121.rows_ref), channel_id=1, source_target_pairs={{3,4},{4,3},{5,6},{6,5},{7,8},{8,7},{9,10},{10,9},{11,12},{12,11},... | collective-permute-start | bytes 196616 | tf_op jit(solution)/shard_map/ppermute | solution.py:383
  153.7 3.1 %collective-permute-start.26 = (bf16[16,2048]{1,0:T(8,128)(2,1)S(1)}, bf16[16,2048]{1,0:T(8,128)(2,1)S(1)}, u32[]{:S(2)}, u32[]{:S(2)}) collective-permute-start(bf16[16,2048]{1,0:T(8,128)(2,1)S(1)} %get-tuple-element.124.rows_ref), channel_id=1, source_target_pairs={{3,4},{4,3},{5,6},{6,5},{7,8},{8,7},{9,10},{10,9},{11,12},{12,11},... | collective-permute-start | bytes 196616 | tf_op jit(solution)/shard_map/ppermute | solution.py:383
  160.7 3.1 %collective-permute-start.28 = (bf16[16,2048]{1,0:T(8,128)(2,1)S(1)}, bf16[16,2048]{1,0:T(8,128)(2,1)S(1)}, u32[]{:S(2)}, u32[]{:S(2)}) collective-permute-start(bf16[16,2048]{1,0:T(8,128)(2,1)S(1)} %get-tuple-element.127.rows_ref), channel_id=1, source_target_pairs={{3,4},{4,3},{5,6},{6,5},{7,8},{8,7},{9,10},{10,9},{11,12},{12,11},... | collective-permute-start | bytes 196616 | tf_op jit(solution)/shard_map/ppermute | solution.py:383
  167.7 3.1 %collective-permute-start.30 = (bf16[16,2048]{1,0:T(8,128)(2,1)S(1)}, bf16[16,2048]{1,0:T(8,128)(2,1)S(1)}, u32[]{:S(2)}, u32[]{:S(2)}) collective-permute-start(bf16[16,2048]{1,0:T(8,128)(2,1)S(1)} %get-tuple-element.130.rows_ref), channel_id=1, source_target_pairs={{3,4},{4,3},{5,6},{6,5},{7,8},{8,7},{9,10},{10,9},{11,12},{12,11},... | collective-permute-start | bytes 196616 | tf_op jit(solution)/shard_map/ppermute | solution.py:383
  174.7 3.1 %collective-permute-start.32 = (bf16[16,2048]{1,0:T(8,128)(2,1)S(1)}, bf16[16,2048]{1,0:T(8,128)(2,1)S(1)}, u32[]{:S(2)}, u32[]{:S(2)}) collective-permute-start(bf16[16,2048]{1,0:T(8,128)(2,1)S(1)} %get-tuple-element.133.rows_ref), channel_id=1, source_target_pairs={{3,4},{4,3},{5,6},{6,5},{7,8},{8,7},{9,10},{10,9},{11,12},{12,11},... | collective-permute-start | bytes 196616 | tf_op jit(solution)/shard_map/ppermute | solution.py:383
  181.7 3.1 %collective-permute-start.34 = (bf16[16,2048]{1,0:T(8,128)(2,1)S(1)}, bf16[16,2048]{1,0:T(8,128)(2,1)S(1)}, u32[]{:S(2)}, u32[]{:S(2)}) collective-permute-start(bf16[16,2048]{1,0:T(8,128)(2,1)S(1)} %get-tuple-element.136.rows_ref), channel_id=1, source_target_pairs={{3,4},{4,3},{5,6},{6,5},{7,8},{8,7},{9,10},{10,9},{11,12},{12,11},... | collective-permute-start | bytes 196616 | tf_op jit(solution)/shard_map/ppermute | solution.py:383
  188.6 10.2 %all_to_all.27.parts_ref = bf16[8,16,1024]{2,1,0:T(8,128)(2,1)S(1)} all-to-all(bf16[8,16,1024]{2,1,0:T(8,128)(2,1)S(1)} %back.15), channel_id=1, replica_groups=mesh['depth'=8,'lat'=64] {'depth'}, dimensions={0} | all-to-all | bytes 524288 | tf_op jit(solution)/shard_map/all_to_all | solution.py:388
  198.9 3.4 %collective-permute-start.36 = (f32[2,8,2048]{2,1,0:T(8,128)S(1)}, f32[2,8,2048]{2,1,0:T(8,128)S(1)}, u32[]{:S(2)}, u32[]{:S(2)}) collective-permute-start(f32[2,8,2048]{2,1,0:T(8,128)S(1)} %gradient.1), channel_id=1, source_target_pairs={{2,0},{3,1},{4,2},{5,3},{6,4},{7,5},{8,6},{9,7},{10,8},{11,9},{12,... | collective-permute-start | bytes 393224 | tf_op jit(solution)/shard_map/ppermute | solution.py:366
  202.3 3.4 %collective-permute-done.36.both_ref = f32[2,8,2048]{2,1,0:T(8,128)S(1)} collective-permute-done((f32[2,8,2048]{2,1,0:T(8,128)S(1)}, f32[2,8,2048]{2,1,0:T(8,128)S(1)}, u32[]{:S(2)}, u32[]{:S(2)}) %collective-permute-start.36) | collective-permute-done | bytes 131104 | tf_op jit(solution)/shard_map/ppermute | solution.py:366
  (124 shorter events, 77.2 us)
Async XLA Ops:
  2.6 21.5 %all-to-all-start.1 = ((bf16[8,2,3,64,128]{4,3,2,1,0:T(8,128)(2,1)}), bf16[8,2,3,64,128]{4,3,2,1,0:T(8,128)(2,1)S(1)}, u32[]{:S(2)}, u32[]{:S(2)}) async-start(bf16[8,2,3,64,128]{4,3,2,1,0:T(8,128)(2,1)} %share.1), calls=%async_computation.1 | async-start | bytes 1572864 | tf_op jit(solution)/shard_map/all_to_all | solution.py:388
  12.1 10.9 %collective-permute-start = (f32[2,8,2048]{2,1,0:T(8,128)S(1)}, f32[2,8,2048]{2,1,0:T(8,128)S(1)}, u32[]{:S(2)}, u32[]{:S(2)}) collective-permute-start(f32[2,8,2048]{2,1,0:T(8,128)S(1)} %pad_maximum_fusion), channel_id=1, source_target_pairs={{0,2},{1,3},{2,4},{3,5},{4,6},{5,7},{6,8},{7,9},{8,10},{9,11},{10,... | collective-permute-start | bytes 393224 | tf_op jit(solution)/shard_map/ppermute | solution.py:366
  24.1 19.0 %all-to-all-start = ((f32[8,2,8,2048]{3,2,1,0:T(8,128)}), f32[8,2,8,2048]{3,2,1,0:T(8,128)S(1)}, u32[]{:S(2)}, u32[]{:S(2)}) async-start(f32[8,2,8,2048]{3,2,1,0:T(8,128)} %copies.1), calls=%async_computation | async-start | bytes 2097152 | tf_op jit(solution)/shard_map/all_to_all | solution.py:388
  29.8 21.6 %collective-permute-start.1 = (bf16[8,2,3,64,128]{4,3,2,1,0:T(8,128)(2,1)S(1)}, bf16[8,2,3,64,128]{4,3,2,1,0:T(8,128)(2,1)S(1)}, u32[]{:S(2)}, u32[]{:S(2)}) collective-permute-start(bf16[8,2,3,64,128]{4,3,2,1,0:T(8,128)(2,1)S(1)} %all-to-all-done.1.own_ref), channel_id=1, source_target_pairs={{0,1},{1,0},{2,3},{3,2},{4,5},{5,4},{6,7},{7,6},{8,9},{9,8},{10,11... | collective-permute-start | bytes 2359304 | tf_op jit(solution)/shard_map/ppermute | solution.py:434
  31.8 8.5 %collective-permute-start.2 = (bf16[16,2048]{1,0:T(8,128)(2,1)S(1)}, bf16[16,2048]{1,0:T(8,128)(2,1)S(1)}, u32[]{:S(2)}, u32[]{:S(2)}) collective-permute-start(bf16[16,2048]{1,0:T(8,128)(2,1)S(1)} %dynamic-slice_bitcast_fusion.1), channel_id=1, source_target_pairs={{0,2},{1,3},{2,4},{3,5},{4,6},{5,7},{6,8},{7,9},{8,10},{9,11},{10,... | collective-permute-start | bytes 196616 | tf_op jit(solution)/shard_map/ppermute | solution.py:366
  34.5 8.5 %collective-permute-start.3 = (bf16[16,2048]{1,0:T(8,128)(2,1)S(1)}, bf16[16,2048]{1,0:T(8,128)(2,1)S(1)}, u32[]{:S(2)}, u32[]{:S(2)}) collective-permute-start(bf16[16,2048]{1,0:T(8,128)(2,1)S(1)} %dynamic-slice_bitcast_fusion), channel_id=1, source_target_pairs={{0,2},{1,3},{2,4},{3,5},{4,6},{5,7},{6,8},{7,9},{8,10},{9,11},{10,... | collective-permute-start | bytes 196616 | tf_op jit(solution)/shard_map/ppermute | solution.py:366
  43.2 8.9 %collective-permute-start.4 = (bf16[32,2048]{1,0:T(8,128)(2,1)S(1)}, bf16[32,2048]{1,0:T(8,128)(2,1)S(1)}, u32[]{:S(2)}, u32[]{:S(2)}) collective-permute-start(bf16[32,2048]{1,0:T(8,128)(2,1)S(1)} %get-tuple-element.75.rows_ref), channel_id=1, source_target_pairs={{3,4},{4,3},{5,6},{6,5},{7,8},{8,7},{9,10},{10,9},{11,12},{12,11},... | collective-permute-start | bytes 393224 | tf_op jit(solution)/shard_map/ppermute | solution.py:383
  52.9 7.5 %collective-permute-start.6 = (bf16[32,2048]{1,0:T(8,128)(2,1)S(1)}, bf16[32,2048]{1,0:T(8,128)(2,1)S(1)}, u32[]{:S(2)}, u32[]{:S(2)}) collective-permute-start(bf16[32,2048]{1,0:T(8,128)(2,1)S(1)} %get-tuple-element.79.rows_ref), channel_id=1, source_target_pairs={{3,4},{4,3},{5,6},{6,5},{7,8},{8,7},{9,10},{10,9},{11,12},{12,11},... | collective-permute-start | bytes 393224 | tf_op jit(solution)/shard_map/ppermute | solution.py:383
  60.7 7.5 %collective-permute-start.8 = (bf16[32,2048]{1,0:T(8,128)(2,1)S(1)}, bf16[32,2048]{1,0:T(8,128)(2,1)S(1)}, u32[]{:S(2)}, u32[]{:S(2)}) collective-permute-start(bf16[32,2048]{1,0:T(8,128)(2,1)S(1)} %get-tuple-element.84.rows_ref), channel_id=1, source_target_pairs={{3,4},{4,3},{5,6},{6,5},{7,8},{8,7},{9,10},{10,9},{11,12},{12,11},... | collective-permute-start | bytes 393224 | tf_op jit(solution)/shard_map/ppermute | solution.py:383
  68.4 7.5 %collective-permute-start.10 = (bf16[32,2048]{1,0:T(8,128)(2,1)S(1)}, bf16[32,2048]{1,0:T(8,128)(2,1)S(1)}, u32[]{:S(2)}, u32[]{:S(2)}) collective-permute-start(bf16[32,2048]{1,0:T(8,128)(2,1)S(1)} %get-tuple-element.89.rows_ref), channel_id=1, source_target_pairs={{3,4},{4,3},{5,6},{6,5},{7,8},{8,7},{9,10},{10,9},{11,12},{12,11},... | collective-permute-start | bytes 393224 | tf_op jit(solution)/shard_map/ppermute | solution.py:383
  76.2 7.5 %collective-permute-start.12 = (bf16[32,2048]{1,0:T(8,128)(2,1)S(1)}, bf16[32,2048]{1,0:T(8,128)(2,1)S(1)}, u32[]{:S(2)}, u32[]{:S(2)}) collective-permute-start(bf16[32,2048]{1,0:T(8,128)(2,1)S(1)} %get-tuple-element.94.rows_ref), channel_id=1, source_target_pairs={{3,4},{4,3},{5,6},{6,5},{7,8},{8,7},{9,10},{10,9},{11,12},{12,11},... | collective-permute-start | bytes 393224 | tf_op jit(solution)/shard_map/ppermute | solution.py:383
  83.9 7.5 %collective-permute-start.14 = (bf16[32,2048]{1,0:T(8,128)(2,1)S(1)}, bf16[32,2048]{1,0:T(8,128)(2,1)S(1)}, u32[]{:S(2)}, u32[]{:S(2)}) collective-permute-start(bf16[32,2048]{1,0:T(8,128)(2,1)S(1)} %get-tuple-element.99.rows_ref), channel_id=1, source_target_pairs={{3,4},{4,3},{5,6},{6,5},{7,8},{8,7},{9,10},{10,9},{11,12},{12,11},... | collective-permute-start | bytes 393224 | tf_op jit(solution)/shard_map/ppermute | solution.py:383
  91.7 7.5 %collective-permute-start.16 = (bf16[32,2048]{1,0:T(8,128)(2,1)S(1)}, bf16[32,2048]{1,0:T(8,128)(2,1)S(1)}, u32[]{:S(2)}, u32[]{:S(2)}) collective-permute-start(bf16[32,2048]{1,0:T(8,128)(2,1)S(1)} %get-tuple-element.104.rows_ref), channel_id=1, source_target_pairs={{3,4},{4,3},{5,6},{6,5},{7,8},{8,7},{9,10},{10,9},{11,12},{12,11},... | collective-permute-start | bytes 393224 | tf_op jit(solution)/shard_map/ppermute | solution.py:383
  99.4 7.5 %collective-permute-start.18 = (bf16[32,2048]{1,0:T(8,128)(2,1)S(1)}, bf16[32,2048]{1,0:T(8,128)(2,1)S(1)}, u32[]{:S(2)}, u32[]{:S(2)}) collective-permute-start(bf16[32,2048]{1,0:T(8,128)(2,1)S(1)} %get-tuple-element.109.rows_ref), channel_id=1, source_target_pairs={{3,4},{4,3},{5,6},{6,5},{7,8},{8,7},{9,10},{10,9},{11,12},{12,11},... | collective-permute-start | bytes 393224 | tf_op jit(solution)/shard_map/ppermute | solution.py:383
  132.7 6.8 %collective-permute-start.20 = (bf16[16,2048]{1,0:T(8,128)(2,1)S(1)}, bf16[16,2048]{1,0:T(8,128)(2,1)S(1)}, u32[]{:S(2)}, u32[]{:S(2)}) collective-permute-start(bf16[16,2048]{1,0:T(8,128)(2,1)S(1)} %get-tuple-element.115.rows_ref), channel_id=1, source_target_pairs={{3,4},{4,3},{5,6},{6,5},{7,8},{8,7},{9,10},{10,9},{11,12},{12,11},... | collective-permute-start | bytes 196616 | tf_op jit(solution)/shard_map/ppermute | solution.py:383
  135.1 4.3 %collective-permute-start.21 = (bf16[16,2048]{1,0:T(8,128)(2,1)S(1)}, bf16[16,2048]{1,0:T(8,128)(2,1)S(1)}, u32[]{:S(2)}, u32[]{:S(2)}) collective-permute-start(bf16[16,2048]{1,0:T(8,128)(2,1)S(1)} %get-tuple-element.115.rows_ref), channel_id=1, source_target_pairs={{2,3},{3,2},{4,5},{5,4},{6,7},{7,6},{8,9},{9,8},{10,11},{11,10},{1... | collective-permute-start | bytes 196616 | tf_op jit(solution)/shard_map/ppermute | solution.py:383
  139.7 6.8 %collective-permute-start.22 = (bf16[16,2048]{1,0:T(8,128)(2,1)S(1)}, bf16[16,2048]{1,0:T(8,128)(2,1)S(1)}, u32[]{:S(2)}, u32[]{:S(2)}) collective-permute-start(bf16[16,2048]{1,0:T(8,128)(2,1)S(1)} %get-tuple-element.118.rows_ref), channel_id=1, source_target_pairs={{3,4},{4,3},{5,6},{6,5},{7,8},{8,7},{9,10},{10,9},{11,12},{12,11},... | collective-permute-start | bytes 196616 | tf_op jit(solution)/shard_map/ppermute | solution.py:383
  146.7 6.8 %collective-permute-start.24 = (bf16[16,2048]{1,0:T(8,128)(2,1)S(1)}, bf16[16,2048]{1,0:T(8,128)(2,1)S(1)}, u32[]{:S(2)}, u32[]{:S(2)}) collective-permute-start(bf16[16,2048]{1,0:T(8,128)(2,1)S(1)} %get-tuple-element.121.rows_ref), channel_id=1, source_target_pairs={{3,4},{4,3},{5,6},{6,5},{7,8},{8,7},{9,10},{10,9},{11,12},{12,11},... | collective-permute-start | bytes 196616 | tf_op jit(solution)/shard_map/ppermute | solution.py:383
  153.7 6.8 %collective-permute-start.26 = (bf16[16,2048]{1,0:T(8,128)(2,1)S(1)}, bf16[16,2048]{1,0:T(8,128)(2,1)S(1)}, u32[]{:S(2)}, u32[]{:S(2)}) collective-permute-start(bf16[16,2048]{1,0:T(8,128)(2,1)S(1)} %get-tuple-element.124.rows_ref), channel_id=1, source_target_pairs={{3,4},{4,3},{5,6},{6,5},{7,8},{8,7},{9,10},{10,9},{11,12},{12,11},... | collective-permute-start | bytes 196616 | tf_op jit(solution)/shard_map/ppermute | solution.py:383
  160.7 6.8 %collective-permute-start.28 = (bf16[16,2048]{1,0:T(8,128)(2,1)S(1)}, bf16[16,2048]{1,0:T(8,128)(2,1)S(1)}, u32[]{:S(2)}, u32[]{:S(2)}) collective-permute-start(bf16[16,2048]{1,0:T(8,128)(2,1)S(1)} %get-tuple-element.127.rows_ref), channel_id=1, source_target_pairs={{3,4},{4,3},{5,6},{6,5},{7,8},{8,7},{9,10},{10,9},{11,12},{12,11},... | collective-permute-start | bytes 196616 | tf_op jit(solution)/shard_map/ppermute | solution.py:383
  167.7 6.8 %collective-permute-start.30 = (bf16[16,2048]{1,0:T(8,128)(2,1)S(1)}, bf16[16,2048]{1,0:T(8,128)(2,1)S(1)}, u32[]{:S(2)}, u32[]{:S(2)}) collective-permute-start(bf16[16,2048]{1,0:T(8,128)(2,1)S(1)} %get-tuple-element.130.rows_ref), channel_id=1, source_target_pairs={{3,4},{4,3},{5,6},{6,5},{7,8},{8,7},{9,10},{10,9},{11,12},{12,11},... | collective-permute-start | bytes 196616 | tf_op jit(solution)/shard_map/ppermute | solution.py:383
  174.7 6.8 %collective-permute-start.32 = (bf16[16,2048]{1,0:T(8,128)(2,1)S(1)}, bf16[16,2048]{1,0:T(8,128)(2,1)S(1)}, u32[]{:S(2)}, u32[]{:S(2)}) collective-permute-start(bf16[16,2048]{1,0:T(8,128)(2,1)S(1)} %get-tuple-element.133.rows_ref), channel_id=1, source_target_pairs={{3,4},{4,3},{5,6},{6,5},{7,8},{8,7},{9,10},{10,9},{11,12},{12,11},... | collective-permute-start | bytes 196616 | tf_op jit(solution)/shard_map/ppermute | solution.py:383
  181.7 6.8 %collective-permute-start.34 = (bf16[16,2048]{1,0:T(8,128)(2,1)S(1)}, bf16[16,2048]{1,0:T(8,128)(2,1)S(1)}, u32[]{:S(2)}, u32[]{:S(2)}) collective-permute-start(bf16[16,2048]{1,0:T(8,128)(2,1)S(1)} %get-tuple-element.136.rows_ref), channel_id=1, source_target_pairs={{3,4},{4,3},{5,6},{6,5},{7,8},{8,7},{9,10},{10,9},{11,12},{12,11},... | collective-permute-start | bytes 196616 | tf_op jit(solution)/shard_map/ppermute | solution.py:383
  198.9 6.9 %collective-permute-start.36 = (f32[2,8,2048]{2,1,0:T(8,128)S(1)}, f32[2,8,2048]{2,1,0:T(8,128)S(1)}, u32[]{:S(2)}, u32[]{:S(2)}) collective-permute-start(f32[2,8,2048]{2,1,0:T(8,128)S(1)} %gradient.1), channel_id=1, source_target_pairs={{2,0},{3,1},{4,2},{5,3},{6,4},{7,5},{8,6},{9,7},{10,8},{11,9},{12,... | collective-permute-start | bytes 393224 | tf_op jit(solution)/shard_map/ppermute | solution.py:366
  (25 other events, 227.2 us)
